TPU v7x, 32 devices: a whole 2x2x4 slice. The times are simulated.
32 devices in a mesh: seg: 4 (over y, core), seq: 8 (over z, x).
Axes of the slice: x: 2, y: 2, z: 4, core: 2. Of those that a mesh axis runs over, the one named last changes fastest.
Arguments:
- tokens: bfloat16 [4096, 2048], P(('seg', 'seq')), may hold values from -6 to 6
- tm_mats: bfloat16 [5, 2048, 2048], P(None, ('seg', 'seq')), may hold values from -0.125 to 0.125
- low_rank: bfloat16 [2, 2048, 224], P(None, ('seg', 'seq')), may hold values from -0.6 to 0.6
- channel_parameters: float32 [16, 2048], replicated, may hold values from -12 to 2
- piece_opening_memory: float32 [4, 32, 64, 64], P('seg'), may hold values from -16 to 16
- cm_key: bfloat16 [2048, 7168], P(None, 'seq'), may hold values from -0.125 to 0.125
- cm_value: bfloat16 [7168, 2048], P('seq'), may hold values from -0.0625 to 0.0625
- cm_recept: bfloat16 [2048, 2048], P(None, 'seq'), may hold values from -0.125 to 0.125
- out_grad: bfloat16 [4096, 2048], P(('seg', 'seq')), may hold values from -6 to 6
Outputs:
- block_out: bfloat16 [4096, 2048], P(('seg', 'seq'))
- input_grad: float32 [4096, 2048], P(('seg', 'seq'))
- tm_mats_grad: float32 [5, 2048, 2048], P(None, ('seg', 'seq'))
- low_rank_grad: float32 [2, 2048, 224], P(None, ('seg', 'seq'))
- vectors_grad: float32 [16, 2048], P(None, ('seg', 'seq'))
- cm_key_grad: float32 [2048, 7168], P(None, 'seq')
- cm_value_grad: float32 [7168, 2048], P('seq')
- cm_recept_grad: float32 [2048, 2048], P(None, 'seq')
All inputs are finite; a program needn't handle non-finite values.
Results may differ from a plain program's by a relative error of at most 0.025.
Values may be sent and summed in bfloat16 or wider, within the bound.
No kernel may reach another device: no remote copies, remote signals or barrier semaphores. Data moves between devices by JAX's collectives and lax.ppermute only.
A program may use at most 448 MiB of HBM per device.

v0:
```python
import jax
import jax.numpy as jnp
from jax import lax
from jax.sharding import PartitionSpec as P

CHANNEL_GROUP = 64
MIX_RANK = 32
BLOCK = 16


eps_norm = 1e-05
eps_group = 0.00064
exact_matmul_mode = lax.Precision.HIGHEST


def passed_along(value, axis, by):
    length = lax.axis_size(axis)
    pairs = [(i, i + by) for i in range(length) if 0 <= i + by < length]
    return lax.ppermute(value, axis, pairs)


def rounded(values):
    return values.astype(jnp.bfloat16)


def product(left_operand, right_operand):
    return jnp.dot(left_operand, right_operand, preferred_element_type=jnp.float32)


def product_tn(left_operand, right_operand):
    return lax.dot_general(
        left_operand, right_operand, (((0,), (0,)), ((), ())), preferred_element_type=jnp.float32
    )


def product_nt(left_operand, right_operand):
    return lax.dot_general(
        left_operand, right_operand, (((1,), (1,)), ((), ())), preferred_element_type=jnp.float32
    )


def layer_norm(values, gain_row, bias_row):
    center = values - jnp.mean(values, axis=-1, keepdims=True)
    spread = jnp.mean(center * center, axis=-1, keepdims=True)
    return center * lax.rsqrt(spread + eps_norm) * gain_row + bias_row


def first_norm(values, channel_parameters):
    return layer_norm(values, channel_parameters[0], channel_parameters[1])


def second_norm(values, channel_parameters):
    return layer_norm(values, channel_parameters[12], channel_parameters[13])


def shift_mix(normed, prev_row, channel_parameters):
    before = jnp.concatenate([prev_row, normed[:-1]], axis=0)
    difference = before - normed
    return (difference, normed + difference * channel_parameters[2])


def five_mixes(normed, difference, mixes, channel_parameters):
    return tuple(
        (
            normed + difference * (channel_parameters[3 + number] + mixes[number])
            for number in range(5)
        )
    )


def decay_rate(raised, channel_parameters):
    log_rate = channel_parameters[8] + raised
    return (log_rate, -jnp.exp(log_rate))


def channel_shift(inputs, channel_parameters):
    before = jnp.concatenate([jnp.zeros_like(inputs[:1]), inputs[:-1]], axis=0)
    difference = before - inputs
    return (
        inputs + difference * channel_parameters[14],
        inputs + difference * channel_parameters[15],
    )


def group_gate(mixed, gate_pre, channel_parameters):
    row_count, model_width = mixed.shape
    grouped = mixed.reshape(row_count, model_width // CHANNEL_GROUP, CHANNEL_GROUP)
    center = grouped - jnp.mean(grouped, axis=-1, keepdims=True)
    spread = jnp.mean(center * center, axis=-1, keepdims=True)
    normed = (center * lax.rsqrt(spread + eps_group)).reshape(row_count, model_width)
    return (normed * channel_parameters[10] + channel_parameters[11]) * jax.nn.silu(gate_pre)


def wkv_blocks(
    acceptor_lines,
    entering_lookup_lines,
    entering_payload_lines,
    fading_exponent_log,
    channel_parameters,
):
    row_count, model_width = fading_exponent_log.shape
    group_count_total = model_width // CHANNEL_GROUP
    block_count = row_count // BLOCK
    group_reward_entries = channel_parameters[9].reshape(group_count_total, CHANNEL_GROUP)
    positions = jnp.arange(BLOCK)
    earlier = (positions[:, None] > positions[None, :])[:, :, None, None]

    def shaped(array):
        return array.reshape(block_count, BLOCK, group_count_total, CHANNEL_GROUP)

    def one_block(carried, member):
        running_memory, total_decay = carried
        acceptor_patch, lookup_patch, payload_patch, decay_block = member
        inclusive = jnp.cumsum(decay_block, axis=0)
        exclusive = inclusive - decay_block
        decay_reach_current = jnp.exp(exclusive)
        from_state = jnp.einsum(
            "eop,opt->eot",
            acceptor_patch * decay_reach_current,
            running_memory,
            precision=exact_matmul_mode,
        )
        decay_gaps = exclusive[:, None] - inclusive[None, :]
        weights_pair = jnp.where(earlier, jnp.exp(jnp.where(earlier, decay_gaps, 0.0)), 0.0)
        scores = jnp.einsum(
            "thk,tshk,shk->tsh",
            acceptor_patch,
            weights_pair,
            lookup_patch,
            precision=exact_matmul_mode,
        )
        diagonal_reward_part = jnp.sum(
            acceptor_patch * group_reward_entries * lookup_patch, axis=-1
        )
        within = (
            jnp.einsum("tsh,shv->thv", scores, payload_patch, precision=exact_matmul_mode)
            + diagonal_reward_part[..., None] * payload_patch
        )
        decay_until_end = jnp.exp(inclusive[-1][None] - inclusive)
        new_state = jnp.exp(inclusive[-1])[..., None] * running_memory + jnp.einsum(
            "ylt,ylr->ltr",
            lookup_patch * decay_until_end,
            payload_patch,
            precision=exact_matmul_mode,
        )
        reach_now = jnp.exp(total_decay[None] + exclusive)
        return ((new_state, total_decay + inclusive[-1]), (from_state + within, reach_now))

    start = (
        jnp.zeros((group_count_total, CHANNEL_GROUP, CHANNEL_GROUP), jnp.float32),
        jnp.zeros((group_count_total, CHANNEL_GROUP), jnp.float32),
    )
    finals, per_block = lax.scan(
        one_block,
        start,
        (
            shaped(acceptor_lines),
            shaped(entering_lookup_lines),
            shaped(entering_payload_lines),
            shaped(fading_exponent_log),
        ),
    )
    local_state, total_decay = finals
    output_rows, reach_all = per_block
    return (
        output_rows.reshape(row_count, group_count_total, CHANNEL_GROUP),
        reach_all.reshape(row_count, group_count_total, CHANNEL_GROUP),
        jnp.exp(total_decay),
        local_state,
    )


def wkv_full(
    acceptor_lines,
    entering_lookup_lines,
    entering_payload_lines,
    fading_exponent_log,
    channel_parameters,
    incoming_state,
):
    row_count, model_width = fading_exponent_log.shape
    output_rows, reach_all, decay_all, local_state = wkv_blocks(
        acceptor_lines,
        entering_lookup_lines,
        entering_payload_lines,
        fading_exponent_log,
        channel_parameters,
    )
    weighted_values = acceptor_lines.reshape(output_rows.shape) * reach_all
    final_result = output_rows + jnp.einsum(
        "rse,sey->rsy", weighted_values, incoming_state, precision=exact_matmul_mode
    )
    return (
        final_result.reshape(row_count, model_width),
        decay_all[..., None] * incoming_state + local_state,
    )


def neighbour_row(row_values, step_by):
    return passed_along(row_values, "seq", step_by)


def carry_states(decay_all, local_state, start_state, step_by):
    chain_length = lax.axis_size("seq")
    position = lax.axis_index("seq")
    first_place = 0 if step_by > 0 else chain_length - 1

    def one_turn(turn_number, incoming_state):
        outgoing = decay_all[..., None] * incoming_state + local_state
        received = passed_along(outgoing.astype(jnp.bfloat16), "seq", step_by).astype(
            outgoing.dtype
        )
        return jnp.where(position == first_place, start_state, received)

    return lax.fori_loop(0, chain_length - 1, one_turn, start_state)


def shards(
    tokens,
    tm_mats,
    low_rank,
    channel_parameters,
    piece_opening_memory,
    cm_key,
    cm_value,
    cm_recept,
    out_grad,
):
    row_count, model_width = tokens.shape
    group_count_total = model_width // CHANNEL_GROUP
    mix_width = 5 * MIX_RANK
    tokens_f = tokens.astype(jnp.float32)
    whole_mats, whole_rank = (
        lax.all_gather(tm_mats, ("seg", "seq"), axis=1, tiled=True),
        lax.all_gather(low_rank, ("seg", "seq"), axis=1, tiled=True),
    )
    w_recept, w_key, w_value, w_gate, w_output = (whole_mats[number] for number in range(5))
    down_mix = whole_rank[0][:, :mix_width]
    down_decay = whole_rank[0][:, mix_width:]
    up_mix = whole_rank[1][:, :mix_width]
    up_decay = whole_rank[1][:, mix_width:]
    normed = first_norm(tokens_f, channel_parameters)
    prev_row = neighbour_row(normed[-1:], 1)
    difference, mixed_x = shift_mix(normed, prev_row, channel_parameters)
    mixed_x_b = rounded(mixed_x)
    mix_tanh = jnp.tanh(product(mixed_x_b, down_mix))
    mix_groups = rounded(mix_tanh).reshape(row_count, 5, MIX_RANK)
    up_groups = up_mix.reshape(model_width, 5, MIX_RANK)
    mixes = jnp.einsum("tgr,dgr->gtd", mix_groups, up_groups, preferred_element_type=jnp.float32)
    inputs_five = five_mixes(normed, difference, mixes, channel_parameters)
    x_decay, x_key, x_value, x_recept, x_gate = (rounded(member) for member in inputs_five)
    decay_tanh = jnp.tanh(product(x_decay, down_decay))
    decay_low = rounded(decay_tanh)
    raised = product_nt(decay_low, up_decay)
    log_rate, fading_exponent_log = decay_rate(raised, channel_parameters)
    recept_low = rounded(product(x_recept, w_recept))
    keys_low = rounded(product(x_key, w_key))
    values_low = rounded(product(x_value, w_value))
    gate_pre = product(x_gate, w_gate)
    recept_f = recept_low.astype(jnp.float32)
    keys_f = keys_low.astype(jnp.float32)
    values_f = values_low.astype(jnp.float32)
    output_rows, reach_all, decay_all, local_state = wkv_blocks(
        recept_f, keys_f, values_f, fading_exponent_log, channel_parameters
    )
    incoming_state = carry_states(decay_all, local_state, piece_opening_memory[0], 1)
    weighted_values = recept_f.reshape(row_count, group_count_total, CHANNEL_GROUP) * reach_all
    weighted_kv_output = (
        output_rows
        + jnp.einsum("rse,sey->rsy", weighted_values, incoming_state, precision=exact_matmul_mode)
    ).reshape(row_count, model_width)
    gated = rounded(group_gate(weighted_kv_output, gate_pre, channel_parameters))
    residual = tokens_f + product(gated, w_output)
    second = rounded(second_norm(residual, channel_parameters))
    seg_inputs = lax.all_gather(second, "seq", axis=0, tiled=True)
    seg_inputs_f = seg_inputs.astype(jnp.float32)
    key_mix, recept_mix = channel_shift(seg_inputs_f, channel_parameters)
    key_mix_b = rounded(key_mix)
    recept_mix_b = rounded(recept_mix)
    hidden_pre = product(key_mix_b, cm_key)
    hidden = rounded(jnp.square(jax.nn.relu(hidden_pre)))
    partial_kv = product(hidden, cm_value)
    kv_cols = lax.psum_scatter(
        partial_kv.astype(jnp.bfloat16), "seq", scatter_dimension=1, tiled=True
    ).astype(jnp.float32)
    gate_cols = jax.nn.sigmoid(product(recept_mix_b, cm_recept))
    channel_cols = rounded(gate_cols * kv_cols)
    channel_rows = lax.all_to_all(channel_cols, "seq", split_axis=0, concat_axis=1, tiled=True)
    block_out = rounded(residual + channel_rows.astype(jnp.float32))
    grad_cols = lax.all_to_all(out_grad, "seq", split_axis=1, concat_axis=0, tiled=True).astype(
        jnp.float32
    )
    grad_kv = rounded(grad_cols * gate_cols)
    grad_gate_cm = rounded(grad_cols * kv_cols * gate_cols * (1.0 - gate_cols))
    grad_kv_all = lax.all_gather(grad_kv, "seq", axis=1, tiled=True)
    cm_value_grad = product_tn(hidden, grad_kv_all)
    grad_hidden = product_nt(grad_kv_all, cm_value)
    grad_hidden_pre = rounded(grad_hidden * 2.0 * jax.nn.relu(hidden_pre))
    cm_key_grad = product_tn(key_mix_b, grad_hidden_pre)
    cm_recept_grad = product_tn(recept_mix_b, grad_gate_cm)
    grad_key_mix = product_nt(grad_hidden_pre, cm_key)
    grad_recept_mix = product_nt(grad_gate_cm, cm_recept)
    shift_pair, shift_back = jax.vjp(channel_shift, seg_inputs_f, channel_parameters)
    grad_inputs_part, vec_grad_cm = shift_back((grad_key_mix, grad_recept_mix))
    grad_second = lax.psum_scatter(
        grad_inputs_part.astype(jnp.bfloat16), "seq", scatter_dimension=0, tiled=True
    ).astype(jnp.float32)
    cm_grads = (
        lax.psum(cm_key_grad.astype(jnp.bfloat16), "seg").astype(jnp.float32),
        lax.psum(cm_value_grad.astype(jnp.bfloat16), "seg").astype(jnp.float32),
        lax.psum(cm_recept_grad.astype(jnp.bfloat16), "seg").astype(jnp.float32),
    )
    norm_two, norm_two_back = jax.vjp(second_norm, residual, channel_parameters)
    grad_residual_ln, vec_grad_ln2 = norm_two_back(grad_second)
    grad_residual = out_grad.astype(jnp.float32) + grad_residual_ln
    grad_branch = rounded(grad_residual)
    grad_w_output = product_tn(gated, grad_branch)
    grad_gated = product_nt(grad_branch, w_output)
    group_value, group_back = jax.vjp(group_gate, weighted_kv_output, gate_pre, channel_parameters)
    grad_wkv, grad_gate_raw, vec_grad_group = group_back(grad_gated)
    grad_gate_b = rounded(grad_gate_raw)
    head_gradient_rows = grad_wkv.reshape(row_count, group_count_total, CHANNEL_GROUP)
    segment_local_gradient = jnp.einsum(
        "ofn,ofp->fnp", weighted_values, head_gradient_rows, precision=exact_matmul_mode
    )
    grad_end = carry_states(
        decay_all, segment_local_gradient, jnp.zeros_like(segment_local_gradient), -1
    )

    def wkv_closed(recept_in, entering_lookup_lines, entering_payload_lines, decay_in, vectors_in):
        return wkv_full(
            recept_in,
            entering_lookup_lines,
            entering_payload_lines,
            decay_in,
            vectors_in,
            incoming_state,
        )

    wkv_value, wkv_back = jax.vjp(
        wkv_closed, recept_f, keys_f, values_f, fading_exponent_log, channel_parameters
    )
    grad_recept_f, grad_key_f, grad_value_f, grad_decay, vec_grad_wkv = wkv_back(
        (grad_wkv, grad_end)
    )
    grad_recept = rounded(grad_recept_f)
    grad_key = rounded(grad_key_f)
    grad_value = rounded(grad_value_f)
    rate_pair, rate_back = jax.vjp(decay_rate, raised, channel_parameters)
    grad_raised_raw, vec_grad_rate = rate_back((jnp.zeros_like(log_rate), grad_decay))
    grad_raised = rounded(grad_raised_raw)
    grad_w_recept = product_tn(x_recept, grad_recept)
    grad_w_key = product_tn(x_key, grad_key)
    grad_w_value = product_tn(x_value, grad_value)
    grad_w_gate = product_tn(x_gate, grad_gate_b)
    grad_x_recept = product_nt(grad_recept, w_recept)
    grad_x_key = product_nt(grad_key, w_key)
    grad_x_value = product_nt(grad_value, w_value)
    grad_x_gate = product_nt(grad_gate_b, w_gate)
    grad_up_decay = product_tn(grad_raised, decay_low)
    grad_decay_low = product(grad_raised, up_decay)
    grad_decay_pre = rounded(grad_decay_low * (1.0 - decay_tanh * decay_tanh))
    grad_down_decay = product_tn(x_decay, grad_decay_pre)
    grad_x_decay = product_nt(grad_decay_pre, down_decay)
    five_value, five_back = jax.vjp(five_mixes, normed, difference, mixes, channel_parameters)
    grad_normed_five, grad_difference, grad_mixes_raw, vec_grad_five = five_back(
        (grad_x_decay, grad_x_key, grad_x_value, grad_x_recept, grad_x_gate)
    )
    grad_mixes = rounded(grad_mixes_raw)
    grad_up_groups = jnp.einsum(
        "gtd,tgr->dgr", grad_mixes, mix_groups, preferred_element_type=jnp.float32
    )
    grad_mix_groups = jnp.einsum(
        "gtd,dgr->tgr", grad_mixes, up_groups, preferred_element_type=jnp.float32
    )
    grad_mix_pre = rounded(
        grad_mix_groups.reshape(row_count, mix_width) * (1.0 - mix_tanh * mix_tanh)
    )
    grad_down_mix = product_tn(mixed_x_b, grad_mix_pre)
    grad_mixed_x = product_nt(grad_mix_pre, down_mix)
    shift_value, shift_back_tm = jax.vjp(shift_mix, normed, prev_row, channel_parameters)
    grad_normed_shift, grad_prev_row, vec_grad_shift = shift_back_tm(
        (grad_difference, grad_mixed_x)
    )
    from_next = neighbour_row(grad_prev_row, -1)
    grad_normed = (grad_normed_five + grad_normed_shift).at[-1:].add(from_next)
    norm_one, norm_one_back = jax.vjp(first_norm, tokens_f, channel_parameters)
    grad_tokens_ln, vec_grad_ln1 = norm_one_back(grad_normed)
    input_grad = grad_residual + grad_tokens_ln
    vec_grad = (
        vec_grad_cm
        + vec_grad_ln2
        + vec_grad_group
        + vec_grad_wkv
        + vec_grad_rate
        + vec_grad_five
        + vec_grad_shift
        + vec_grad_ln1
    )
    rank_grad = jnp.stack(
        [
            jnp.concatenate([grad_down_mix, grad_down_decay], axis=1),
            jnp.concatenate(
                [grad_up_groups.reshape(model_width, mix_width), grad_up_decay], axis=1
            ),
        ]
    )
    pending = (
        jnp.stack([grad_w_recept, grad_w_key, grad_w_value, grad_w_gate, grad_w_output]),
        rank_grad,
        vec_grad,
    )
    mats_part, rank_part, vectors_part = (
        lax.psum_scatter(pending[0], ("seg", "seq"), scatter_dimension=1, tiled=True),
        lax.psum_scatter(pending[1], ("seg", "seq"), scatter_dimension=1, tiled=True),
        lax.psum_scatter(pending[2], ("seg", "seq"), scatter_dimension=1, tiled=True),
    )
    return (
        block_out,
        input_grad,
        mats_part,
        rank_part,
        vectors_part,
        cm_grads[0],
        cm_grads[1],
        cm_grads[2],
    )


def solution(mesh):
    in_specs = (
        P(("seg", "seq"), None),
        P(None, ("seg", "seq"), None),
        P(None, ("seg", "seq"), None),
        P(),
        P("seg", None, None, None),
        P(None, "seq"),
        P("seq", None),
        P(None, "seq"),
        P(("seg", "seq"), None),
    )
    out_specs = (
        P(("seg", "seq"), None),
        P(("seg", "seq"), None),
        P(None, ("seg", "seq"), None),
        P(None, ("seg", "seq"), None),
        P(None, ("seg", "seq")),
        P(None, "seq"),
        P("seq", None),
        P(None, "seq"),
    )
    return jax.shard_map(shards, mesh=mesh, in_specs=in_specs, out_specs=out_specs, check_vma=False)
```

profile of v0, /device:TPU:0, one launch (start us, length us, event | category | flops | bytes accessed | tf_op | source)
XLA Modules:
  0.0 3987.2 jit_solution(14360024126059356605)
XLA Ops:
  25.4 45.0 %all-gather.5.cloned.1.call-done = bf16[2,2048,224]{2,1,0:T(8,128)(2,1)} async-done(((bf16[2,64,224]{2,1,0:T(8,128)(2,1)}), bf16[2,2048,224]{2,1,0:T(8,128)(2,1)}) %all-gather.5.cloned.1.call-update) | async-done | bytes 1835024 | tf_op jit(solution)/shard_map/all_gather | solution.py:235
  89.3 218.0 %all-gather.7.cloned.1.call-done = bf16[5,2048,2048]{2,1,0:T(8,128)(2,1)} async-done(((bf16[5,64,2048]{2,1,0:T(8,128)(2,1)}), bf16[5,2048,2048]{2,1,0:T(8,128)(2,1)}) %all-gather.7.cloned.1.call-update) | async-done | bytes 41943056 | tf_op jit(solution)/shard_map/all_gather | solution.py:234
  343.5 205.1 %while.119 = (s32[]{:T(128)}, f32[32,64,64]{2,1,0:T(8,128)S(1)}, f32[32,64]{1,0:T(8,128)S(1)}, f32[8,16,32,64]{3,2,1,0:T(8,128)}, f32[8,16,32,64]{3,2,1,0:T(8,12...) while((s32[]{:T(128)}, f32[32,64,64]{2,1,0:T(8,128)S(1)}, ...), condition=%wide.region_5.6_spmd.clone.clone, body=%wide.region_2.5_spmd.clone.clone.sunk | while | flops 66424576 | bytes 11308189 | solution.py:153
  350.0 9.6 fusion.331
  375.6 9.6 fusion.331
  401.2 9.6 fusion.331
  426.8 9.6 fusion.331
  452.4 9.6 fusion.331
  477.9 9.6 fusion.331
  503.5 9.6 fusion.331
  558.6 120.4 %while.117 = (s32[]{:T(128)}, f32[32,64,64]{2,1,0:T(8,128)S(1)}, pred[]{:T(512)}, f32[32,64]{1,0:T(8,128)S(1)}, f32[32,64,64]{2,1,0:T(8,128)S(1)}, /*index=5*/f32[32,64,64]{2,1,0:T(8,128)}, s32[]{:T(128)}) while((s32[]{:T(128)}, f32[32,64,64]{2,1,0:T(8,128)S(1)}, pred[]{:T(512)}, f32[32,64]{1,0:T(8,128)S(1)}, f32[32,64,64]{2,1,0:T(8,128)S(1)}, ...), condition=%wide.region_7.8_spmd, body=%wide.region_6.7_spmd.sunk | while | flops 655362 | bytes 4726930 | solution.py:215
  563.1 11.9 collective-permute-done
  582.4 11.0 collective-permute-done
  600.9 10.1 collective-permute-done
  699.3 74.4 %all-gather.9.cloned.1.call-done = bf16[1024,2048]{1,0:T(8,128)(2,1)} async-done(((bf16[128,2048]{1,0:T(8,128)(2,1)}), bf16[1024,2048]{1,0:T(8,128)(2,1)}) %all-gather.9.cloned.1.call-update) | async-done | bytes 4194320 | tf_op jit(solution)/shard_map/all_gather | solution.py:275
  796.0 29.9 all_to_all.26
  826.0 65.7 %reduce-scatter.7.cloned.1.call-done = bf16[1024,256]{1,0:T(8,128)(2,1)} async-done(((bf16[1024,2048]{1,0:T(8,128)(2,1)}), bf16[1024,256]{1,0:T(8,128)(2,1)}) %reduce-scatter.7.cloned.1.call-update) | async-done | bytes 524304 | tf_op jit(solution)/shard_map/reduce_scatter | solution.py:283
  903.4 77.8 %all-gather.11.cloned.1.call-done = bf16[1024,2048]{1,0:T(8,128)(2,1)} async-done(((bf16[1024,256]{1,0:T(8,128)(2,1)}), bf16[1024,2048]{1,0:T(8,128)(2,1)}) %all-gather.11.cloned.1.call-update) | async-done | bytes 4194320 | tf_op jit(solution)/shard_map/all_gather | solution.py:295
  997.5 10.6 multiply_reduce_fusion.2
  1030.4 228.7 %while.120 = (s32[]{:T(128)}, f32[32,64,64]{2,1,0:T(8,128)S(1)}, f32[32,64]{1,0:T(8,128)S(1)}, f32[8,16,32,64]{3,2,1,0:T(8,128)}, f32[8,16,32,64]{3,2,1,0:T(8,12...) while((s32[]{:T(128)}, f32[32,64,64]{2,1,0:T(8,128)S(1)}, ...), condition=%wide.region_21.22_spmd.clone.clone, body=%wide.region_18.21_spmd.clone.clone.sunk | while | flops 38637056 | bytes 25331696 | solution.py:153
  1315.6 119.9 %while.118 = (s32[]{:T(128)}, f32[32,64,64]{2,1,0:T(8,128)S(1)}, pred[]{:T(512)}, f32[32,64]{1,0:T(8,128)S(1)}, f32[32,64,64]{2,1,0:T(8,128)S(1)}, /*index=5*/s32[]{:T(128)}, s32[]{:T(128)}) while((s32[]{:T(128)}, f32[32,64,64]{2,1,0:T(8,128)S(1)}, pred[]{:T(512)}, f32[32,64]{1,0:T(8,128)S(1)}, f32[32,64,64]{2,1,0:T(8,128)S(1)}, ...), condition=%wide.region_23.24_spmd.clone, body=%wide.region_22.23_spmd.clone.sunk | while | flops 786435 | bytes 4202652 | solution.py:215
  1318.0 14.0 collective-permute-done.1
  1336.4 14.7 collective-permute-done.1
  1355.6 13.8 collective-permute-done.1
  1373.8 12.9 collective-permute-done.1
  1391.1 11.9 collective-permute-done.1
  1407.5 11.0 collective-permute-done.1
  1422.9 10.6 collective-permute-done.1
  1443.0 400.8 %while.121 = (s32[]{:T(128)}, f32[32,64]{1,0:T(8,128)S(1)}, f32[32,64,64]{2,1,0:T(8,128)S(1)}, f32[32,64]{1,0:T(8,128)S(1)}, f32[8,16,32,64]{3,2,1,0:T(8,128)}, ...) while((s32[]{:T(128)}, f32[32,64]{1,0:T(8,128)S(1)}, ...), condition=%wide.region_34.35_spmd.clone.clone, body=%wide.region_25.0_spmd.clone.clone.sunk | while | flops 126942720 | bytes 26118804 | solution.py:153
  1994.9 87.6 %reduce-scatter.13.cloned.1.call-done = f32[64,16]{1,0:T(8,128)} async-done(((f32[2048,16]{1,0:T(8,128)}), f32[64,16]{1,0:T(8,128)}) %reduce-scatter.13.cloned.1.call-update) | async-done | bytes 4112
  2084.0 143.2 %all-reduce.32.cloned.1.call-done = f32[2,2048,224]{2,0,1:T(2,128)} async-done(((f32[2,2048,224]{2,0,1:T(2,128)}), f32[2,2048,224]{2,0,1:T(2,128)}) %all-reduce.32.cloned.1.call-update) | async-done | bytes 3670032
  2228.7 1751.2 %reduce-scatter.11.cloned.1.call-done = f32[5,64,2048]{2,1,0:T(8,128)} async-done(((f32[5,2048,2048]{2,1,0:T(8,128)}), f32[5,64,2048]{2,1,0:T(8,128)}) %reduce-scatter.11.cloned.1.call-update) | async-done | bytes 2621456 | tf_op jit(solution)/shard_map/reduce_scatter | solution.py:414
  (1046 shorter events, 1274.5 us)
Async XLA Ops:
  7.2 884.5 %copy-start = (bf16[2048,256]{1,0:T(8,128)(2,1)S(1)}, bf16[2048,256]{1,0:T(8,128)(2,1)}, u32[]{:S(2)}) copy-start(bf16[2048,256]{1,0:T(8,128)(2,1)} %param.28) | copy-start | bytes 3145732
  7.2 63.2 %all-gather.5.cloned.1.call-start = ((), (), s32[]{:S(2)}) async-start(), calls=%async_computation.6 | async-start | bytes 2162688 | tf_op jit(solution)/shard_map/all_gather | solution.py:235
  7.9 299.4 %all-gather.7.cloned.1.call-start = ((), (), s32[]{:S(2)}) async-start(), calls=%async_computation.7 | async-start | bytes 43253760 | tf_op jit(solution)/shard_map/all_gather | solution.py:234
  8.7 765.0 %all-gather.9.cloned.1.call-start = ((), (), s32[]{:S(2)}) async-start(), calls=%async_computation.8 | async-start | bytes 4718592 | tf_op jit(solution)/shard_map/all_gather | solution.py:275
  9.9 70.3 %copy-start.102 = (f32[128]{0:T(128)}, f32[128]{0:T(128)S(1)}, u32[]{:S(2)}) copy-start(f32[128]{0:T(128)S(1)} %broadcast_multiply_fusion.3) | copy-start | bytes 1540
  13.6 672.2 %copy-start.98 = (f32[1,2048]{1,0:T(1,128)}, f32[1,2048]{1,0:T(1,128)S(1)}, u32[]{:S(2)}) copy-start(f32[1,2048]{1,0:T(1,128)S(1)} %get-tuple-element.2033) | copy-start | bytes 24580
  16.0 6.2 collective-permute-start.2
  84.4 228.6 %copy-start.75 = (f32[128,64]{0,1:T(8,128)}, f32[128,64]{0,1:T(8,128)S(1)}, u32[]{:S(2)}) copy-start(f32[128,64]{0,1:T(8,128)S(1)} %convolution_tanh_fusion.1) | copy-start | bytes 98308
  559.7 15.2 collective-permute-start
  578.4 15.0 collective-permute-start
  596.9 14.1 collective-permute-start
  614.5 13.9 collective-permute-start
  631.8 13.5 collective-permute-start
  648.8 12.6 collective-permute-start
  664.9 11.9 collective-permute-start
  699.2 192.4 %reduce-scatter.7.cloned.1.call-start = ((), (), s32[]{:S(2)}) async-start(), calls=%async_computation.9 | async-start | bytes 4718592 | tf_op jit(solution)/shard_map/reduce_scatter | solution.py:283
  795.0 186.2 %all-gather.11.cloned.1.call-start = ((), (), s32[]{:S(2)}) async-start(), calls=%async_computation.10 | async-start | bytes 4718592 | tf_op jit(solution)/shard_map/all_gather | solution.py:295
  899.0 368.3 %all-to-all-start = ((bf16[8,128,256]{2,1,0:T(8,128)(2,1)}), bf16[8,128,256]{2,1,0:T(8,128)(2,1)}, u32[]{:S(2)}, u32[]{:S(2)}) async-start(bf16[8,128,256]{2,1,0:T(8,128)(2,1)} %bitcast.752), calls=%async_computation.1 | async-start | bytes 1048576 | tf_op jit(solution)/shard_map/all_to_all | solution.py:288
  903.3 381.8 %reduce-scatter.9.cloned.1.call-start = ((), (), s32[]{:S(2)}) async-start(), calls=%async_computation.11 | async-start | bytes 4718592 | tf_op jit(solution)/shard_map/reduce_scatter | solution.py:305
  1020.8 961.4 %all-reduce.34.cloned.1.call-start = ((), (), s32[]{:S(2)}) async-start(), calls=%async_computation.15 | async-start | bytes 16777216 | tf_op jit(solution)/shard_map/psum | solution.py:309
  1284.6 797.9 %reduce-scatter.13.cloned.1.call-start = ((), (), s32[]{:S(2)}) async-start(), calls=%async_computation.13 | async-start | bytes 1081344
  1316.7 15.3 collective-permute-start.1
  1335.1 16.0 collective-permute-start.1
  1354.3 15.1 collective-permute-start.1
  1372.5 14.2 collective-permute-start.1
  1389.8 13.2 collective-permute-start.1
  1406.2 12.3 collective-permute-start.1
  1421.6 11.9 collective-permute-start.1
  1912.5 30.4 collective-permute-start.3
  1945.7 281.4 %all-reduce.32.cloned.1.call-start = ((), (), s32[]{:S(2)}) async-start(), calls=%async_computation.14 | async-start | bytes 8388608
  1957.3 2022.6 %reduce-scatter.11.cloned.1.call-start = ((), (), s32[]{:S(2)}) async-start(), calls=%async_computation.12 | async-start | bytes 86507520 | tf_op jit(solution)/shard_map/reduce_scatter | solution.py:414
  1988.0 1991.9 %copy-start.1 = (bf16[2048,256]{1,0:T(8,128)(2,1)S(1)}, bf16[2048,256]{1,0:T(8,128)(2,1)}, u32[]{:S(2)}) copy-start(bf16[2048,256]{1,0:T(8,128)(2,1)} %param.28) | copy-start | bytes 3145732
  (129 other events, 1164.8 us)
Sparse Core Ops, SparseCore 0:
  11.1 59.2 all-gather.4
  73.4 233.8 all-gather.6
  699.3 74.2 all-gather.8
  795.1 96.4 reduce-scatter.6
  896.8 84.3 all-gather.10
  1020.9 86.0 reduce-scatter.8
  1284.7 151.8 all-reduce.33
  1945.8 136.6 reduce-scatter.12
  2089.0 138.0 all-reduce.31
  2230.0 1749.8 reduce-scatter.10
where the time goes:
time: 4010 us; the launch traced here: 3990 us
  waiting for transfers between devices  2620 us (65%)
  matrix products  586 us (15%)
  other arithmetic  365 us (9%)
  local copies, waits for them, and re-layouts  315 us (8%)
  starting transfers between devices  51.2 us (1%)
    reduce_scatter x1, waiting for transfers between devices, shards(): lax.psum_scatter(pending[0], ('seg', 'seq'), scatter_dimension=1, tiled=T...  1750 us
    unnamed x12, waiting for transfers between devices  232 us
    all_gather x1, waiting for transfers between devices, shards(): lax.all_gather(tm_mats, ('seg', 'seq'), axis=1, tiled=True)  218 us
    dot_general x24, matrix products, one_block(): jnp.einsum('thk,tshk,shk->tsh', acceptor_patch, weights_pair, lookup_patc...  198 us
    ppermute x16, waiting for transfers between devices, passed_along(): return lax.ppermute(value, axis, pairs)  155 us
    dynamic_update_slice x48, other arithmetic, wkv_blocks(): lax.scan(one_block, start, (shaped(acceptor_lines), shaped(entering_looku...  103 us
    dynamic_slice x112, local copies, waits for them, and re-layouts, wkv_blocks(): lax.scan(one_block, start, (shaped(acceptor_lines), shaped(entering_looku...  90.8 us
    dot_general x32, matrix products, one_block(): jnp.einsum('ylt,ylr->ltr', lookup_patch * decay_until_end, payload_patch,...  83.4 us
  transfers between devices with their start and end apart: 27, of which 23 were waited for; matrix products, arithmetic and copies ran while one was open for 23% of the time, Pallas kernels for 0%

commit v1 on v0

v1 whole, which is shorter than its diff:
```python
import functools
import jax
import jax.numpy as jnp
from jax import lax
from jax.experimental import pallas as pl
from jax.experimental.pallas import tpu as pltpu
from jax.sharding import PartitionSpec as P

F = jnp.float32
HB = jnp.bfloat16
G = 64
B = 16
LANES = 128
MIX_RANK = 32
EPS_N = 1e-05
EPS_G = 0.00064
FLOOR = -120.0


def mm(a, b):
    return jnp.dot(a, b, preferred_element_type=F)


def mm_nt(a, b):
    return lax.dot_general(a, b, (((1,), (1,)), ((), ())), preferred_element_type=F)


def mm_tn(a, b):
    return lax.dot_general(a, b, (((0,), (0,)), ((), ())), preferred_element_type=F)


def head_mask(dt):
    i = lax.broadcasted_iota(jnp.int32, (LANES, LANES), 0) // G
    j = lax.broadcasted_iota(jnp.int32, (LANES, LANES), 1) // G
    return (i == j).astype(dt)


def head_sum(x, ones):
    hi = x.astype(HB)
    lo = (x - hi.astype(F)).astype(HB)
    return mm(hi, ones) + mm(lo, ones)


def block_sums(d):
    row = lax.broadcasted_iota(jnp.int32, d.shape, 1)
    run = d
    for step in (1, 2, 4, 8):
        run = run + jnp.where(row >= step, pltpu.roll(run, step, 1), 0.0)
    return run


def pair_rows(s):
    if s < 7:
        return 0, 16
    return 8, 8


def pair_weight(excl, incl, s):
    first, rows = pair_rows(s)
    gap = excl[:, first : first + rows, :] - incl[:, s : s + 1, :]
    if s != 7:
        u = first + lax.broadcasted_iota(jnp.int32, gap.shape, 1)
        gap = jnp.where(u > s, gap, -1e30)
    return jnp.exp(gap)


def silu_parts(g):
    sig = 1.0 / (1.0 + jnp.exp(-g))
    return sig, g * sig


def fwd_body(groups, nb, r_ref, k_ref, v_ref, rate_ref, gp_ref, vec_ref, s0_ref,
             z_ref, y_ref, st_ref, state):
    @pl.when(pl.program_id(0) == 0)
    def _():
        state[...] = s0_ref[...]

    ones = head_mask(HB)
    keep = head_mask(F)
    rows = nb * B
    for g in range(groups):
        cols = slice(g * LANES, (g + 1) * LANES)

        def blocks(ref):
            return ref[:, cols].astype(F).reshape(nb, B, LANES)

        r, k, v = blocks(r_ref), blocks(k_ref), blocks(v_ref)
        decay = jnp.maximum(-jnp.exp(blocks(rate_ref)), FLOOR)
        bonus, gn_g, gn_b = (vec_ref[i : i + 1, cols] for i in range(3))
        incl = block_sums(decay)
        excl = incl - decay
        last = incl[:, B - 1 : B, :]
        rq = (r * jnp.exp(excl)).astype(HB)
        kk = (k * jnp.exp(last - incl)).astype(HB)
        whole = jnp.exp(last)
        vb = v.astype(HB)
        from_state = []
        st = state[g]
        for b in range(nb):
            stb = st.astype(HB)
            st_ref[b, g] = stb
            from_state.append(mm_nt(rq[b], stb))
            st = st * whole[b] + keep * mm_tn(vb[b], kk[b])
        state[g] = st
        bits = []
        for s in range(B - 1):
            first, n = pair_rows(s)
            e = pair_weight(excl, incl, s)
            bits.append((r[:, first : first + n, :] * k[:, s : s + 1, :] * e).astype(HB).reshape(nb * n, LANES))
        bits.append((r * k * bonus).astype(HB).reshape(rows, LANES))
        scores = mm(jnp.concatenate(bits, axis=0), ones)
        at = 0
        low = jnp.zeros((nb, 8, LANES), F)
        high = jnp.zeros((nb, 8, LANES), F)
        for s in range(B - 1):
            first, n = pair_rows(s)
            part = scores[at : at + nb * n].reshape(nb, n, LANES) * v[:, s : s + 1, :]
            at += nb * n
            if n == 16:
                low = low + part[:, :8]
                high = high + part[:, 8:]
            else:
                high = high + part
        own = scores[at : at + rows].reshape(nb, B, LANES) * v
        y = jnp.concatenate([low, high], axis=1) + own
        y = y.reshape(rows, LANES) + jnp.concatenate(from_state, axis=0)
        y_ref[:, cols] = y
        center = y - head_sum(y, ones) * (1.0 / G)
        spread = head_sum(center * center, ones) * (1.0 / G)
        normed = center * lax.rsqrt(spread + EPS_G)
        _, act = silu_parts(gp_ref[:, cols])
        z_ref[:, cols] = ((normed * gn_g + gn_b) * act).astype(HB)


def wkv_forward(r, k, v, rate, gp, vec, start, step_tokens=128):
    tokens, width = r.shape
    groups = width // LANES
    nb = step_tokens // B
    steps = tokens // step_tokens
    row = pl.BlockSpec((step_tokens, width), lambda i: (i, 0))
    full = lambda shape: pl.BlockSpec(shape, lambda i: (0,) * len(shape))
    return pl.pallas_call(
        functools.partial(fwd_body, groups, nb),
        grid=(steps,),
        in_specs=[row, row, row, row, row, full(vec.shape), full(start.shape)],
        out_specs=[row, row, pl.BlockSpec((nb, groups, LANES, LANES), lambda i: (i, 0, 0, 0))],
        out_shape=[
            jax.ShapeDtypeStruct((tokens, width), HB),
            jax.ShapeDtypeStruct((tokens, width), F),
            jax.ShapeDtypeStruct((tokens // B, groups, LANES, LANES), HB),
        ],
        scratch_shapes=[pltpu.VMEM((groups, LANES, LANES), F)],
        cost_estimate=pl.CostEstimate(flops=tokens * width * 1024, transcendentals=tokens * width * 16, bytes_accessed=tokens * width * 40),
        name="wkv_forward",
    )(r, k, v, rate, gp, vec, start)


def bwd_body(groups, nb, r_ref, k_ref, v_ref, rate_ref, gp_ref, y_ref, gz_ref, vec_ref, st_ref,
             gr_ref, gk_ref, gv_ref, gg_ref, gd_ref, sums_ref, adj):
    first_step = pl.program_id(0) == 0

    @pl.when(first_step)
    def _():
        adj[...] = jnp.zeros_like(adj)
        sums_ref[...] = jnp.zeros_like(sums_ref)

    ones = head_mask(HB)
    keep = head_mask(F)
    rows = nb * B
    cols_of = []
    for s in range(B - 1):
        first, n = pair_rows(s)
        cols_of.append((s, first, n))
    for g in range(groups):
        cols = slice(g * LANES, (g + 1) * LANES)

        def blocks(x):
            return x.astype(F).reshape(nb, B, LANES)

        r, k, v = blocks(r_ref[:, cols]), blocks(k_ref[:, cols]), blocks(v_ref[:, cols])
        raw = -jnp.exp(blocks(rate_ref[:, cols]))
        decay = jnp.maximum(raw, FLOOR)
        bonus, gn_g, gn_b = (vec_ref[i : i + 1, cols] for i in range(3))
        y, gp, gz = y_ref[:, cols], gp_ref[:, cols], gz_ref[:, cols]
        center = y - head_sum(y, ones) * (1.0 / G)
        spread = head_sum(center * center, ones) * (1.0 / G)
        inv = lax.rsqrt(spread + EPS_G)
        normed = center * inv
        sig, act = silu_parts(gp)
        gated = gz * act
        gg_ref[:, cols] = (gz * (normed * gn_g + gn_b) * sig * (1.0 + gp * (1.0 - sig))).astype(HB)
        sums_ref[2:3, cols] += jnp.sum(gated * normed, axis=0, keepdims=True)
        sums_ref[3:4, cols] += jnp.sum(gated, axis=0, keepdims=True)
        gn = gated * gn_g
        gy = inv * (gn - head_sum(gn, ones) * (1.0 / G) - normed * (head_sum(gn * normed, ones) * (1.0 / G)))
        gy = gy.reshape(nb, B, LANES)
        incl = block_sums(decay)
        excl = incl - decay
        last = incl[:, B - 1 : B, :]
        to_start = jnp.exp(excl)
        to_end = jnp.exp(last - incl)
        whole = jnp.exp(last)
        rq = (r * to_start).astype(HB)
        kk = (k * to_end).astype(HB)
        vb = v.astype(HB)
        gyb = gy.astype(HB)
        lt = adj[g]
        gr_state, gk_state, gv_state, crossing = [None] * nb, [None] * nb, [None] * nb, [None] * nb
        for b in reversed(range(nb)):
            ltb = lt.astype(HB)
            stb = st_ref[b, g]
            gr_state[b] = mm(gyb[b], stb)
            gk_state[b] = mm(vb[b], ltb)
            gv_state[b] = mm_nt(kk[b], ltb)
            crossing[b] = jnp.sum(lt * stb.astype(F), axis=0, keepdims=True) * whole[b]
            lt = lt * whole[b] + keep * mm_tn(gyb[b], rq[b])
        adj[g] = lt
        stack = lambda parts: jnp.concatenate(parts, axis=0).reshape(nb, B, LANES)
        gr_in = stack(gr_state) * to_start
        gk_out = stack(gk_state) * to_end
        gv = stack(gv_state)
        e_bits, m_bits, a_bits, w_cache = [], [], [], []
        for s, first, n in cols_of:
            e = pair_weight(excl, incl, s)
            w_cache.append(e)
            a_bits.append((r[:, first : first + n] * k[:, s : s + 1] * e).astype(HB).reshape(nb * n, LANES))
            m_bits.append((gy[:, first : first + n] * v[:, s : s + 1]).astype(HB).reshape(nb * n, LANES))
        a_bits.append((r * k * bonus).astype(HB).reshape(rows, LANES))
        m_bits.append((gy * v).astype(HB).reshape(rows, LANES))
        scores = mm(jnp.concatenate(a_bits, axis=0), ones)
        dots = mm(jnp.concatenate(m_bits, axis=0), ones)
        at = 0
        low = jnp.zeros((nb, 8, LANES), F)
        high = jnp.zeros((nb, 8, LANES), F)
        p1, p2, p3 = [], [], []
        for (s, first, n), e in zip(cols_of, w_cache):
            m = dots[at : at + nb * n].reshape(nb, n, LANES)
            a = scores[at : at + nb * n].reshape(nb, n, LANES)
            at += nb * n
            me = m * e
            part = me * k[:, s : s + 1]
            if n == 16:
                low = low + part[:, :8]
                high = high + part[:, 8:]
            else:
                high = high + part
            mer = me * r[:, first : first + n]
            p1.append(mer)
            p2.append(a * gy[:, first : first + n])
            p3.append(mer * k[:, s : s + 1])
        a_own = scores[at : at + rows].reshape(nb, B, LANES)
        m_own = dots[at : at + rows].reshape(nb, B, LANES)
        gr = gr_in + jnp.concatenate([low, high], axis=1) + m_own * bonus * k
        gr_ref[:, cols] = gr.reshape(rows, LANES).astype(HB)
        p3.append(gr_in * r)
        p3.append(gk_out * k)
        total = sum(n for _, _, n in cols_of)
        col_s = jnp.concatenate([jnp.full((B, n), s, jnp.int32) for s, _, n in cols_of], axis=1)
        t = lax.broadcasted_iota(jnp.int32, (B, total), 0)
        pick = (col_s == t).astype(HB)
        col_u = jnp.concatenate([first + lax.broadcasted_iota(jnp.int32, (B, n), 1) for _, first, n in cols_of], axis=1)
        around = ((col_s < t) & (col_u > t)).astype(HB)
        i = lax.broadcasted_iota(jnp.int32, (B, B), 0)
        j = lax.broadcasted_iota(jnp.int32, (B, B), 1)
        around = jnp.concatenate([around, (j > i).astype(HB), (j < i).astype(HB)], axis=1)
        gk_pairs, gv_pairs, gd = [], [], []
        for b in range(nb):
            gk_pairs.append(mm(pick, jnp.concatenate([p[b] for p in p1], axis=0).astype(HB)))
            gv_pairs.append(mm(pick, jnp.concatenate([p[b] for p in p2], axis=0).astype(HB)))
            gd.append(mm(around, jnp.concatenate([p[b] for p in p3], axis=0).astype(HB)) + crossing[b])
        gk = gk_out + stack(gk_pairs) + m_own * bonus * r
        gk_ref[:, cols] = gk.reshape(rows, LANES).astype(HB)
        gv = gv + stack(gv_pairs) + a_own * gy
        gv_ref[:, cols] = gv.reshape(rows, LANES).astype(HB)
        grate = (stack(gd) * raw).reshape(rows, LANES)
        gd_ref[:, cols] = grate.astype(HB)
        sums_ref[0:1, cols] += jnp.sum((m_own * r * k).reshape(rows, LANES), axis=0, keepdims=True)
        sums_ref[1:2, cols] += jnp.sum(grate, axis=0, keepdims=True)


def wkv_backward(r, k, v, rate, gp, y, gz, vec, states, step_tokens=128):
    tokens, width = r.shape
    groups = width // LANES
    nb = step_tokens // B
    steps = tokens // step_tokens
    row = pl.BlockSpec((step_tokens, width), lambda i: (steps - 1 - i, 0))
    full = lambda shape: pl.BlockSpec(shape, lambda i: (0,) * len(shape))
    low = jax.ShapeDtypeStruct((tokens, width), HB)
    return pl.pallas_call(
        functools.partial(bwd_body, groups, nb),
        grid=(steps,),
        in_specs=[row] * 7 + [full(vec.shape), pl.BlockSpec((nb, groups, LANES, LANES), lambda i: (steps - 1 - i, 0, 0, 0))],
        out_specs=[row] * 5 + [full((8, width))],
        out_shape=[low] * 5 + [jax.ShapeDtypeStruct((8, width), F)],
        scratch_shapes=[pltpu.VMEM((groups, LANES, LANES), F)],
        cost_estimate=pl.CostEstimate(flops=tokens * width * 4096, transcendentals=tokens * width * 20, bytes_accessed=tokens * width * 60),
        name="wkv_backward",
    )(r, k, v, rate, gp, y, gz, vec, states)


def ring_of(count):
    deep = 4 if count % 4 == 0 and count >= 8 else 1
    wide = count // deep
    if deep == 1 or wide == 1:
        return list(range(count))
    path = []
    for z in range(deep):
        xs = range(1, wide) if z % 2 == 0 else range(wide - 1, 0, -1)
        path += [z * wide + x for x in xs]
    return path + [z * wide for z in reversed(range(deep))]


def ring_tables():
    count = lax.axis_size("seq")
    path = ring_of(count)
    place = [path.index(i) for i in range(count)]
    here = jnp.array(place, jnp.int32)[lax.axis_index("seq")]
    right = [(path[i], path[(i + 1) % count]) for i in range(count)]
    left = [(b, a) for a, b in right]
    return count, jnp.array(path, jnp.int32), here, right, left


def gather_seq(part, dim):
    count, path, here, right, left = ring_tables()
    size = part.shape[dim]
    shape = list(part.shape)
    shape[dim] = size * count
    out = jnp.zeros(shape, part.dtype)

    def put(out, piece, away):
        owner = path[(here + away) % count]
        return lax.dynamic_update_slice_in_dim(out, piece, owner * size, dim)

    out = put(out, part, 0)
    going_right = going_left = part
    for step in range(1, count // 2 + 1):
        going_right = lax.ppermute(going_right, "seq", right)
        if step < count - count // 2:
            going_left = lax.ppermute(going_left, "seq", left)
            out = put(out, going_left, step)
        out = put(out, going_right, -step)
    return out


def scatter_seq(piece_of):
    count, path, here, right, left = ring_tables()
    far = count // 2
    near = count - 1 - far

    def term(away):
        return piece_of(path[(here + away) % count])

    going_right = going_left = None
    for step in range(far, 0, -1):
        going_right = term(step) if going_right is None else term(step) + going_right.astype(F)
        going_right = lax.ppermute(going_right.astype(HB), "seq", right)
        if step <= near:
            going_left = term(-step) if going_left is None else term(-step) + going_left.astype(F)
            going_left = lax.ppermute(going_left.astype(HB), "seq", left)
    return term(0) + going_right.astype(F) + going_left.astype(F)


def exchange_seq(value, split, join):
    return lax.all_to_all(value, "seq", split_axis=split, concat_axis=join, tiled=True)


def previous(rows):
    return jnp.concatenate([jnp.zeros_like(rows[:1]), rows[:-1]], axis=0)


def following(rows):
    return jnp.concatenate([rows[1:], jnp.zeros_like(rows[:1])], axis=0)


def normalize(values):
    center = values - jnp.mean(values, axis=-1, keepdims=True)
    inverse = lax.rsqrt(jnp.mean(center * center, axis=-1, keepdims=True) + EPS_N)
    return center * inverse, inverse


def normalize_back(grad, normed, inverse, gain):
    scaled = grad * gain
    return inverse * (
        scaled
        - jnp.mean(scaled, axis=-1, keepdims=True)
        - normed * jnp.mean(scaled * normed, axis=-1, keepdims=True)
    )


def shards(tokens, tm_mats, low_rank, params, opening, cm_key, cm_value, cm_recept, out_grad):
    rows, width = tokens.shape
    count = lax.axis_size("seq")
    here = lax.axis_index("seq")
    total = rows * count
    cols = width // count
    mix_width = 5 * MIX_RANK
    g1, b1, mu_x = params[0], params[1], params[2]
    g2, b2, cmu_k, cmu_r = params[12], params[13], params[14], params[15]

    def my_cols(array):
        return lax.dynamic_slice_in_dim(array, here * cols, cols, array.ndim - 1)

    def my_rows(array):
        return lax.dynamic_slice_in_dim(array, here * rows, rows, 0)

    x = gather_seq(tokens, 0).astype(F)
    rank = lax.all_gather(low_rank, ("seg", "seq"), axis=1, tiled=True)
    mats = lax.all_gather(exchange_seq(tm_mats[:4], 2, 1), "seg", axis=1, tiled=True)
    w_output = lax.all_gather(tm_mats[4], ("seg", "seq"), axis=0, tiled=True)
    go_cols = exchange_seq(out_grad, 1, 0).astype(F)
    down_mix, down_decay = rank[0][:, :mix_width], rank[0][:, mix_width:]
    up_mix = rank[1][:, :mix_width]
    up_decay = lax.dynamic_slice_in_dim(rank[1], here * cols, cols, 0)[:, mix_width:]

    xhat, x_inv = normalize(x)
    xn = xhat * g1 + b1
    dx = previous(xn) - xn
    xm = (xn + dx * mu_x).astype(HB)
    m_f = jnp.tanh(mm(xm, down_mix))
    m = m_f.astype(HB)

    def group(array, j):
        return array[:, j * MIX_RANK : (j + 1) * MIX_RANK]

    lerp = [params[3 + j] + mm_nt(group(m, j), group(up_mix, j)) for j in range(5)]
    x_w, x_k, x_v, x_r, x_g = ((xn + dx * f).astype(HB) for f in lerp)
    e_f = jnp.tanh(mm(x_w, down_decay))
    e = e_f.astype(HB)
    rate = my_cols(params[8]) + mm_nt(e, up_decay)
    r = mm(x_r, mats[0]).astype(HB)
    k = mm(x_k, mats[1]).astype(HB)
    v = mm(x_v, mats[2]).astype(HB)
    gp = mm(x_g, mats[3])
    vec = my_cols(jnp.concatenate([params[9:12], jnp.zeros((5, width), F)], axis=0))
    groups = cols // LANES
    heads = lax.dynamic_slice_in_dim(opening[0], here * (cols // G), cols // G, 0)
    start = jnp.einsum(
        "ghkv,hi->ghvik", heads.reshape(groups, LANES // G, G, G), jnp.eye(LANES // G, dtype=F),
        precision=lax.Precision.HIGHEST,
    ).reshape(groups, LANES, LANES)
    z_cols, y, states = wkv_forward(r, k, v, rate, gp, vec, start)
    z = gather_seq(z_cols, 1)
    x1 = x + mm(z, w_output)

    x1hat, x1_inv = normalize(x1)
    xs = (x1hat * g2 + b2).astype(HB).astype(F)
    dxs = previous(xs) - xs
    ck = (xs + dxs * cmu_k).astype(HB)
    cr = (xs + dxs * cmu_r).astype(HB)
    sg = jax.nn.sigmoid(mm(cr, cm_recept))
    gkv = gather_seq((go_cols * sg).astype(HB), 1)
    hp = mm(ck, cm_key)
    hid = jnp.square(jax.nn.relu(hp)).astype(HB)
    kv = scatter_seq(lambda owner: mm(hid, lax.dynamic_slice_in_dim(cm_value, owner * cols, cols, 1)))
    cm_rows = exchange_seq((sg * kv).astype(HB), 0, 1)
    block_out = (my_rows(x1) + cm_rows.astype(F)).astype(HB)
    gsp = (go_cols * kv * sg * (1.0 - sg)).astype(HB)
    ghp = (mm_nt(gkv, cm_value) * (2.0 * jax.nn.relu(hp))).astype(HB)
    cm_value_grad = mm_tn(hid, gkv)
    cm_key_grad = mm_tn(ck, ghp)
    cm_recept_grad = mm_tn(cr, gsp)
    cm_grads = tuple(
        lax.psum(value.astype(HB), "seg").astype(F) for value in (cm_key_grad, cm_value_grad, cm_recept_grad)
    )
    gck = mm_nt(ghp, cm_key)
    gcr = mm_nt(gsp, cm_recept)
    d_cmu_k = jnp.sum(gck * dxs, axis=0)
    d_cmu_r = jnp.sum(gcr * dxs, axis=0)
    gxs_part = gck * (1.0 - cmu_k) + gcr * (1.0 - cmu_r) + following(gck * cmu_k + gcr * cmu_r)
    gxs = scatter_seq(lambda owner: lax.dynamic_slice_in_dim(gxs_part, owner * rows, rows, 0))
    own_hat, own_inv = my_rows(x1hat), my_rows(x1_inv)
    gx1 = out_grad.astype(F) + normalize_back(gxs, own_hat, own_inv, g2)
    d_g2 = jnp.sum(gxs * own_hat, axis=0)
    d_b2 = jnp.sum(gxs, axis=0)

    go1 = gather_seq(gx1.astype(HB), 0)
    gz = mm_nt(go1, lax.dynamic_slice_in_dim(w_output, here * cols, cols, 0))
    gr, gk, gv, ggp, grb, sums = wkv_backward(r, k, v, rate, gp, y, gz, vec, states)
    d_mats = jnp.stack(
        [mm_tn(a, b).astype(HB) for a, b in ((x_r, gr), (x_k, gk), (x_v, gv), (x_g, ggp), (z, my_cols(go1)))]
    )
    d_mats = lax.psum_scatter(d_mats, "seg", scatter_dimension=1, tiled=True)
    d_mats = exchange_seq(d_mats, 1, 2).astype(F)
    d_up_decay = mm_tn(grb, e)
    ge = (mm(grb, up_decay) * (1.0 - e_f * e_f)).astype(HB)
    d_down_decay = mm_tn(x_w, ge)
    gx = [
        mm_nt(ge, down_decay),
        mm_nt(gk, mats[1]),
        mm_nt(gv, mats[2]),
        mm_nt(gr, mats[0]),
        mm_nt(ggp, mats[3]),
    ]
    gdx = gx[0] * lerp[0] + gx[1] * lerp[1] + gx[2] * lerp[2] + gx[3] * lerp[3] + gx[4] * lerp[4]
    gmix = [a * dx for a in gx]
    d_mu = [jnp.sum(a, axis=0) for a in gmix]
    gmix = [a.astype(HB) for a in gmix]
    d_up_mix = jnp.concatenate([mm_tn(a, group(m, j)) for j, a in enumerate(gmix)], axis=1)
    gm = jnp.concatenate([mm(a, group(up_mix, j)) for j, a in enumerate(gmix)], axis=1)
    gm = (gm * (1.0 - m_f * m_f)).astype(HB)
    d_down_mix = mm_tn(xm, gm)
    gxm = mm_nt(gm, down_mix)
    d_mu_x = jnp.sum(gxm * dx, axis=0)
    gdx = gdx + gxm * mu_x
    gxn_part = gx[0] + gx[1] + gx[2] + gx[3] + gx[4] + gxm - gdx + following(gdx)
    gxn = scatter_seq(lambda owner: lax.dynamic_slice_in_dim(gxn_part, owner * rows, rows, 0))
    own_hat, own_inv = my_rows(xhat), my_rows(x_inv)
    input_grad = gx1 + normalize_back(gxn, own_hat, own_inv, g1)
    d_g1 = jnp.sum(gxn * own_hat, axis=0)
    d_b1 = jnp.sum(gxn, axis=0)

    def spread_out(array, dim):
        shape = list(array.shape)
        shape[dim] = width
        return lax.dynamic_update_slice_in_dim(jnp.zeros(shape, F), array, here * cols, dim)

    of_heads = spread_out(sums, 1)
    vectors = jnp.stack(
        [d_g1, d_b1, d_mu_x, *d_mu, of_heads[1], of_heads[0], of_heads[2], of_heads[3], d_g2, d_b2, d_cmu_k, d_cmu_r]
    )
    packed = jnp.concatenate(
        [d_down_mix, d_down_decay, d_up_mix, spread_out(d_up_decay, 0), vectors.T, jnp.zeros((width, 48), F)], axis=1
    )
    packed = lax.psum_scatter(packed, ("seg", "seq"), scatter_dimension=0, tiled=True)
    half = low_rank.shape[2]
    rank_grad = jnp.stack([packed[:, :half], packed[:, half : 2 * half]])
    vectors_grad = packed[:, 2 * half : 2 * half + 16].T
    return (block_out, input_grad, d_mats, rank_grad, vectors_grad, *cm_grads)


def solution(mesh):
    by_token = P(("seg", "seq"), None)
    in_specs = (
        by_token,
        P(None, ("seg", "seq"), None),
        P(None, ("seg", "seq"), None),
        P(),
        P("seg", None, None, None),
        P(None, "seq"),
        P("seq", None),
        P(None, "seq"),
        by_token,
    )
    out_specs = (
        by_token,
        by_token,
        P(None, ("seg", "seq"), None),
        P(None, ("seg", "seq"), None),
        P(None, ("seg", "seq")),
        P(None, "seq"),
        P("seq", None),
        P(None, "seq"),
    )
    return jax.shard_map(shards, mesh=mesh, in_specs=in_specs, out_specs=out_specs, check_vma=False)
```

time: 4010 us -> 1020 us (0.25)
  waiting for transfers between devices: 2620 us -> 351 us
  matrix products: 586 us -> 243 us
  other arithmetic: 365 us -> 117 us
  local copies, waits for them, and re-layouts: 315 us -> 99.6 us
  Pallas kernels: 0 us -> 60.9 us
    reduce_scatter x3 -> x1, waiting for transfers between devices: 1820 us -> 0.01 us  [shards(): d_mats = lax.psum_scatter(d_mats, 'seg', scatter_dimension=1, tiled=True)]
    all_gather x4 -> x3, waiting for transfers between devices: 415 us -> 0.01 us  [the longest x1 0.01 us: shards(): rank = lax.all_gather(low_rank, ('seg', 'seq'), axis=1, tiled=True)]
    dot_general x143 -> x55, matrix products: 586 us -> 243 us  [the longest x16 141 us: mm_nt(): lax.dot_general(a, b, (((1,), (1,)), ((), ())), preferred_element_type=F)]
    unnamed x12 -> x7, waiting for transfers between devices: 232 us -> 106 us
    dynamic_update_slice x48 -> x1, other arithmetic: 103 us -> 2.55 us  [put(): return lax.dynamic_update_slice_in_dim(out, piece, owner * size, dim)]
    dynamic_slice x112 -> x6, local copies, waits for them, and re-layouts: 90.8 us -> 5.69 us  [the longest x2 1.83 us: my_cols(): return lax.dynamic_slice_in_dim(array, here * cols, cols, array.ndim - 1)]
    ppermute x16 -> x49, waiting for transfers between devices: 155 us -> 227 us  [the longest x16 117 us: gather_seq(): going_right = lax.ppermute(going_right, 'seq', right)]
    reduce_sum x60 -> x6, other arithmetic: 88 us -> 26.1 us  [the longest x1 17.5 us: shards(): d_cmu_r = jnp.sum(gcr * dxs, axis=0)]
  transfers between devices with their start and end apart: 27 -> 58, of which waited for: 23 -> 37; matrix products, arithmetic and copies ran while one was open for 23% -> 36% of each run, Pallas kernels for 0% -> 2%
where the time goes in v1:
time: 1020 us; the launch traced here: 1010 us
  waiting for transfers between devices  351 us (34%)
  matrix products  243 us (24%)
  other arithmetic  117 us (11%)
  local copies, waits for them, and re-layouts  99.6 us (10%)
  starting transfers between devices  72.6 us (7%)
  Pallas kernels  60.9 us (6%)
  blocking collectives  37.2 us (4%)
  between operations  34.3 us (3%)
    dot_general x16, matrix products, mm_nt(): lax.dot_general(a, b, (((1,), (1,)), ((), ())), preferred_element_type=F)  141 us
    ppermute x16, waiting for transfers between devices, gather_seq(): going_right = lax.ppermute(going_right, 'seq', right)  117 us
    unnamed x7, waiting for transfers between devices  106 us
    ppermute x12, waiting for transfers between devices, scatter_seq(): going_right = lax.ppermute(going_right.astype(HB), 'seq', right)  79.7 us
    dot_general x23, matrix products, mm(): return jnp.dot(a, b, preferred_element_type=F)  58.1 us
    dot_general x16, matrix products, mm_tn(): lax.dot_general(a, b, (((0,), (0,)), ((), ())), preferred_element_type=F)  44.1 us
    pallas_call x1, Pallas kernels, wkv_backward(): pl.pallas_call(functools.partial(bwd_body, groups, nb), grid=(steps,), in...  39.4 us
    all_to_all x1, blocking collectives, exchange_seq(): lax.all_to_all(value, 'seq', split_axis=split, concat_axis=join, tiled=True)  37.2 us
  transfers between devices with their start and end apart: 58, of which 37 were waited for; matrix products, arithmetic and copies ran while one was open for 36% of the time, Pallas kernels for 2%

profile of v1, /device:TPU:0, one launch (start us, length us, event | category | flops | bytes accessed | tf_op | source)
XLA Modules:
  0.0 1014.9 jit_solution(15041455792233827806)
XLA Ops:
  15.8 37.2 %all_to_all.53 = bf16[8,2,32768]{2,1,0:T(2,128)(2,1)} all-to-all(bf16[8,2,32768]{2,1,0:T(2,128)(2,1)} %reshape.236), channel_id=1, replica_groups=mesh['seg'=4,'seq'=8] {'seq'}, dimensions={0} | all-to-all | bytes 2097152 | tf_op jit(solution)/shard_map/all_to_all | solution.py:364
  64.2 12.9 %collective-permute-done.1 = bf16[128,2048]{1,0:T(8,128)(2,1)S(1)} collective-permute-done((bf16[128,2048]{1,0:T(8,128)(2,1)}, bf16[128,2048]{1,0:T(8,128)(2,1)S(1)}, u32[]{:S(2)}, u32[]{:S(2)}) %collective-permute-start.1) | collective-permute-done | bytes 524320 | tf_op jit(solution)/shard_map/ppermute | solution.py:337
  101.9 8.7 collective-permute-done.5
  111.7 10.4 %collective-permute-done.6 = bf16[128,2048]{1,0:T(8,128)(2,1)S(1)} collective-permute-done((bf16[128,2048]{1,0:T(8,128)(2,1)S(1)}, bf16[128,2048]{1,0:T(8,128)(2,1)S(1)}, u32[]{:S(2)}, u32[]{:S(2)}) %collective-permute-start.6) | collective-permute-done | bytes 524320 | tf_op jit(solution)/shard_map/ppermute | solution.py:337
  126.1 9.7 add_convert_fusion.8
  161.4 22.7 %add_convert_fusion.3 = (bf16[1024,2048]{1,0:T(8,128)(2,1)}, bf16[1024,2048]{1,0:T(8,128)(2,1)}, bf16[1024,2048]{1,0:T(8,128)(2,1)}, bf16[1024,2048]{1,0:T(8,128...) fusion(f32[1024,2048]{1,0:T(8,128)S(1)} %bitcast.211, f32[2048]{0:T(1024)S(1)} %bitcast.233, ...), kind=kOutput, calls=%fused_computation.22 | convolution fusion | flops 186646528 | bytes 76152832 | tf_op jit(solution)/shard_map/dot_general | solution.py:25
  203.7 21.5 %wkv_forward.1 = (bf16[1024,256]{1,0:T(8,128)(2,1)}, f32[1024,256]{1,0:T(8,128)}, bf16[64,2,128,128]{3,2,1,0:T(8,128)(2,1)}) custom-call(bf16[1024,256]{1,0:T(8,128)(2,1)} %convolution_convert_fusion.12.r_ref, bf16[1024,256]{1,0:T(8,128)(2,1)} %convolution_convert_fusion.11.k_ref, bf16[1024,256]{1,0:T(8,128)(2,1)} %convolution_convert_fusion.10.v_ref, ...), custom_call_target="tpu_custom_call" | custom-call | flops 268435456 | bytes 10485760 | tf_op jit(solution)/shard_map/wkv_forward/pallas_call | solution.py:142
  227.3 10.1 collective-permute-done.8
  239.5 9.8 collective-permute-done.10
  279.8 13.6 %fusion.103 = (f32[1024]{0:T(1024)S(1)}, f32[1024,2048]{1,0:T(8,128)S(1)}) fusion(bf16[1024,2048]{1,0:T(8,128)(2,1)} %constant_dynamic-update-slice_fusion.8, bf16[1,2048,2048]{2,1,0:T(8,128)(2,1)} %all-gather.9.cloned.1.call-done, bf16[1024,2048]{1,0:T(8,128)(2,1)} %copy-done.2), kind=kOutput, calls=%fused_computation.262 | convolution fusion | flops 8596225024 | bytes 25169920 | tf_op jit(solution)/shard_map/dot_general | solution.py:21
  320.5 9.8 collective-permute-done.14
  334.7 8.3 collective-permute-done.15
  347.9 6.5 collective-permute-done.16
  361.6 6.8 collective-permute-done.17
  374.7 11.3 %collective-permute-done.22 = bf16[1024,256]{1,0:T(8,128)(2,1)} collective-permute-done((bf16[1024,256]{1,0:T(8,128)(2,1)S(1)}, bf16[1024,256]{1,0:T(8,128)(2,1)}, u32[]{:S(2)}, u32[]{:S(2)}) %collective-permute-start.22) | collective-permute-done | bytes 524320 | tf_op jit(solution)/shard_map/ppermute | solution.py:337
  389.2 10.8 %collective-permute-done.24 = bf16[1024,256]{1,0:T(8,128)(2,1)} collective-permute-done((bf16[1024,256]{1,0:T(8,128)(2,1)}, bf16[1024,256]{1,0:T(8,128)(2,1)}, u32[]{:S(2)}, u32[]{:S(2)}) %collective-permute-start.24) | collective-permute-done | bytes 524320 | tf_op jit(solution)/shard_map/ppermute | solution.py:337
  406.0 6.4 collective-permute-done.26
  441.0 17.5 %multiply_reduce_fusion = (f32[2048]{0:T(1024)}, f32[2048]{0:T(1024)}, f32[1024,2048]{1,0:T(8,128)}) fusion(f32[1024,2048]{1,0:T(8,128)} %copy-done.6, bf16[1024,2048]{1,0:T(8,128)(2,1)S(1)} %copy-done.5, f32[1023,2048]{1,0:T(8,128)} %copy-done.7, f32[1024,2048]{1,0:T(8,128)} %copy-done.23, f32[1023,2048]{1,0:T(8,128)} %fusion.3, f32[2048]{0:T(1024)S(1)} %bitcast.250, ...), kind=kLoop, calls=%fused_computation.11 | loop fusion | flops 20967424 | bytes 46153728 | tf_op jit(solution)/shard_map/reduce_sum | solution.py:468
  460.7 10.9 %collective-permute-done.28 = bf16[128,2048]{1,0:T(8,128)(2,1)S(1)} collective-permute-done((bf16[128,2048]{1,0:T(8,128)(2,1)S(1)}, bf16[128,2048]{1,0:T(8,128)(2,1)S(1)}, u32[]{:S(2)}, u32[]{:S(2)}) %collective-permute-start.28) | collective-permute-done | bytes 524320 | tf_op jit(solution)/shard_map/ppermute | solution.py:356
  475.0 8.3 collective-permute-done.29
  485.0 9.9 collective-permute-done.30
  498.7 7.2 collective-permute-done.33
  508.6 10.6 %collective-permute-done.34 = bf16[128,2048]{1,0:T(8,128)(2,1)} collective-permute-done((bf16[128,2048]{1,0:T(8,128)(2,1)S(1)}, bf16[128,2048]{1,0:T(8,128)(2,1)}, u32[]{:S(2)}, u32[]{:S(2)}) %collective-permute-start.34) | collective-permute-done | bytes 524320 | tf_op jit(solution)/shard_map/ppermute | solution.py:359
  527.4 9.9 collective-permute-done.36
  570.6 39.4 %wkv_backward.1 = (bf16[1024,256]{1,0:T(8,128)(2,1)}, bf16[1024,256]{1,0:T(8,128)(2,1)}, bf16[1024,256]{1,0:T(8,128)(2,1)}, bf16[1024,256]{1,0:T(8,128)(2,1)}, b...) custom-call(bf16[1024,256]{1,0:T(8,128)(2,1)} %convolution_convert_fusion.12.r_ref, ...), custom_call_target="tpu_custom_call" | custom-call | flops 1073741824 | bytes 15728640 | tf_op jit(solution)/shard_map/wkv_backward/pallas_call | solution.py:289
  663.4 25.7 %multiply_convert_fusion = (bf16[1024,2048]{1,0:T(8,128)(2,1)}, bf16[1024,2048]{1,0:T(8,128)(2,1)}, bf16[1024,2048]{1,0:T(8,128)(2,1)}, bf16[1024,2048]{1,0:T(8,...) fusion(f32[1024,2048]{1,0:T(8,128)} %get-tuple-element.85, f32[1024,2048]{1,0:T(8,128)} %fusion.29, ...), kind=kOutput, calls=%fused_computation.33 | convolution fusion | flops 1094713344 | bytes 72876032 | tf_op jit(solution)/shard_map/dot_general | solution.py:25
  698.7 38.6 %multiply_reduce_fusion.4 = (f32[2048]{0:T(1024)S(1)}, f32[2048]{0:T(1024)S(1)}, f32[2048]{0:T(1024)S(1)}, f32[2048]{0:T(1024)S(1)}, f32[2048]{0:T(1024)S(1)}, /...) fusion(f32[1024,2048]{1,0:T(8,128)} %get-tuple-element.150, f32[1024,2048]{1,0:T(8,128)} %get-tuple-element.85, ...), kind=kOutput, calls=%fused_computation.32 | convolution fusion | flops 729796608 | bytes 110395392 | tf_op jit(solution)/shard_map/dot_general | solution.py:25
  737.3 8.6 slice.227
  745.9 28.6 %pad_add_fusion = f32[1024,2048]{1,0:T(8,128)} fusion(f32[1023,2048]{1,0:T(8,128)} %slice.227, f32[1024,2048]{1,0:T(8,128)} %get-tuple-element.86, f32[1024,2048]{1,0:T(8,128)} %get-tuple-element.151, f32[1024,2048]{1,0:T(8,128)} %get-tuple-element.150, f32[1024,2048]{1,0:T(8,128)} %fusion.29, f32[1024,2048]{1,0:T(8,128)} %fusion.31, ...), kind=kLoop, calls=%fused_computation.14 | loop fusion | flops 14680064 | bytes 75489280 | tf_op jit(solution)/shard_map/add | solution.py:505
  792.2 6.8 collective-permute-done.43
  851.4 17.7 %all-to-all-done.1 = bf16[8,128,256]{2,1,0:T(8,128)(2,1)S(1)} async-done(((bf16[8,128,256]{2,1,0:T(8,128)(2,1)}), bf16[8,128,256]{2,1,0:T(8,128)(2,1)S(1)}, u32[]{:S(2)}, u32[]{:S(2)}) %all-to-all-start.1) | async-done | bytes 524320 | tf_op jit(solution)/shard_map/all_to_all | solution.py:364
  891.1 105.7 %reduce-scatter.7.cloned.1.call-done = f32[64,512]{1,0:T(8,128)} async-done(((f32[2048,512]{1,0:T(8,128)}), f32[64,512]{1,0:T(8,128)}) %reduce-scatter.7.cloned.1.call-update) | async-done | bytes 131088
  (467 shorter events, 418.4 us)
Async XLA Ops:
  7.2 128.6 %all-gather.5.cloned.1.call-start = ((), (), s32[]{:S(2)}) async-start(), calls=%async_computation.6 | async-start | bytes 2162688 | tf_op jit(solution)/shard_map/all_gather | solution.py:407
  7.9 182.0 %all-gather.7.cloned.1.call-start = ((), (), s32[]{:S(2)}) async-start(), calls=%async_computation.7 | async-start | bytes 5242880 | tf_op jit(solution)/shard_map/all_gather | solution.py:408
  58.5 221.2 %all-gather.9.cloned.1.call-start = ((), (), s32[]{:S(2)}) async-start(), calls=%async_computation.9 | async-start | bytes 8650752 | tf_op jit(solution)/shard_map/all_gather | solution.py:409
  60.3 16.7 %collective-permute-start.1 = (bf16[128,2048]{1,0:T(8,128)(2,1)}, bf16[128,2048]{1,0:T(8,128)(2,1)S(1)}, u32[]{:S(2)}, u32[]{:S(2)}) collective-permute-start(bf16[128,2048]{1,0:T(8,128)(2,1)} %param.23), channel_id=1, source_target_pairs={{1,3},{3,5},{5,7},{7,6},{6,4},{4,2},{2,0},{0,1},{9,11},{11,13},{13... | collective-permute-start | bytes 1572872 | tf_op jit(solution)/shard_map/ppermute | solution.py:337
  61.9 16.8 %collective-permute-start = (bf16[128,2048]{1,0:T(8,128)(2,1)}, bf16[128,2048]{1,0:T(8,128)(2,1)S(1)}, u32[]{:S(2)}, u32[]{:S(2)}) collective-permute-start(bf16[128,2048]{1,0:T(8,128)(2,1)} %param.23), channel_id=1, source_target_pairs={{3,1},{5,3},{7,5},{6,7},{4,6},{2,4},{0,2},{1,0},{11,9},{13,11},{15... | collective-permute-start | bytes 1572872 | tf_op jit(solution)/shard_map/ppermute | solution.py:339
  77.1 21.5 %collective-permute-start.3 = (bf16[128,2048]{1,0:T(8,128)(2,1)S(1)}, bf16[128,2048]{1,0:T(8,128)(2,1)S(1)}, u32[]{:S(2)}, u32[]{:S(2)}) collective-permute-start(bf16[128,2048]{1,0:T(8,128)(2,1)S(1)} %collective-permute-done.1), channel_id=1, source_target_pairs={{1,3},{3,5},{5,7},{7,6},{6,4},{4,2},{2,0},{0,1},{9,11},{11,13},{13... | collective-permute-start | bytes 1572872 | tf_op jit(solution)/shard_map/ppermute | solution.py:337
  78.7 20.0 %collective-permute-start.2 = (bf16[128,2048]{1,0:T(8,128)(2,1)S(1)}, bf16[128,2048]{1,0:T(8,128)(2,1)}, u32[]{:S(2)}, u32[]{:S(2)}) collective-permute-start(bf16[128,2048]{1,0:T(8,128)(2,1)S(1)} %collective-permute-done), channel_id=1, source_target_pairs={{3,1},{5,3},{7,5},{6,7},{4,6},{2,4},{0,2},{1,0},{11,9},{13,11},{15... | collective-permute-start | bytes 1572872 | tf_op jit(solution)/shard_map/ppermute | solution.py:339
  98.5 12.1 %collective-permute-start.5 = (bf16[128,2048]{1,0:T(8,128)(2,1)S(1)}, bf16[128,2048]{1,0:T(8,128)(2,1)S(1)}, u32[]{:S(2)}, u32[]{:S(2)}) collective-permute-start(bf16[128,2048]{1,0:T(8,128)(2,1)S(1)} %collective-permute-done.3), channel_id=1, source_target_pairs={{1,3},{3,5},{5,7},{7,6},{6,4},{4,2},{2,0},{0,1},{9,11},{11,13},{13... | collective-permute-start | bytes 1572872 | tf_op jit(solution)/shard_map/ppermute | solution.py:337
  98.7 12.9 %collective-permute-start.4 = (bf16[128,2048]{1,0:T(8,128)(2,1)}, bf16[128,2048]{1,0:T(8,128)(2,1)S(1)}, u32[]{:S(2)}, u32[]{:S(2)}) collective-permute-start(bf16[128,2048]{1,0:T(8,128)(2,1)} %collective-permute-done.2), channel_id=1, source_target_pairs={{3,1},{5,3},{7,5},{6,7},{4,6},{2,4},{0,2},{1,0},{11,9},{13,11},{15... | collective-permute-start | bytes 1572872 | tf_op jit(solution)/shard_map/ppermute | solution.py:339
  225.2 12.2 %collective-permute-start.8 = (bf16[1024,256]{1,0:T(8,128)(2,1)}, bf16[1024,256]{1,0:T(8,128)(2,1)S(1)}, u32[]{:S(2)}, u32[]{:S(2)}) collective-permute-start(bf16[1024,256]{1,0:T(8,128)(2,1)} %get-tuple-element.17), channel_id=1, source_target_pairs={{1,3},{3,5},{5,7},{7,6},{6,4},{4,2},{2,0},{0,1},{9,11},{11,13},{13... | collective-permute-start | bytes 1572872 | tf_op jit(solution)/shard_map/ppermute | solution.py:337
  237.5 24.4 %collective-permute-start.9 = (bf16[1024,256]{1,0:T(8,128)(2,1)}, bf16[1024,256]{1,0:T(8,128)(2,1)}, u32[]{:S(2)}, u32[]{:S(2)}) collective-permute-start(bf16[1024,256]{1,0:T(8,128)(2,1)} %collective-permute-done.7), channel_id=1, source_target_pairs={{3,1},{5,3},{7,5},{6,7},{4,6},{2,4},{0,2},{1,0},{11,9},{13,11},{15... | collective-permute-start | bytes 1572872 | tf_op jit(solution)/shard_map/ppermute | solution.py:339
  249.3 19.8 %collective-permute-start.12 = (bf16[1024,256]{1,0:T(8,128)(2,1)}, bf16[1024,256]{1,0:T(8,128)(2,1)}, u32[]{:S(2)}, u32[]{:S(2)}) collective-permute-start(bf16[1024,256]{1,0:T(8,128)(2,1)} %collective-permute-done.10), channel_id=1, source_target_pairs={{1,3},{3,5},{5,7},{7,6},{6,4},{4,2},{2,0},{0,1},{9,11},{11,13},{13... | collective-permute-start | bytes 1572872 | tf_op jit(solution)/shard_map/ppermute | solution.py:337
  250.2 110.6 %all-to-all-start.2 = ((bf16[128,8,256]{2,0,1:T(8,128)(2,1)}), bf16[128,8,256]{2,0,1:T(8,128)(2,1)S(1)}, u32[]{:S(2)}, u32[]{:S(2)}) async-start(bf16[128,8,256]{2,0,1:T(8,128)(2,1)} %bitcast.208), calls=%async_computation.2 | async-start | bytes 1048576 | tf_op jit(solution)/shard_map/all_to_all | solution.py:364
  256.3 591.6 %reduce-scatter.5.cloned.1.call-start = ((), (), s32[]{:S(2)}) async-start(), calls=%async_computation.8 | async-start | bytes 6553600 | tf_op jit(solution)/shard_map/reduce_scatter | solution.py:482
  314.9 17.0 %collective-permute-start.18 = (bf16[1024,256]{1,0:T(8,128)(2,1)S(1)}, bf16[1024,256]{1,0:T(8,128)(2,1)S(1)}, u32[]{:S(2)}, u32[]{:S(2)}) collective-permute-start(bf16[1024,256]{1,0:T(8,128)(2,1)S(1)} %convolution_convert_fusion.8), channel_id=1, source_target_pairs={{3,1},{5,3},{7,5},{6,7},{4,6},{2,4},{0,2},{1,0},{11,9},{13,11},{15... | collective-permute-start | bytes 1572872 | tf_op jit(solution)/shard_map/ppermute | solution.py:359
  332.7 12.3 %collective-permute-start.19 = (bf16[1024,256]{1,0:T(8,128)(2,1)S(1)}, bf16[1024,256]{1,0:T(8,128)(2,1)S(1)}, u32[]{:S(2)}, u32[]{:S(2)}) collective-permute-start(bf16[1024,256]{1,0:T(8,128)(2,1)S(1)} %add_convert_fusion.21), channel_id=1, source_target_pairs={{3,1},{5,3},{7,5},{6,7},{4,6},{2,4},{0,2},{1,0},{11,9},{13,11},{15... | collective-permute-start | bytes 1572872 | tf_op jit(solution)/shard_map/ppermute | solution.py:359
  346.0 14.8 %collective-permute-start.20 = (bf16[1024,256]{1,0:T(8,128)(2,1)}, bf16[1024,256]{1,0:T(8,128)(2,1)}, u32[]{:S(2)}, u32[]{:S(2)}) collective-permute-start(bf16[1024,256]{1,0:T(8,128)(2,1)} %add_convert_fusion.20), channel_id=1, source_target_pairs={{3,1},{5,3},{7,5},{6,7},{4,6},{2,4},{0,2},{1,0},{11,9},{13,11},{15... | collective-permute-start | bytes 1572872 | tf_op jit(solution)/shard_map/ppermute | solution.py:359
  355.4 12.9 %collective-permute-start.17 = (bf16[1024,256]{1,0:T(8,128)(2,1)}, bf16[1024,256]{1,0:T(8,128)(2,1)}, u32[]{:S(2)}, u32[]{:S(2)}) collective-permute-start(bf16[1024,256]{1,0:T(8,128)(2,1)} %add_convert_fusion.22), channel_id=1, source_target_pairs={{1,3},{3,5},{5,7},{7,6},{6,4},{4,2},{2,0},{0,1},{9,11},{11,13},{13... | collective-permute-start | bytes 1572872 | tf_op jit(solution)/shard_map/ppermute | solution.py:356
  371.6 14.4 %collective-permute-start.22 = (bf16[1024,256]{1,0:T(8,128)(2,1)S(1)}, bf16[1024,256]{1,0:T(8,128)(2,1)}, u32[]{:S(2)}, u32[]{:S(2)}) collective-permute-start(bf16[1024,256]{1,0:T(8,128)(2,1)S(1)} %get-tuple-element.114), channel_id=1, source_target_pairs={{1,3},{3,5},{5,7},{7,6},{6,4},{4,2},{2,0},{0,1},{9,11},{11,13},{13... | collective-permute-start | bytes 1572872 | tf_op jit(solution)/shard_map/ppermute | solution.py:337
  374.1 14.2 %collective-permute-start.21 = (bf16[1024,256]{1,0:T(8,128)(2,1)S(1)}, bf16[1024,256]{1,0:T(8,128)(2,1)}, u32[]{:S(2)}, u32[]{:S(2)}) collective-permute-start(bf16[1024,256]{1,0:T(8,128)(2,1)S(1)} %get-tuple-element.114), channel_id=1, source_target_pairs={{3,1},{5,3},{7,5},{6,7},{4,6},{2,4},{0,2},{1,0},{11,9},{13,11},{15... | collective-permute-start | bytes 1572872 | tf_op jit(solution)/shard_map/ppermute | solution.py:339
  386.0 14.0 %collective-permute-start.24 = (bf16[1024,256]{1,0:T(8,128)(2,1)}, bf16[1024,256]{1,0:T(8,128)(2,1)}, u32[]{:S(2)}, u32[]{:S(2)}) collective-permute-start(bf16[1024,256]{1,0:T(8,128)(2,1)} %collective-permute-done.22), channel_id=1, source_target_pairs={{1,3},{3,5},{5,7},{7,6},{6,4},{4,2},{2,0},{0,1},{9,11},{11,13},{13... | collective-permute-start | bytes 1572872 | tf_op jit(solution)/shard_map/ppermute | solution.py:337
  388.2 14.1 %collective-permute-start.23 = (bf16[1024,256]{1,0:T(8,128)(2,1)}, bf16[1024,256]{1,0:T(8,128)(2,1)}, u32[]{:S(2)}, u32[]{:S(2)}) collective-permute-start(bf16[1024,256]{1,0:T(8,128)(2,1)} %collective-permute-done.21), channel_id=1, source_target_pairs={{3,1},{5,3},{7,5},{6,7},{4,6},{2,4},{0,2},{1,0},{11,9},{13,11},{15... | collective-permute-start | bytes 1572872 | tf_op jit(solution)/shard_map/ppermute | solution.py:339
  400.0 12.4 %collective-permute-start.26 = (bf16[1024,256]{1,0:T(8,128)(2,1)}, bf16[1024,256]{1,0:T(8,128)(2,1)S(1)}, u32[]{:S(2)}, u32[]{:S(2)}) collective-permute-start(bf16[1024,256]{1,0:T(8,128)(2,1)} %collective-permute-done.24), channel_id=1, source_target_pairs={{1,3},{3,5},{5,7},{7,6},{6,4},{4,2},{2,0},{0,1},{9,11},{11,13},{13... | collective-permute-start | bytes 1572872 | tf_op jit(solution)/shard_map/ppermute | solution.py:337
  402.3 14.0 %collective-permute-start.25 = (bf16[1024,256]{1,0:T(8,128)(2,1)}, bf16[1024,256]{1,0:T(8,128)(2,1)S(1)}, u32[]{:S(2)}, u32[]{:S(2)}) collective-permute-start(bf16[1024,256]{1,0:T(8,128)(2,1)} %collective-permute-done.23), channel_id=1, source_target_pairs={{3,1},{5,3},{7,5},{6,7},{4,6},{2,4},{0,2},{1,0},{11,9},{13,11},{15... | collective-permute-start | bytes 1572872 | tf_op jit(solution)/shard_map/ppermute | solution.py:339
  525.2 12.1 %collective-permute-start.36 = (bf16[128,2048]{1,0:T(8,128)(2,1)S(1)}, bf16[128,2048]{1,0:T(8,128)(2,1)S(1)}, u32[]{:S(2)}, u32[]{:S(2)}) collective-permute-start(bf16[128,2048]{1,0:T(8,128)(2,1)S(1)} %get-tuple-element.79), channel_id=1, source_target_pairs={{1,3},{3,5},{5,7},{7,6},{6,4},{4,2},{2,0},{0,1},{9,11},{11,13},{13... | collective-permute-start | bytes 1572872 | tf_op jit(solution)/shard_map/ppermute | solution.py:337
  527.4 12.9 %collective-permute-start.35 = (bf16[128,2048]{1,0:T(8,128)(2,1)S(1)}, bf16[128,2048]{1,0:T(8,128)(2,1)S(1)}, u32[]{:S(2)}, u32[]{:S(2)}) collective-permute-start(bf16[128,2048]{1,0:T(8,128)(2,1)S(1)} %get-tuple-element.79), channel_id=1, source_target_pairs={{3,1},{5,3},{7,5},{6,7},{4,6},{2,4},{0,2},{1,0},{11,9},{13,11},{15... | collective-permute-start | bytes 1572872 | tf_op jit(solution)/shard_map/ppermute | solution.py:339
  626.5 249.6 %all-reduce.8.cloned.1.call-start = ((), (), s32[]{:S(2)}) async-start(), calls=%async_computation.11 | async-start | bytes 16777216 | tf_op jit(solution)/shard_map/psum | solution.py:463
  643.0 353.8 %reduce-scatter.7.cloned.1.call-start = ((), (), s32[]{:S(2)}) async-start(), calls=%async_computation.10 | async-start | bytes 4325376
  780.5 24.4 %collective-permute-start.46 = (bf16[128,2048]{1,0:T(8,128)(2,1)S(1)}, bf16[128,2048]{1,0:T(8,128)(2,1)S(1)}, u32[]{:S(2)}, u32[]{:S(2)}) collective-permute-start(bf16[128,2048]{1,0:T(8,128)(2,1)S(1)} %get-tuple-element.98), channel_id=1, source_target_pairs={{3,1},{5,3},{7,5},{6,7},{4,6},{2,4},{0,2},{1,0},{11,9},{13,11},{15... | collective-permute-start | bytes 1572872 | tf_op jit(solution)/shard_map/ppermute | solution.py:359
  815.6 12.4 %collective-permute-start.45 = (bf16[128,2048]{1,0:T(8,128)(2,1)S(1)}, bf16[128,2048]{1,0:T(8,128)(2,1)S(1)}, u32[]{:S(2)}, u32[]{:S(2)}) collective-permute-start(bf16[128,2048]{1,0:T(8,128)(2,1)S(1)} %get-tuple-element.95), channel_id=1, source_target_pairs={{1,3},{3,5},{5,7},{7,6},{6,4},{4,2},{2,0},{0,1},{9,11},{11,13},{13... | collective-permute-start | bytes 1572872 | tf_op jit(solution)/shard_map/ppermute | solution.py:356
  841.9 27.3 %all-to-all-start.1 = ((bf16[8,128,256]{2,1,0:T(8,128)(2,1)}), bf16[8,128,256]{2,1,0:T(8,128)(2,1)S(1)}, u32[]{:S(2)}, u32[]{:S(2)}) async-start(bf16[8,128,256]{2,1,0:T(8,128)(2,1)} %bitcast.46), calls=%async_computation.1 | async-start | bytes 1048576 | tf_op jit(solution)/shard_map/all_to_all | solution.py:364
  869.2 131.2 %all-to-all-start.3 = ((bf16[5,512,256]{2,0,1:T(8,128)(2,1)}), bf16[5,512,256]{2,0,1:T(8,128)(2,1)S(1)}, u32[]{:S(2)}, u32[]{:S(2)}) async-start(bf16[5,512,256]{2,0,1:T(8,128)(2,1)} %copy.52), calls=%async_computation.4 | async-start | bytes 4194304 | tf_op jit(solution)/shard_map/all_to_all | solution.py:364
  (124 other events, 1616.4 us)
Sparse Core Ops, SparseCore 0:
  11.1 65.8 all-gather.4
  79.1 32.9 all-gather.6
  115.1 77.4 all-gather.8
  626.7 51.7 reduce-scatter.4
  681.4 153.5 all-reduce.7
  842.0 154.7 reduce-scatter.6

commit v2 on v1

--- a/solution.py
+++ b/solution.py
@@ -1,6 +1,7 @@
 import functools
 import jax
 import jax.numpy as jnp
+import numpy as np
 from jax import lax
 from jax.experimental import pallas as pl
 from jax.experimental.pallas import tpu as pltpu
@@ -14,6 +15,8 @@
 MIX_RANK = 32
 EPS_N = 1e-05
 EPS_G = 0.00064
+VMEM = 60 << 20
+PAD = 256
 FLOOR = -120.0
 
 
@@ -155,14 +158,13 @@
     )(r, k, v, rate, gp, vec, start)
 
 
-def bwd_body(groups, nb, r_ref, k_ref, v_ref, rate_ref, gp_ref, y_ref, gz_ref, vec_ref, st_ref,
-             gr_ref, gk_ref, gv_ref, gg_ref, gd_ref, sums_ref, adj):
-    first_step = pl.program_id(0) == 0
-
-    @pl.when(first_step)
+def bwd_body(groups, nb, r_ref, k_ref, v_ref, rate_ref, gp_ref, y_ref, gz_ref, vec_ref, st_ref, adj_in, sums_in, *rest):
+    gr_ref, gk_ref, gv_ref, gg_ref, gd_ref, adj, sums_ref = rest[-7:]
+
+    @pl.when(pl.program_id(0) == 0)
     def _():
-        adj[...] = jnp.zeros_like(adj)
-        sums_ref[...] = jnp.zeros_like(sums_ref)
+        adj[...] = adj_in[...]
+        sums_ref[...] = sums_in[...]
 
     ones = head_mask(HB)
     keep = head_mask(F)
@@ -278,24 +280,346 @@
         sums_ref[1:2, cols] += jnp.sum(grate, axis=0, keepdims=True)
 
 
-def wkv_backward(r, k, v, rate, gp, y, gz, vec, states, step_tokens=128):
+def wkv_backward(r, k, v, rate, gp, y, gz, vec, states, at, count, adj, sums, outs, step_tokens=128):
     tokens, width = r.shape
     groups = width // LANES
     nb = step_tokens // B
-    steps = tokens // step_tokens
-    row = pl.BlockSpec((step_tokens, width), lambda i: (steps - 1 - i, 0))
+    steps = count // step_tokens
     full = lambda shape: pl.BlockSpec(shape, lambda i: (0,) * len(shape))
     low = jax.ShapeDtypeStruct((tokens, width), HB)
-    return pl.pallas_call(
+    top = at // step_tokens + steps - 1
+    high = gz.shape[0] // step_tokens - 1 - (tokens - at - count) % gz.shape[0] // step_tokens
+    row = pl.BlockSpec((step_tokens, width), lambda i: (top - i, 0))
+    state = pl.BlockSpec((nb, groups, LANES, LANES), lambda i: (top - i, 0, 0, 0))
+    *outs, adj, sums = pl.pallas_call(
         functools.partial(bwd_body, groups, nb),
         grid=(steps,),
-        in_specs=[row] * 7 + [full(vec.shape), pl.BlockSpec((nb, groups, LANES, LANES), lambda i: (steps - 1 - i, 0, 0, 0))],
-        out_specs=[row] * 5 + [full((8, width))],
-        out_shape=[low] * 5 + [jax.ShapeDtypeStruct((8, width), F)],
-        scratch_shapes=[pltpu.VMEM((groups, LANES, LANES), F)],
-        cost_estimate=pl.CostEstimate(flops=tokens * width * 4096, transcendentals=tokens * width * 20, bytes_accessed=tokens * width * 60),
+        in_specs=[row] * 6 + [pl.BlockSpec((step_tokens, width), lambda i: (high - i, 0))]
+        + [full(vec.shape), state, full(adj.shape), full(sums.shape)] + [pl.BlockSpec(memory_space=pl.ANY)] * len(outs),
+        out_specs=[row] * 5 + [full(adj.shape), full(sums.shape)],
+        out_shape=[low] * 5 + [jax.ShapeDtypeStruct(adj.shape, F), jax.ShapeDtypeStruct(sums.shape, F)],
+        input_output_aliases={11 + i: i for i in range(len(outs))},
+        cost_estimate=pl.CostEstimate(flops=count * width * 4096, transcendentals=count * width * 20, bytes_accessed=count * width * 60),
         name="wkv_backward",
-    )(r, k, v, rate, gp, y, gz, vec, states)
+    )(r, k, v, rate, gp, y, gz, vec, states, adj, sums, *outs)
+    return outs, adj, sums
+
+
+def normalize(values):
+    center = values - jnp.mean(values, axis=-1, keepdims=True)
+    inverse = lax.rsqrt(jnp.mean(center * center, axis=-1, keepdims=True) + EPS_N)
+    return center * inverse, inverse
+
+
+def normalize_back(grad, normed, inverse, gain):
+    scaled = grad * gain
+    return inverse * (
+        scaled
+        - jnp.mean(scaled, axis=-1, keepdims=True)
+        - normed * jnp.mean(scaled * normed, axis=-1, keepdims=True)
+    )
+
+
+def shift_down(values, first_row):
+    row = lax.broadcasted_iota(jnp.int32, values.shape, 0)
+    return jnp.where(row == 0, first_row, pltpu.roll(values, 1, 0))
+
+
+def shift_up(values, last_row):
+    row = lax.broadcasted_iota(jnp.int32, values.shape, 0)
+    count = values.shape[0]
+    return jnp.where(row == count - 1, last_row, pltpu.roll(values, count - 1, 0))
+
+
+def whole(array):
+    return pl.BlockSpec(array.shape, lambda i: (0,) * array.ndim, pipeline_mode=pl.Buffered(1))
+
+
+def lane_groups(shape):
+    return lax.broadcasted_iota(jnp.int32, shape, 1) // MIX_RANK
+
+
+def weight_cols(refs, slot):
+    for ref in refs:
+        yield ref[:, slot].reshape(ref.shape[0] * ref.shape[2], ref.shape[3])
+
+
+def mix_forward_body(segs, x_ref, prm_ref, down_ref, up_ref, at_ref, *rest):
+    w_refs = rest[:segs]
+    r_ref, k_ref, v_ref, gp_ref, rate_ref, t_ref, xr_ref, xk_ref, xv_ref, xg_ref, last = rest[segs:]
+
+    @pl.when(pl.program_id(0) == 0)
+    def _():
+        last[...] = jnp.zeros_like(last)
+
+    prm = lambda i: prm_ref[i : i + 1, :]
+    width, cols = x_ref.shape[1], r_ref.shape[1]
+    normed, _ = normalize(x_ref[...].astype(F))
+    xn = normed * prm(0) + prm(1)
+    dx = shift_down(xn, last[0:1, :]) - xn
+    last[0:1, :] = xn[xn.shape[0] - 1 :, :]
+    t_mix = jnp.tanh(mm((xn + dx * prm(2)).astype(HB), down_ref[...]))
+    group = lane_groups(t_mix.shape)
+    low = t_mix.astype(HB)
+
+    def mixed(j):
+        own = jnp.where(group == j, low, jnp.zeros_like(low))
+        return (xn + dx * (prm(3 + j) + mm_nt(own, up_ref[...]))).astype(HB)
+
+    t_dec = jnp.tanh(mm(mixed(0), down_ref[...]))
+    t_ref[...] = jnp.where(group < 5, t_mix, t_dec)
+    dec = t_dec.astype(HB)
+    own_cols = pl.ds(pl.multiple_of(at_ref[0], cols), cols)
+    rate_ref[...] = prm_ref[8:9, own_cols] + mm_nt(jnp.where(group < 5, jnp.zeros_like(dec), dec), up_ref[own_cols, :])
+    part = width // segs
+    for j, slot, x_out, y_out in ((1, 1, xk_ref, k_ref), (2, 2, xv_ref, v_ref), (3, 0, xr_ref, r_ref), (4, 3, xg_ref, gp_ref)):
+        x_out[...] = mixed(j)
+        total = None
+        for i, w in enumerate(weight_cols(w_refs, slot)):
+            term = mm(x_out[:, pl.ds(pl.multiple_of(at_ref[1 + i], part), part)], w)
+            total = term if total is None else total + term
+        y_out[...] = total.astype(y_out.dtype)
+
+
+def rank_halves(width):
+    half = lambda h: pl.BlockSpec((width, PAD), lambda i, h=h: (0, h), pipeline_mode=pl.Buffered(1))
+    return [half(0), half(1)]
+
+
+SCALARS = pl.BlockSpec(memory_space=pltpu.SMEM)
+
+
+def mix_forward(x, prm, rank, at, mats, tile=256):
+    total, width = x.shape
+    cols = mats[0].shape[3]
+    row = lambda n: pl.BlockSpec((tile, n), lambda i: (i, 0))
+    shape = lambda n, dt: jax.ShapeDtypeStruct((total, n), dt)
+    return pl.pallas_call(
+        functools.partial(mix_forward_body, len(mats)),
+        grid=(total // tile,),
+        in_specs=[row(width), whole(prm)] + rank_halves(width) + [SCALARS] + [whole(a) for a in mats],
+        out_specs=[row(cols)] * 5 + [row(PAD)] + [row(width)] * 4,
+        out_shape=[shape(cols, HB)] * 3 + [shape(cols, F)] * 2 + [shape(PAD, F)] + [shape(width, HB)] * 4,
+        scratch_shapes=[pltpu.VMEM((8, width), F)],
+        compiler_params=pltpu.CompilerParams(vmem_limit_bytes=VMEM),
+        cost_estimate=pl.CostEstimate(flops=total * width * (8 * cols + 14 * 256), transcendentals=total * 512, bytes_accessed=total * width * 12),
+        name="mix_forward",
+    )(x, prm, rank, rank, at, *mats)
+
+
+def residual_forward_body(pieces, x_ref, w_ref, prm_ref, recept_ref, go_ref, at_ref, *rest):
+    z_refs = rest[: pieces + 1]
+    x1_ref, ck_ref, cr_ref, sg_ref, gkv_ref, last = rest[pieces + 1 :]
+
+    @pl.when(pl.program_id(0) == 0)
+    def _():
+        last[...] = jnp.zeros_like(last)
+
+    prm = lambda i: prm_ref[i : i + 1, :]
+    cols = recept_ref.shape[1]
+    x1 = x_ref[...].astype(F)
+    far = jnp.where(pl.program_id(0) < pl.num_programs(0) // 2, z_refs[pieces - 1][...], z_refs[pieces][...])
+    for i, z in enumerate([ref[...] for ref in z_refs[: pieces - 1]] + [far]):
+        x1 = x1 + mm(z, w_ref[pl.ds(pl.multiple_of(at_ref[i], cols), cols), :])
+    x1_ref[...] = x1
+    normed, _ = normalize(x1)
+    xs = (normed * prm(12) + prm(13)).astype(HB).astype(F)
+    dxs = shift_down(xs, last[0:1, :]) - xs
+    last[0:1, :] = xs[xs.shape[0] - 1 :, :]
+    ck_ref[...] = (xs + dxs * prm(14)).astype(HB)
+    cr = (xs + dxs * prm(15)).astype(HB)
+    cr_ref[...] = cr
+    sg = 1.0 / (1.0 + jnp.exp(-mm(cr, recept_ref[...])))
+    sg_ref[...] = sg
+    gkv_ref[...] = (go_ref[...].astype(F) * sg).astype(HB)
+
+
+def residual_forward(x, z, z_far, at, w_output, prm, recept, go_cols, tile=256):
+    total, width = x.shape
+    cols = recept.shape[1]
+    half = total // tile // 2
+    row = lambda n: pl.BlockSpec((tile, n), lambda i: (i, 0))
+    shape = lambda n, dt: jax.ShapeDtypeStruct((total, n), dt)
+    halves = [pl.BlockSpec((tile, cols), lambda i: (jnp.minimum(i, half - 1), 0)), pl.BlockSpec((tile, cols), lambda i: (jnp.maximum(i - half, 0), 0))]
+    return pl.pallas_call(
+        functools.partial(residual_forward_body, len(z) + 1),
+        grid=(total // tile,),
+        in_specs=[row(width), whole(w_output), whole(prm), whole(recept), row(cols), SCALARS] + [row(cols)] * len(z) + halves,
+        out_specs=[row(width)] * 3 + [row(cols)] * 2,
+        out_shape=[shape(width, F), shape(width, HB), shape(width, HB), shape(cols, F), shape(cols, HB)],
+        scratch_shapes=[pltpu.VMEM((8, width), F)],
+        compiler_params=pltpu.CompilerParams(vmem_limit_bytes=VMEM),
+        cost_estimate=pl.CostEstimate(flops=2 * total * width * (width + cols), transcendentals=total * cols, bytes_accessed=total * width * 12),
+        name="residual_forward",
+    )(x, w_output, prm, recept, go_cols, at, *z, *z_far)
+
+
+def residual_backward_body(closes, x1_ref, before_ref, go_ref, ghp_ref, gsp_ref, key_ref, recept_ref, w_ref, prm_ref,
+                           sums_in, ahead_in, *rest):
+    gx1_ref, gz_ref, sums_ref, ahead = rest[-4:]
+    at = pl.program_id(0)
+
+    @pl.when(at == 0)
+    def _():
+        ahead[...] = ahead_in[...]
+        sums_ref[...] = sums_in[...]
+
+    prm = lambda i: prm_ref[i : i + 1, :]
+    normed, inverse = normalize(x1_ref[...])
+    xs = (normed * prm(12) + prm(13)).astype(HB).astype(F)
+    other, _ = normalize(before_ref[...])
+    other = (other[7:8, :] * prm(12) + prm(13)).astype(HB).astype(F)
+    if closes:
+        other = jnp.where(at == pl.num_programs(0) - 1, 0.0, other)
+    dxs = shift_down(xs, other) - xs
+    gck = mm_nt(ghp_ref[...], key_ref[...])
+    gcr = mm_nt(gsp_ref[...], recept_ref[...])
+    moved = gck * prm(14) + gcr * prm(15)
+    gxs = gck + gcr - moved + shift_up(moved, ahead[0:1, :])
+    ahead[0:1, :] = moved[0:1, :]
+    total = lambda a: jnp.sum(a, axis=0, keepdims=True)
+    sums_ref[0:1, :] += total(gxs * normed)
+    sums_ref[1:2, :] += total(gxs)
+    sums_ref[2:3, :] += total(gck * dxs)
+    sums_ref[3:4, :] += total(gcr * dxs)
+    gx1 = (go_ref[...].astype(F) + normalize_back(gxs, normed, inverse, prm(12))).astype(HB)
+    gx1_ref[...] = gx1
+    gz_ref[...] = mm_nt(gx1, w_ref[...]).astype(HB)
+
+
+def residual_backward(x1, go_own, ghp, gsp, key, recept, w_output, prm, part, parts, sums, ahead, tile=256):
+    total, width = x1.shape
+    steps = total // tile // parts
+    top = total // tile - 1 - part * steps
+    row = lambda n: pl.BlockSpec((tile, n), lambda i: (top - i, 0))
+    to = lambda n: pl.BlockSpec((tile, n), lambda i: (steps - 1 - i, 0))
+    before = pl.BlockSpec((8, width), lambda i: (jnp.maximum((top - i) * (tile // 8) - 1, 0), 0))
+    low = jax.ShapeDtypeStruct((total // parts, width), HB)
+    few = jax.ShapeDtypeStruct((8, width), F)
+    const = pl.BlockSpec((8, width), lambda i: (0, 0))
+    flops = steps * tile * width * 2 * (width + ghp.shape[1] + gsp.shape[1])
+    return pl.pallas_call(
+        functools.partial(residual_backward_body, part == parts - 1),
+        grid=(steps,),
+        in_specs=[row(width), before, row(width), row(ghp.shape[1]), row(gsp.shape[1])] + [whole(a) for a in (key, recept, w_output, prm)] + [const, const],
+        out_specs=[to(width), to(width), const, const],
+        out_shape=[low, low, few, few],
+        compiler_params=pltpu.CompilerParams(vmem_limit_bytes=VMEM),
+        cost_estimate=pl.CostEstimate(flops=flops, transcendentals=total, bytes_accessed=steps * tile * width * 12),
+        name="residual_backward",
+    )(x1, x1, go_own, ghp, gsp, key, recept, w_output, prm, sums, ahead)
+
+
+def mix_backward_body(opens, closes, segs, x_ref, before_ref, gr_ref, gk_ref, gv_ref, gg_ref, grb_ref, t_ref, gx1_ref,
+                      prm_ref, two_ref, heads_ref, down_ref, up_ref, at_ref, *rest):
+    w_refs, rest = rest[:segs], rest[segs:]
+    given = rest[: 0 if opens else 3]
+    out_ref, ahead, packed, *more = rest[len(given) :]
+    gmix, mstack, gx_ref = more[-3:]
+    at = pl.program_id(0)
+    width, cols = x_ref.shape[1], gr_ref.shape[1]
+    part = width // segs
+    tile = x_ref.shape[0]
+
+    @pl.when(at == 0)
+    def _():
+        if opens:
+            ahead[...] = jnp.zeros_like(ahead)
+            packed[...] = jnp.zeros_like(packed)
+        else:
+            ahead[...] = given[1][...]
+            packed[...] = given[2][...]
+
+    own_cols = pl.ds(pl.multiple_of(at_ref[0], cols), cols)
+    prm = lambda i: prm_ref[i : i + 1, :]
+    normed, inverse = normalize(x_ref[...].astype(F))
+    xn = normed * prm(0) + prm(1)
+    other, _ = normalize(before_ref[...].astype(F))
+    other = other[15:16, :] * prm(0) + prm(1)
+    if closes:
+        first_tile = at == pl.num_programs(0) - 1
+        other = jnp.where(first_tile, 0.0, other)
+    dx = shift_down(xn, other) - xn
+    t = t_ref[...]
+    slope = 1.0 - t * t
+    low = t.astype(HB)
+    group = lane_groups(t.shape)
+    lane = lax.broadcasted_iota(jnp.int32, t.shape, 1)
+    zero = jnp.zeros_like(low)
+    dec = jnp.where((group < 5) | (group == 7), zero, low)
+    ge = jnp.where(group < 5, 0.0, mm(grb_ref[...], up_ref[own_cols, :]) * slope).astype(HB)
+    packed[PAD : 2 * PAD, own_cols] += mm_tn(dec, grb_ref[...])
+    gdx = gsum = gm = None
+    for j, (slot, g_ref) in enumerate(((None, None), (1, gk_ref), (2, gv_ref), (0, gr_ref), (3, gg_ref))):
+        own = jnp.where(group == j, low, zero)
+        mstack[j * tile : (j + 1) * tile, :] = jnp.where(lane == 7 * MIX_RANK + j, jnp.ones_like(own), own)
+        lerp = prm(3 + j) + mm_nt(own, up_ref[...])
+        if j == 0:
+            gx = mm_nt(ge, down_ref[...])
+            x_w = (xn + dx * lerp).astype(HB)
+        else:
+            for i, w in enumerate(weight_cols(w_refs, slot)):
+                gx_ref[:, pl.ds(pl.multiple_of(at_ref[1 + i], part), part)] = mm_nt(g_ref[...], w)
+            gx = gx_ref[...]
+        moved = gx * lerp
+        gdx = moved if gdx is None else gdx + moved
+        gsum = gx if gsum is None else gsum + gx
+        bits = (gx * dx).astype(HB)
+        gmix[j * tile : (j + 1) * tile, :] = bits
+        part_m = jnp.where(group == j, mm(bits, up_ref[...]), 0.0)
+        gm = part_m if gm is None else gm + part_m
+    gm = (gm * slope).astype(HB)
+    gxm = mm_nt(gm, down_ref[...])
+    gdx = gdx + gxm * prm(2)
+    gxn = gsum + gxm - gdx + shift_up(gdx, ahead[0:1, :])
+    ahead[0:1, :] = gdx[0:1, :]
+    total = lambda a: jnp.sum(a, axis=0, keepdims=True)
+    xm = (xn + dx * prm(2)).astype(HB)
+    packed[:PAD, :] += mm_tn(jnp.concatenate([gm, ge], axis=0), jnp.concatenate([xm, x_w], axis=0))
+    packed[PAD : 2 * PAD, :] += mm_tn(mstack[...], gmix[...])
+    spare = 7 * MIX_RANK
+    packed[spare : spare + 1, :] += total(gxn * normed)
+    packed[spare + 1 : spare + 2, :] += total(gxn)
+    packed[spare + 2 : spare + 3, :] += total(gxm * dx)
+    out_ref[...] = (gx1_ref[...].astype(F) + normalize_back(gxn, normed, inverse, prm(0))).astype(HB)
+    if closes:
+        @pl.when(first_tile)
+        def _():
+            packed[spare + 8 : spare + 16, :] += two_ref[...]
+            packed[spare + 16 : spare + 24, own_cols] += heads_ref[...]
+            block = more[0].shape[2]
+            for i in range(more[0].shape[0]):
+                more[0][i] = packed[:, i * block : (i + 1) * block].astype(HB)
+
+
+def mix_backward(x, grads, t, gx1_parts, mats, rank, prm, two, heads, at, first_tile, steps, given, tile=256):
+    total, width = x.shape
+    segs = len(mats)
+    cols = mats[0].shape[3]
+    lines = 2 * PAD
+    shape = jax.ShapeDtypeStruct
+    fixed = lambda *s: pl.BlockSpec(s, lambda i: (0,) * len(s))
+    top = first_tile
+    row = lambda n: pl.BlockSpec((tile, n), lambda i: (top - i, 0))
+    per = total // tile // len(gx1_parts)
+    first = top // per * per
+    gx1 = gx1_parts[len(gx1_parts) - 1 - top // per]
+    before = pl.BlockSpec((16, width), lambda i: (jnp.maximum((top - i) * (tile // 16) - 1, 0), 0))
+    closes = top - steps < 0
+    return pl.pallas_call(
+        functools.partial(mix_backward_body, not given, closes, segs),
+        grid=(steps,),
+        in_specs=[row(width), before] + [row(cols)] * 5 + [row(PAD), pl.BlockSpec((tile, width), lambda i: (top - first - i, 0))]
+        + [whole(a) for a in (prm, two, heads)] + rank_halves(width) + [SCALARS] + [whole(a) for a in mats]
+        + ([pl.BlockSpec(memory_space=pl.ANY), whole(given[1]), whole(given[2])] if given else []),
+        out_specs=[row(width), fixed(8, width), fixed(lines, width)] + [fixed(segs, lines, width // segs)] * closes,
+        out_shape=[shape((total, width), HB), shape((8, width), F), shape((lines, width), F)] + [shape((segs, lines, width // segs), HB)] * closes,
+        input_output_aliases={15 + segs: 0} if given else {},
+        scratch_shapes=[pltpu.VMEM((5 * tile, width), HB), pltpu.VMEM((5 * tile, PAD), HB), pltpu.VMEM((tile, width), F)],
+        compiler_params=pltpu.CompilerParams(vmem_limit_bytes=VMEM),
+        cost_estimate=pl.CostEstimate(flops=steps * tile * width * (8 * cols + 26 * 256), transcendentals=total, bytes_accessed=steps * tile * width * 10),
+        name="mix_backward",
+    )(x, x, *grads, t, gx1, prm, two, heads, rank, rank, at, *mats, *given)
 
 
 def ring_of(count):
@@ -310,221 +634,364 @@
     return path + [z * wide for z in reversed(range(deep))]
 
 
-def ring_tables():
-    count = lax.axis_size("seq")
-    path = ring_of(count)
-    place = [path.index(i) for i in range(count)]
-    here = jnp.array(place, jnp.int32)[lax.axis_index("seq")]
-    right = [(path[i], path[(i + 1) % count]) for i in range(count)]
-    left = [(b, a) for a, b in right]
-    return count, jnp.array(path, jnp.int32), here, right, left
-
-
-def gather_seq(part, dim):
-    count, path, here, right, left = ring_tables()
+class Ring:
+    def __init__(self, scale=1):
+        self.count = lax.axis_size("seq")
+        self.path = ring_of(self.count)
+        place = [self.path.index(i) for i in range(self.count)]
+        table = [[self.path[(place[i] + away) % self.count] for away in range(self.count)] for i in range(self.count)]
+        self.scale = np.uint32(scale)
+        here = lax.axis_index("seq").astype(jnp.uint32)
+        self.row = lax.dynamic_slice(np.array(table, np.uint32), (here, np.uint32(0)), (1, self.count))
+        self.right = [(self.path[i], self.path[(i + 1) % self.count]) for i in range(self.count)]
+        self.left = [(b, a) for a, b in self.right]
+
+    def owner(self, away):
+        away %= self.count
+        index = lax.reshape(lax.slice(self.row, (0, away), (1, away + 1)), ())
+        return index * self.scale if self.scale > 1 else index
+
+
+def starts(ndim, at):
+    return [at.get(d, np.uint32(0)) for d in range(ndim)]
+
+
+def cut(array, start, size, dim):
+    sizes = list(array.shape)
+    sizes[dim] = size
+    return lax.dynamic_slice(array, starts(array.ndim, {dim: start}), sizes)
+
+
+def put(array, piece, at):
+    return lax.dynamic_update_slice(array, piece, starts(array.ndim, at))
+
+
+def ring_hops(part, other=None):
+    ring = Ring()
+    half = part.shape[0] // 2
+    held = [(0, part)]
+    going_right = going_left = part
+    for step in range(1, ring.count // 2):
+        going_right = lax.ppermute(going_right, "seq", ring.right)
+        going_left = lax.ppermute(going_left, "seq", ring.left)
+        if step == 1 and other is not None:
+            going_right, going_left = after((going_right, going_left), other)
+        held += [(-step, going_right), (step, going_left)]
+    far = lax.ppermute(going_right[:half], "seq", ring.right), lax.ppermute(going_left[half:], "seq", ring.left)
+    return held, far
+
+
+def assembled(held, far, dim):
+    part = held[0][1]
     size = part.shape[dim]
+    ring = Ring(size)
     shape = list(part.shape)
-    shape[dim] = size * count
+    shape[dim] = size * ring.count
     out = jnp.zeros(shape, part.dtype)
-
-    def put(out, piece, away):
-        owner = path[(here + away) % count]
-        return lax.dynamic_update_slice_in_dim(out, piece, owner * size, dim)
-
-    out = put(out, part, 0)
-    going_right = going_left = part
-    for step in range(1, count // 2 + 1):
-        going_right = lax.ppermute(going_right, "seq", right)
-        if step < count - count // 2:
-            going_left = lax.ppermute(going_left, "seq", left)
-            out = put(out, going_left, step)
-        out = put(out, going_right, -step)
+    for away, piece in held:
+        out = put(out, piece, {dim: ring.owner(away)})
+    half = part.shape[0] // 2
+    start = ring.owner(ring.count // 2)
+    out = put(out, far[0], {dim: start})
+    low = {dim: start + np.uint32(half)} if dim == 0 else {dim: start, 0: np.uint32(half)}
+    return put(out, far[1], low)
+
+
+def gather_seq(part, dim, other=None):
+    return assembled(*ring_hops(part, other), dim)
+
+
+def after(value, other):
+    return lax.optimization_barrier((value, other))[0]
+
+
+class Scatter:
+    def __init__(self, piece_of, scale):
+        self.ring = Ring(scale)
+        self.right, self.left = self.ring.right, self.ring.left
+        self.piece_of = piece_of
+        self.hops = self.step = self.ring.count // 2
+        self.going = None
+
+    def term(self, away):
+        return self.piece_of(self.ring.owner(away))
+
+    def hop(self, other=None):
+        if self.going is None:
+            last = self.term(self.hops)
+            half = last.shape[0] // 2
+            more, less = last[:half], last[half:]
+        else:
+            from_left, from_right = self.going if other is None else after(self.going, other)
+            more, less = self.term(self.step), self.term(-self.step)
+            if self.step == self.hops - 1:
+                half = from_left.shape[0]
+                more = jnp.concatenate([more[:half] + from_left.astype(F), more[half:]], axis=0)
+                less = jnp.concatenate([less[:half], less[half:] + from_right.astype(F)], axis=0)
+            else:
+                more = more + from_left.astype(F)
+                less = less + from_right.astype(F)
+        sent = more.astype(HB), less.astype(HB)
+        self.going = lax.ppermute(sent[0], "seq", self.right), lax.ppermute(sent[1], "seq", self.left)
+        self.step -= 1
+        return sent
+
+    def finish(self, other=None):
+        while self.step > 0:
+            self.hop()
+        from_left, from_right = self.going if other is None else after(self.going, other)
+        return self.term(0) + from_left.astype(F) + from_right.astype(F)
+
+
+def scatter_seq(piece_of, scale):
+    return Scatter(piece_of, scale).finish()
+
+
+def gather_seg(part):
+    count = lax.axis_size("seg")
+    held = {0: part}
+    step = count // 2
+    while step:
+        pairs = [(i, i ^ step) for i in range(count)]
+        held.update({i ^ step: lax.ppermute(value, "seg", pairs) for i, value in list(held.items())})
+        step //= 2
+    return [held[i] for i in range(count)]
+
+
+def seg_bit(step):
+    return (lax.axis_index("seg").astype(jnp.uint32) & np.uint32(step)) // np.uint32(step) if step > 1 else lax.axis_index("seg").astype(jnp.uint32) & np.uint32(1)
+
+
+def seg_round(parts, step):
+    count = lax.axis_size("seg")
+    bit = seg_bit(step)
+    shaped = parts.reshape((parts.shape[0] // 2, 2) + parts.shape[1:])
+    keep = lax.squeeze(cut(shaped, bit, 1, 1), (1,))
+    give = lax.squeeze(cut(shaped, np.uint32(1) - bit, 1, 1), (1,))
+    return keep, lax.ppermute(give, "seg", [(i, i ^ step) for i in range(count)])
+
+
+def scatter_seg(parts):
+    step = 1
+    while step < lax.axis_size("seg"):
+        keep, come = seg_round(parts, step)
+        parts = (keep.astype(F) + come.astype(F)).astype(HB)
+        step *= 2
+    return parts[0]
+
+
+class Pump:
+    def __init__(self, values):
+        count = lax.axis_size("seg")
+        self.values, self.done, self.coming = list(values), [], None
+        self.rounds = [[(i, i ^ (2 << n)) for i in range(count)] for n in range((count // 2).bit_length() - 1)]
+
+    def send(self):
+        self.coming = lax.ppermute(self.values[len(self.done)], "seg", self.rounds[0])
+
+    def turn(self, other):
+        at = len(self.done)
+        if self.coming is None and at < len(self.values):
+            self.values[at] = after(self.values[at], other)
+            self.send()
+            return self.values[at]
+        if at < len(self.values):
+            value = self.values[at]
+            value = (value.astype(F) + after(self.coming, other).astype(F)).astype(HB)
+            for pairs in self.rounds[1:]:
+                value = (value.astype(F) + lax.ppermute(value, "seg", pairs).astype(F)).astype(HB)
+            self.done.append(value)
+            if at + 1 < len(self.values):
+                self.send()
+            return value
+        return other
+
+
+def direct_exchange(array, cols):
+    ring = Ring(cols)
+    count, order = ring.count, ring.path
+    entry = lambda away: cut(array, ring.owner(away), cols, array.ndim - 1)[None]
+    senders = Ring()
+    out = put(jnp.zeros((count,) + entry(0).shape[1:], array.dtype), entry(0), {0: senders.owner(0)})
+    for away in sorted(range(1, count), key=lambda d: -min(d, count - d)):
+        pairs = [(order[i], order[(i + away) % count]) for i in range(count)]
+        out = put(out, lax.ppermute(entry(away), "seq", pairs), {0: senders.owner(-away)})
     return out
-
-
-def scatter_seq(piece_of):
-    count, path, here, right, left = ring_tables()
-    far = count // 2
-    near = count - 1 - far
-
-    def term(away):
-        return piece_of(path[(here + away) % count])
-
-    going_right = going_left = None
-    for step in range(far, 0, -1):
-        going_right = term(step) if going_right is None else term(step) + going_right.astype(F)
-        going_right = lax.ppermute(going_right.astype(HB), "seq", right)
-        if step <= near:
-            going_left = term(-step) if going_left is None else term(-step) + going_left.astype(F)
-            going_left = lax.ppermute(going_left.astype(HB), "seq", left)
-    return term(0) + going_right.astype(F) + going_left.astype(F)
 
 
 def exchange_seq(value, split, join):
     return lax.all_to_all(value, "seq", split_axis=split, concat_axis=join, tiled=True)
-
-
-def previous(rows):
-    return jnp.concatenate([jnp.zeros_like(rows[:1]), rows[:-1]], axis=0)
-
-
-def following(rows):
-    return jnp.concatenate([rows[1:], jnp.zeros_like(rows[:1])], axis=0)
-
-
-def normalize(values):
-    center = values - jnp.mean(values, axis=-1, keepdims=True)
-    inverse = lax.rsqrt(jnp.mean(center * center, axis=-1, keepdims=True) + EPS_N)
-    return center * inverse, inverse
-
-
-def normalize_back(grad, normed, inverse, gain):
-    scaled = grad * gain
-    return inverse * (
-        scaled
-        - jnp.mean(scaled, axis=-1, keepdims=True)
-        - normed * jnp.mean(scaled * normed, axis=-1, keepdims=True)
-    )
 
 
 def shards(tokens, tm_mats, low_rank, params, opening, cm_key, cm_value, cm_recept, out_grad):
     rows, width = tokens.shape
     count = lax.axis_size("seq")
-    here = lax.axis_index("seq")
+    segs = lax.axis_size("seg")
+    here = lax.axis_index("seq").astype(jnp.uint32)
     total = rows * count
     cols = width // count
-    mix_width = 5 * MIX_RANK
-    g1, b1, mu_x = params[0], params[1], params[2]
-    g2, b2, cmu_k, cmu_r = params[12], params[13], params[14], params[15]
+    ranks = low_rank.shape[2]
+    first_row, first_col = here * np.uint32(rows), here * np.uint32(cols)
 
     def my_cols(array):
-        return lax.dynamic_slice_in_dim(array, here * cols, cols, array.ndim - 1)
+        return cut(array, first_col, cols, array.ndim - 1)
 
     def my_rows(array):
-        return lax.dynamic_slice_in_dim(array, here * rows, rows, 0)
-
-    x = gather_seq(tokens, 0).astype(F)
-    rank = lax.all_gather(low_rank, ("seg", "seq"), axis=1, tiled=True)
-    mats = lax.all_gather(exchange_seq(tm_mats[:4], 2, 1), "seg", axis=1, tiled=True)
-    w_output = lax.all_gather(tm_mats[4], ("seg", "seq"), axis=0, tiled=True)
-    go_cols = exchange_seq(out_grad, 1, 0).astype(F)
-    down_mix, down_decay = rank[0][:, :mix_width], rank[0][:, mix_width:]
-    up_mix = rank[1][:, :mix_width]
-    up_decay = lax.dynamic_slice_in_dim(rank[1], here * cols, cols, 0)[:, mix_width:]
-
-    xhat, x_inv = normalize(x)
-    xn = xhat * g1 + b1
-    dx = previous(xn) - xn
-    xm = (xn + dx * mu_x).astype(HB)
-    m_f = jnp.tanh(mm(xm, down_mix))
-    m = m_f.astype(HB)
-
-    def group(array, j):
-        return array[:, j * MIX_RANK : (j + 1) * MIX_RANK]
-
-    lerp = [params[3 + j] + mm_nt(group(m, j), group(up_mix, j)) for j in range(5)]
-    x_w, x_k, x_v, x_r, x_g = ((xn + dx * f).astype(HB) for f in lerp)
-    e_f = jnp.tanh(mm(x_w, down_decay))
-    e = e_f.astype(HB)
-    rate = my_cols(params[8]) + mm_nt(e, up_decay)
-    r = mm(x_r, mats[0]).astype(HB)
-    k = mm(x_k, mats[1]).astype(HB)
-    v = mm(x_v, mats[2]).astype(HB)
-    gp = mm(x_g, mats[3])
+        return cut(array, first_row, rows, 0)
+
+    low = jnp.pad(low_rank, ((0, 0), (0, 0), (0, PAD - ranks))).transpose(1, 0, 2).reshape(-1, 2 * PAD)
+    rank = lax.all_gather(low, ("seg", "seq"), axis=0, tiled=True)
+    mine = direct_exchange(tm_mats[:4], cols)
+    mats = gather_seg(mine)
+    x = gather_seq(tokens, 0, mine)
+    w_output = lax.all_gather(after(tm_mats[4], x), ("seg", "seq"), axis=0, tiled=True)
+    go_cols = exchange_seq(after(out_grad, x), 1, 0)
+    part = width // segs
+    seg_starts = [(lax.axis_index("seg") ^ i) * part for i in range(segs)]
+    at = jnp.stack([first_col.astype(jnp.int32)] + seg_starts)
+
+    r, k, v, gp, rate, t, x_r, x_k, x_v, x_g = mix_forward(x, params, rank, at, mats)
     vec = my_cols(jnp.concatenate([params[9:12], jnp.zeros((5, width), F)], axis=0))
     groups = cols // LANES
-    heads = lax.dynamic_slice_in_dim(opening[0], here * (cols // G), cols // G, 0)
+    heads = cut(opening[0], here * np.uint32(cols // G), cols // G, 0)
     start = jnp.einsum(
         "ghkv,hi->ghvik", heads.reshape(groups, LANES // G, G, G), jnp.eye(LANES // G, dtype=F),
         precision=lax.Precision.HIGHEST,
     ).reshape(groups, LANES, LANES)
+    r, go_cols = lax.optimization_barrier((r, go_cols))
     z_cols, y, states = wkv_forward(r, k, v, rate, gp, vec, start)
-    z = gather_seq(z_cols, 1)
-    x1 = x + mm(z, w_output)
-
-    x1hat, x1_inv = normalize(x1)
-    xs = (x1hat * g2 + b2).astype(HB).astype(F)
-    dxs = previous(xs) - xs
-    ck = (xs + dxs * cmu_k).astype(HB)
-    cr = (xs + dxs * cmu_r).astype(HB)
-    sg = jax.nn.sigmoid(mm(cr, cm_recept))
-    gkv = gather_seq((go_cols * sg).astype(HB), 1)
+    z_held, z_far = ring_hops(z_cols)
+    ring_cols = Ring(cols)
+    z_at = jnp.stack([ring_cols.owner(away).astype(jnp.int32) for away in [a for a, _ in z_held] + [count // 2]])
+
+    x1, ck, cr, sg, gkv_cols = residual_forward(
+        x, [piece for _, piece in z_held], z_far, z_at, w_output, params, cm_recept, go_cols
+    )
+    gkv = gather_seq(gkv_cols, 1)
     hp = mm(ck, cm_key)
     hid = jnp.square(jax.nn.relu(hp)).astype(HB)
-    kv = scatter_seq(lambda owner: mm(hid, lax.dynamic_slice_in_dim(cm_value, owner * cols, cols, 1)))
+    late = after(hid, gkv)
+    kv = scatter_seq(lambda start: mm(late, cut(cm_value, start, cols, 1)), cols)
     cm_rows = exchange_seq((sg * kv).astype(HB), 0, 1)
     block_out = (my_rows(x1) + cm_rows.astype(F)).astype(HB)
-    gsp = (go_cols * kv * sg * (1.0 - sg)).astype(HB)
+    gsp = (go_cols.astype(F) * kv * sg * (1.0 - sg)).astype(HB)
     ghp = (mm_nt(gkv, cm_value) * (2.0 * jax.nn.relu(hp))).astype(HB)
-    cm_value_grad = mm_tn(hid, gkv)
-    cm_key_grad = mm_tn(ck, ghp)
-    cm_recept_grad = mm_tn(cr, gsp)
+    bit = seg_bit(1)
+    near = [(i, i ^ 1) for i in range(segs)]
+
+    def cm_half(which, ordered):
+        part = lambda a: cut(a, which * np.uint32(a.shape[1] // 2), a.shape[1] // 2, 1)
+        pairs = ((ck, ghp), (hid, gkv), (cr, gsp))
+        return tuple(mm_tn(part(a), b).astype(HB) for a, b in pairs[ordered:])
+
+    cm_come = tuple(lax.ppermute(value, "seg", near) for value in cm_half(np.uint32(1) - bit, 0))
+    cm_kept = cm_half(bit, 0)
+    gsp, ghp, cm_kept = lax.optimization_barrier((gsp, ghp, cm_kept))
+    go_own = put(jnp.zeros((total, width), HB), out_grad, {0: first_row})
+
+    def piece_cols(array):
+        return lambda start: cut(array, start, cols, 1).astype(F)
+
+    back = lambda part, *carried: residual_backward(
+        x1, go_own, ghp, gsp, cm_key, cm_recept, w_output, params, part, 2, *carried
+    )
+    start_row = jnp.zeros((8, width), F)
+    gx1_late, gz_late, sums_two, ahead = back(0, start_row, start_row)
+    cm_kept = [(a.astype(F) + b.astype(F)).astype(HB) for a, b in zip(cm_kept, after(cm_come, ahead))]
+    pump = Pump([a[i * (a.shape[0] // 2) : (i + 1) * (a.shape[0] // 2)] for a in cm_kept[:2] for i in range(2)] + cm_kept[2:])
+    sent = pump.turn(ahead)
+    late = Scatter(piece_cols(gz_late), cols)
+    sent = (late.hop(), sent)
+    gx1_early, gz_early, sums_two, ahead = back(1, sums_two, after(ahead, sent))
+    token = pump.turn(gz_early)
+    while late.step > 0:
+        sent = late.hop((gz_early, sent))
+    early = Scatter(piece_cols(gz_early), cols)
+    gz_late = late.finish((sent, token))
+
+    adj = jnp.zeros((groups, LANES, LANES), F)
+    sums = jnp.zeros((8, cols), F)
+    outs = ()
+    half = total // 2
+    runs = 2
+    run = half // runs
+    wkv = lambda gz, at, adj, sums, outs: wkv_backward(r, k, v, rate, gp, y, gz, vec, states, at, run, adj, sums, outs)
+    sent = early.hop(None)
+    for i in range(runs):
+        outs, adj, sums = wkv(gz_late, total - (i + 1) * run, after(adj, sent), sums, outs)
+        sent = pump.turn(sums)
+        while early.step > early.hops * (runs - 1 - i) // runs:
+            sent = (early.hop(sums), sent)
+    gz_early = early.finish((sums, sent))
+    go1 = Scatter(piece_cols(jnp.concatenate([gx1_early, gx1_late], axis=0)), cols)
+    first_pieces = go1.piece_of
+    go1.piece_of = lambda owner: after(first_pieces(owner), gz_early)
+    sent = go1.hop()
+    for i in range(runs):
+        outs, adj, sums = wkv(gz_early, half - (i + 1) * run, after(adj, sent), sums, outs)
+        sent = (go1.hop(sums), pump.turn(sums))
+    gr, gk, gv, ggp, grb = outs
+    d_four = jnp.stack([mm_tn(a, b).astype(HB) for a, b in ((x_r, gr), (x_k, gk), (x_v, gv), (x_g, ggp))], axis=1)
+    keep, come = seg_round(d_four.reshape(segs, -1, 4, cols), 1)
+    tiles = total // 256
+    splits = (tiles // 4, tiles // 4, tiles // 2)
+
+    def mix(run, grad, given):
+        return mix_backward(
+            x, (grad, gk, gv, ggp, grb), t, (gx1_late, gx1_early), mats, rank, params, sums_two, sums,
+            at, tiles - 1 - sum(splits[:run]), splits[run], given,
+        )
+
+    def seg_rest(keep, come, step):
+        parts = (keep.astype(F) + come.astype(F)).astype(HB)
+        while step * 2 < segs:
+            step *= 2
+            keep, come = seg_round(parts, step)
+            parts = (keep.astype(F) + come.astype(F)).astype(HB)
+        return parts[0]
+
+    d_four = (keep.astype(F) + come.astype(F)).astype(HB)
+    keep, come = seg_round(d_four, 2)
+    gr, _ = lax.optimization_barrier((gr, (sent, keep)))
+    out, ahead, packed = mix(0, gr, ())
+    while go1.step > 0:
+        sent = go1.hop(ahead)
+    sent = (sent, pump.turn(ahead))
+    d_four = seg_rest(keep, after(come, sent), 2)
+    d_four = exchange_seq(d_four.reshape(count, -1, 4, cols).transpose(0, 2, 1, 3).reshape(count, -1, cols), 0, 0)
+    out, ahead, packed = mix(1, gr, (out, after(ahead, (sent, keep)), packed))
+    while len(pump.done) < len(pump.values):
+        token = pump.turn(ahead)
+    cm_sums = [jnp.concatenate(pump.done[i : i + 2], axis=0) for i in (0, 2)] + pump.done[4:]
+    cm_come = [lax.ppermute(value, "seg", near) for value in cm_sums]
+    go1_cols = go1.finish(ahead).astype(HB)
+    z = assembled(z_held, z_far, 1)
+    d_out = mm_tn(z, go1_cols).astype(HB).reshape(segs, -1, cols)
+    keep, come = seg_round(d_out, 1)
+    d_out = (keep.astype(F) + come.astype(F)).astype(HB)
+    keep, come = seg_round(d_out, 2)
+    ahead, d_four, cm_sums = after((ahead, d_four, cm_sums), keep)
+    out, _, _, packed = mix(2, gr, (out, ahead, packed))
+    d_out = exchange_seq(seg_rest(keep, after(come, packed), 2).reshape(count, -1, cols), 0, 0)
+
+    def joined(blocks, mats_in):
+        return blocks.reshape(count, mats_in, -1, cols).transpose(1, 2, 0, 3).reshape(mats_in, -1, width).astype(F)
+
+    d_mats = jnp.concatenate([joined(d_four, 4), joined(d_out, 1)], axis=0)
     cm_grads = tuple(
-        lax.psum(value.astype(HB), "seg").astype(F) for value in (cm_key_grad, cm_value_grad, cm_recept_grad)
+        jnp.where(bit == 0, jnp.concatenate([a, b], axis=0), jnp.concatenate([b, a], axis=0)).astype(F)
+        for a, b in zip(cm_sums, after(cm_come, packed))
     )
-    gck = mm_nt(ghp, cm_key)
-    gcr = mm_nt(gsp, cm_recept)
-    d_cmu_k = jnp.sum(gck * dxs, axis=0)
-    d_cmu_r = jnp.sum(gcr * dxs, axis=0)
-    gxs_part = gck * (1.0 - cmu_k) + gcr * (1.0 - cmu_r) + following(gck * cmu_k + gcr * cmu_r)
-    gxs = scatter_seq(lambda owner: lax.dynamic_slice_in_dim(gxs_part, owner * rows, rows, 0))
-    own_hat, own_inv = my_rows(x1hat), my_rows(x1_inv)
-    gx1 = out_grad.astype(F) + normalize_back(gxs, own_hat, own_inv, g2)
-    d_g2 = jnp.sum(gxs * own_hat, axis=0)
-    d_b2 = jnp.sum(gxs, axis=0)
-
-    go1 = gather_seq(gx1.astype(HB), 0)
-    gz = mm_nt(go1, lax.dynamic_slice_in_dim(w_output, here * cols, cols, 0))
-    gr, gk, gv, ggp, grb, sums = wkv_backward(r, k, v, rate, gp, y, gz, vec, states)
-    d_mats = jnp.stack(
-        [mm_tn(a, b).astype(HB) for a, b in ((x_r, gr), (x_k, gk), (x_v, gv), (x_g, ggp), (z, my_cols(go1)))]
-    )
-    d_mats = lax.psum_scatter(d_mats, "seg", scatter_dimension=1, tiled=True)
-    d_mats = exchange_seq(d_mats, 1, 2).astype(F)
-    d_up_decay = mm_tn(grb, e)
-    ge = (mm(grb, up_decay) * (1.0 - e_f * e_f)).astype(HB)
-    d_down_decay = mm_tn(x_w, ge)
-    gx = [
-        mm_nt(ge, down_decay),
-        mm_nt(gk, mats[1]),
-        mm_nt(gv, mats[2]),
-        mm_nt(gr, mats[0]),
-        mm_nt(ggp, mats[3]),
-    ]
-    gdx = gx[0] * lerp[0] + gx[1] * lerp[1] + gx[2] * lerp[2] + gx[3] * lerp[3] + gx[4] * lerp[4]
-    gmix = [a * dx for a in gx]
-    d_mu = [jnp.sum(a, axis=0) for a in gmix]
-    gmix = [a.astype(HB) for a in gmix]
-    d_up_mix = jnp.concatenate([mm_tn(a, group(m, j)) for j, a in enumerate(gmix)], axis=1)
-    gm = jnp.concatenate([mm(a, group(up_mix, j)) for j, a in enumerate(gmix)], axis=1)
-    gm = (gm * (1.0 - m_f * m_f)).astype(HB)
-    d_down_mix = mm_tn(xm, gm)
-    gxm = mm_nt(gm, down_mix)
-    d_mu_x = jnp.sum(gxm * dx, axis=0)
-    gdx = gdx + gxm * mu_x
-    gxn_part = gx[0] + gx[1] + gx[2] + gx[3] + gx[4] + gxm - gdx + following(gdx)
-    gxn = scatter_seq(lambda owner: lax.dynamic_slice_in_dim(gxn_part, owner * rows, rows, 0))
-    own_hat, own_inv = my_rows(xhat), my_rows(x_inv)
-    input_grad = gx1 + normalize_back(gxn, own_hat, own_inv, g1)
-    d_g1 = jnp.sum(gxn * own_hat, axis=0)
-    d_b1 = jnp.sum(gxn, axis=0)
-
-    def spread_out(array, dim):
-        shape = list(array.shape)
-        shape[dim] = width
-        return lax.dynamic_update_slice_in_dim(jnp.zeros(shape, F), array, here * cols, dim)
-
-    of_heads = spread_out(sums, 1)
-    vectors = jnp.stack(
-        [d_g1, d_b1, d_mu_x, *d_mu, of_heads[1], of_heads[0], of_heads[2], of_heads[3], d_g2, d_b2, d_cmu_k, d_cmu_r]
-    )
-    packed = jnp.concatenate(
-        [d_down_mix, d_down_decay, d_up_mix, spread_out(d_up_decay, 0), vectors.T, jnp.zeros((width, 48), F)], axis=1
-    )
-    packed = lax.psum_scatter(packed, ("seg", "seq"), scatter_dimension=0, tiled=True)
-    half = low_rank.shape[2]
-    rank_grad = jnp.stack([packed[:, :half], packed[:, half : 2 * half]])
-    vectors_grad = packed[:, 2 * half : 2 * half + 16].T
+
+    rest = scatter_seg(packed).T
+    final = Scatter(lambda start: cut(out, start, rows, 0).astype(F), rows)
+    final.hop()
+    rest = exchange_seq(rest.reshape(count, -1, 2 * PAD), 0, 0).astype(F)
+    input_grad = final.finish()
+    rest = jnp.sum(rest, axis=0)
+    rank_grad = jnp.stack([rest[:, :ranks], rest[:, PAD : PAD + ranks]])
+    few = jnp.concatenate([rest[:, ranks:PAD], rest[:, PAD + ranks :]], axis=1).T
+    vectors_grad = jnp.concatenate([few[0:3], few[32:37], few[17:18], few[16:17], few[18:20], few[8:12]], axis=0)
     return (block_out, input_grad, d_mats, rank_grad, vectors_grad, *cm_grads)
 
 

time: 1020 us -> 786 us (0.77)
  matrix products: 243 us -> 43.2 us
  Pallas kernels: 60.9 us -> 229 us
  waiting for transfers between devices: 351 us -> 183 us
  starting transfers between devices: 72.6 us -> 126 us
  blocking collectives: 37.2 us -> 0 us
  other arithmetic: 117 us -> 86.1 us
  local copies, waits for them, and re-layouts: 99.6 us -> 82.7 us
    pallas_call x0 -> x7, Pallas kernels: none -> 161 us  [the longest x3 74.7 us: mix_backward(): pl.pallas_call(functools.partial(mix_backward_body, not given, closes, se...]
    dot_general x16 -> x1, matrix products: 141 us -> 4.53 us  [mm_nt(): lax.dot_general(a, b, (((1,), (1,)), ((), ())), preferred_element_type=F)]
    unnamed x7 -> x2, waiting for transfers between devices: 106 us -> 0.03 us
    ppermute x49 -> x91, waiting for transfers between devices: 227 us -> 176 us  [the longest x9 67.8 us: ring_hops(): going_right = lax.ppermute(going_right, 'seq', ring.right)]
    ppermute x49 -> x91, starting transfers between devices: 56.1 us -> 106 us  [the longest x20 27.4 us: hop(): lax.ppermute(sent[0], 'seq', self.right)]
    dot_general x23 -> x9, matrix products: 58.1 us -> 10.4 us  [mm(): return jnp.dot(a, b, preferred_element_type=F)]
    all_to_all x1 -> x0, blocking collectives: 37.2 us -> none  [exchange_seq(): lax.all_to_all(value, 'seq', split_axis=split, concat_axis=join, tiled=True)]
    add x4 -> x3, other arithmetic: 37.9 us -> 5.31 us  [finish(): return self.term(0) + from_left.astype(F) + from_right.astype(F)]
  transfers between devices with their start and end apart: 58 -> 98, of which waited for: 37 -> 41; matrix products, arithmetic and copies ran while one was open for 36% -> 23% of each run, Pallas kernels for 2% -> 25%
where the time goes in v2:
time: 786 us; the launch traced here: 776 us
  Pallas kernels  229 us (29%)
  waiting for transfers between devices  183 us (23%)
  starting transfers between devices  126 us (16%)
  other arithmetic  86.1 us (11%)
  local copies, waits for them, and re-layouts  82.7 us (11%)
  matrix products  43.2 us (5%)
  between operations  25.7 us (3%)
    pallas_call x3, Pallas kernels, mix_backward(): pl.pallas_call(functools.partial(mix_backward_body, not given, closes, se...  74.7 us
    ppermute x9, waiting for transfers between devices, ring_hops(): going_right = lax.ppermute(going_right, 'seq', ring.right)  67.8 us
    pallas_call x4, Pallas kernels, wkv_backward(): pl.pallas_call(functools.partial(bwd_body, groups, nb), grid=(steps,), in...  45.9 us
    pallas_call x2, Pallas kernels, residual_backward(): pl.pallas_call(functools.partial(residual_backward_body, part == parts -...  38.9 us
    ppermute x20, waiting for transfers between devices, hop(): lax.ppermute(sent[0], 'seq', self.right)  36.7 us
    dynamic_update_slice x36, local copies, waits for them, and re-layouts, put(): return lax.dynamic_update_slice(array, piece, starts(array.ndim, at))  30 us
    dot_general x11, matrix products, mm_tn(): lax.dot_general(a, b, (((0,), (0,)), ((), ())), preferred_element_type=F)  28.3 us
    ppermute x20, starting transfers between devices, hop(): lax.ppermute(sent[0], 'seq', self.right)  27.4 us
  transfers between devices with their start and end apart: 98, of which 41 were waited for; matrix products, arithmetic and copies ran while one was open for 23% of the time, Pallas kernels for 25%

profile of v2, /device:TPU:0, one launch (start us, length us, event | category | flops | bytes accessed | tf_op | source)
XLA Modules:
  0.0 776.2 jit_solution(17805899864203005836)
XLA Ops:
  16.1 6.0 collective-permute-start.2
  31.1 11.3 %collective-permute-done.3 = bf16[1,4,64,256]{3,2,1,0:T(8,128)(2,1)S(1)} collective-permute-done((bf16[1,4,64,256]{3,2,1,0:T(8,128)(2,1)S(1)}, bf16[1,4,64,256]{3,2,1,0:T(8,128)(2,1)S(1)}, u32[]{:S(2)}, u32[]{:S(2)}) %collective-permute-start.3) | collective-permute-done | bytes 131104 | tf_op jit(solution)/shard_map/ppermute | solution.py:818
  42.5 11.8 %collective-permute-start.6 = (bf16[1,4,64,256]{3,2,1,0:T(8,128)(2,1)S(1)}, bf16[1,4,64,256]{3,2,1,0:T(8,128)(2,1)S(1)}, u32[]{:S(2)}, u32[]{:S(2)}) collective-permute-start(bf16[1,4,64,256]{3,2,1,0:T(8,128)(2,1)S(1)} %get-tuple-element.360), channel_id=1, source_target_pairs={{1,2},{3,0},{5,1},{7,3},{6,5},{4,7},{2,6},{0,4},{9,10},{11,8},{13,... | collective-permute-start | bytes 393224 | tf_op jit(solution)/shard_map/ppermute | solution.py:818
  88.1 5.7 collective-permute-done.11
  104.0 22.0 %collective-permute-done.16.rest_2_ = bf16[8,4,64,256]{3,2,1,0:T(8,128)(2,1)S(1)} collective-permute-done((bf16[8,4,64,256]{3,2,1,0:T(8,128)(2,1)S(1)}, bf16[8,4,64,256]{3,2,1,0:T(8,128)(2,1)S(1)}, u32[]{:S(2)}, u32[]{:S(2)}) %collective-permute-start.16) | collective-permute-done | bytes 1048608 | tf_op jit(solution)/shard_map/ppermute | solution.py:756
  135.4 25.7 %mix_forward.1 = (bf16[1024,256]{1,0:T(8,128)(2,1)}, bf16[1024,256]{1,0:T(8,128)(2,1)}, bf16[1024,256]{1,0:T(8,128)(2,1)}, f32[1024,256]{1,0:T(8,128)}, f32[1024...) custom-call(bf16[1024,2048]{1,0:T(8,128)(2,1)} %constant_dynamic-upd, ...), custom_call_target="tpu_custom_call" | custom-call | flops 11811160064 | bytes 25165824 | tf_op jit(solution)/shard_map/mix_forward/pallas_call | solution.py:397
  161.0 21.7 %wkv_forward.1 = (bf16[1024,256]{1,0:T(8,128)(2,1)}, f32[1024,256]{1,0:T(8,128)}, bf16[64,2,128,128]{3,2,1,0:T(8,128)(2,1)}) custom-call(bf16[1024,256]{1,0:T(8,128)(2,1)} %get-tuple-element.144.r_ref, bf16[1024,256]{1,0:T(8,128)(2,1)} %get-tuple-element.145.k_ref, bf16[1024,256]{1,0:T(8,128)(2,1)} %get-tuple-element.146.v_ref, ...), custom_call_target="tpu_custom_call" | custom-call | flops 268435456 | bytes 10485760 | tf_op jit(solution)/shard_map/wkv_forward/pallas_call | solution.py:145
  184.9 12.1 %collective-permute-done.18.rest_1_ = bf16[1024,256]{1,0:T(8,128)(2,1)S(1)} collective-permute-done((bf16[1024,256]{1,0:T(8,128)(2,1)}, bf16[1024,256]{1,0:T(8,128)(2,1)S(1)}, u32[]{:S(2)}, u32[]{:S(2)}) %collective-permute-start.18) | collective-permute-done | bytes 524320 | tf_op jit(solution)/shard_map/ppermute | solution.py:675
  199.0 11.1 %collective-permute-done.20.rest_3_ = bf16[1024,256]{1,0:T(8,128)(2,1)S(1)} collective-permute-done((bf16[1024,256]{1,0:T(8,128)(2,1)S(1)}, bf16[1024,256]{1,0:T(8,128)(2,1)S(1)}, u32[]{:S(2)}, u32[]{:S(2)}) %collective-permute-start.20) | collective-permute-done | bytes 524320 | tf_op jit(solution)/shard_map/ppermute | solution.py:675
  212.2 10.2 %collective-permute-done.22.rest_5_ = bf16[1024,256]{1,0:T(8,128)(2,1)S(1)} collective-permute-done((bf16[1024,256]{1,0:T(8,128)(2,1)S(1)}, bf16[1024,256]{1,0:T(8,128)(2,1)S(1)}, u32[]{:S(2)}, u32[]{:S(2)}) %collective-permute-start.22) | collective-permute-done | bytes 524320 | tf_op jit(solution)/shard_map/ppermute | solution.py:675
  231.9 22.3 %residual_forward.1 = (f32[1024,2048]{1,0:T(8,128)}, bf16[1024,2048]{1,0:T(8,128)(2,1)}, bf16[1024,2048]{1,0:T(8,128)(2,1)}, f32[1024,256]{1,0:T(8,128)}, bf16[1024,256]{1,0:T(8,128)(2,1)}) custom-call(bf16[1024,2048]{1,0:T(8,128)(2,1)} %constant_dynamic-update-slice_fusion.17.x_ref.before_ref, bf16[2048,2048]{1,0:T(8,128)(2,1)} %all-gather.3.cloned.1.call-done.w_ref, ...), custom_call_target="tpu_custom_call" | custom-call | flops 9663676416 | bytes 25165824 | tf_op jit(solution)/shard_map/residual_forward/pallas_call | solution.py:444
  256.3 10.3 %collective-permute-done.26 = bf16[1024,256]{1,0:T(8,128)(2,1)S(1)} collective-permute-done((bf16[1024,256]{1,0:T(8,128)(2,1)}, bf16[1024,256]{1,0:T(8,128)(2,1)S(1)}, u32[]{:S(2)}, u32[]{:S(2)}) %collective-permute-start.26) | collective-permute-done | bytes 524320 | tf_op jit(solution)/shard_map/ppermute | solution.py:675
  268.6 10.4 %collective-permute-done.28 = bf16[1024,256]{1,0:T(8,128)(2,1)} collective-permute-done((bf16[1024,256]{1,0:T(8,128)(2,1)S(1)}, bf16[1024,256]{1,0:T(8,128)(2,1)}, u32[]{:S(2)}, u32[]{:S(2)}) %collective-permute-start.28) | collective-permute-done | bytes 524320 | tf_op jit(solution)/shard_map/ppermute | solution.py:675
  286.4 4.8 collective-permute-done.30
  300.5 4.5 fusion.66
  305.1 4.6 multiply_convert_fusion
  324.0 8.2 %collective-permute-done.35 = bf16[1024,256]{1,0:T(8,128)(2,1)S(1)} collective-permute-done((bf16[1024,256]{1,0:T(8,128)(2,1)S(1)}, bf16[1024,256]{1,0:T(8,128)(2,1)S(1)}, u32[]{:S(2)}, u32[]{:S(2)}) %collective-permute-start.35) | collective-permute-done | bytes 524320 | tf_op jit(solution)/shard_map/ppermute | solution.py:735
  339.5 7.1 collective-permute-done.36
  354.1 5.9 collective-permute-done.37
  367.2 19.8 %residual_backward.2 = (bf16[512,2048]{1,0:T(8,128)(2,1)}, bf16[512,2048]{1,0:T(8,128)(2,1)}, f32[8,2048]{1,0:T(8,128)}, f32[8,2048]{1,0:T(8,128)}) custom-call(f32[1024,2048]{1,0:T(8,128)} %get-tuple-element.150.x1_ref.before_ref, f32[1024,2048]{1,0:T(8,128)} %get-tuple-element.150.x1_ref.before_ref, ...), custom_call_target="tpu_custom_call" | custom-call | flops 6710886400 | bytes 12582912 | tf_op jit(solution)/shard_map/residual_backward/pallas_call | solution.py:501
  398.4 19.1 %residual_backward.3 = (bf16[512,2048]{1,0:T(8,128)(2,1)}, bf16[512,2048]{1,0:T(8,128)(2,1)}, f32[8,2048]{1,0:T(8,128)}, f32[8,2048]{1,0:T(8,128)}) custom-call(f32[1024,2048]{1,0:T(8,128)} %get-tuple-element.150.x1_ref.before_ref, f32[1024,2048]{1,0:T(8,128)} %get-tuple-element.150.x1_ref.before_ref, ...), custom_call_target="tpu_custom_call" | custom-call | flops 6710886400 | bytes 12582912 | tf_op jit(solution)/shard_map/residual_backward/pallas_call | solution.py:501
  449.6 11.4 %wkv_backward.4 = (bf16[1024,256]{1,0:T(8,128)(2,1)}, bf16[1024,256]{1,0:T(8,128)(2,1)}, bf16[1024,256]{1,0:T(8,128)(2,1)}, bf16[1024,256]{1,0:T(8,128)(2,1)}, b...) custom-call(bf16[1024,256]{1,0:T(8,128)(2,1)} %get-tuple-element.144.r_ref, ...), custom_call_target="tpu_custom_call" | custom-call | flops 268435456 | bytes 3932160 | tf_op jit(solution)/shard_map/wkv_backward/pallas_call | solution.py:294
  466.9 11.4 %wkv_backward.5 = (bf16[1024,256]{1,0:T(8,128)(2,1)}, bf16[1024,256]{1,0:T(8,128)(2,1)}, bf16[1024,256]{1,0:T(8,128)(2,1)}, bf16[1024,256]{1,0:T(8,128)(2,1)}, b...) custom-call(bf16[1024,256]{1,0:T(8,128)(2,1)} %get-tuple-element.144, ...), custom_call_target="tpu_custom_call", output_to_operand_aliasing={{0}: (11, {}), {1}: (12, {}), {2}: (13, {}), {3}: (14, {}),... | custom-call | flops 268435456 | bytes 3932160 | tf_op jit(solution)/shard_map/wkv_backward/pallas_call | solution.py:294
  481.5 4.9 dynamic-slice_convert_fusion
  500.5 11.4 %wkv_backward.6 = (bf16[1024,256]{1,0:T(8,128)(2,1)}, bf16[1024,256]{1,0:T(8,128)(2,1)}, bf16[1024,256]{1,0:T(8,128)(2,1)}, bf16[1024,256]{1,0:T(8,128)(2,1)}, b...) custom-call(bf16[1024,256]{1,0:T(8,128)(2,1)} %get-tuple-element.144, ...), custom_call_target="tpu_custom_call", output_to_operand_aliasing={{0}: (11, {}), {1}: (12, {}), {2}: (13, {}), {3}: (14, {}),... | custom-call | flops 268435456 | bytes 3932160 | tf_op jit(solution)/shard_map/wkv_backward/pallas_call | solution.py:294
  518.4 11.8 %wkv_backward.7 = (bf16[1024,256]{1,0:T(8,128)(2,1)}, bf16[1024,256]{1,0:T(8,128)(2,1)}, bf16[1024,256]{1,0:T(8,128)(2,1)}, bf16[1024,256]{1,0:T(8,128)(2,1)}, b...) custom-call(bf16[1024,256]{1,0:T(8,128)(2,1)} %get-tuple-element.144, ...), custom_call_target="tpu_custom_call", output_to_operand_aliasing={{0}: (11, {}), {1}: (12, {}), {2}: (13, {}), {3}: (14, {}),... | custom-call | flops 268435456 | bytes 3932160 | tf_op jit(solution)/shard_map/wkv_backward/pallas_call | solution.py:294
  582.2 19.5 %mix_backward.3 = (bf16[1024,2048]{1,0:T(8,128)(2,1)}, f32[8,2048]{1,0:T(8,128)}, f32[512,2048]{1,0:T(8,128)}) custom-call(bf16[1024,2048]{1,0:T(8,128)(2,1)} %constant_dynamic-update-slice_fusion.17.x_ref.before_ref, bf16[1024,2048]{1,0:T(8,128)(2,1)} %constant_dynamic-update-slice_fusion.17.x_ref.before_ref, bf16[1024,256]{1,0:T(8,128)(2,1)} %get-tuple-element.238.gr_ref, ...), custom_call_target="tpu_custom_call" | custom-call | flops 4563402752 | bytes 5242880 | tf_op jit(solution)/shard_map/mix_backward/pallas_call | solution.py:609
  613.0 20.4 %mix_backward.4 = (bf16[1024,2048]{1,0:T(8,128)(2,1)}, f32[8,2048]{1,0:T(8,128)}, f32[512,2048]{1,0:T(8,128)}) custom-call(bf16[1024,2048]{1,0:T(8,128)(2,1)} %constant_dynamic-update-slice_fusion.17.x_ref.before_ref, bf16[1024,2048]{1,0:T(8,128)(2,1)} %constant_dynamic-update-slice_fusion.17.x_ref.before_ref, ...), custom_call_target="tpu_custom_call", output_to_operand_aliasing={{0}: (19, {})} | custom-call | flops 4563402752 | bytes 5242880 | tf_op jit(solution)/shard_map/mix_backward/pallas_call | solution.py:609
  642.7 34.8 %mix_backward.5 = (bf16[1024,2048]{1,0:T(8,128)(2,1)}, f32[8,2048]{1,0:T(8,128)}, f32[512,2048]{1,0:T(8,128)}, bf16[4,512,512]{2,1,0:T(8,128)(2,1)}) custom-call(bf16[1024,2048]{1,0:T(8,128)(2,1)} %constant_dynamic-update-slice_fusion.17.x_ref.before_ref, ...), custom_call_target="tpu_custom_call", output_to_operand_aliasing={{0}: (19, {})} | custom-call | flops 9126805504 | bytes 10485760 | tf_op jit(solution)/shard_map/mix_backward/pallas_call | solution.py:609
  710.8 6.1 fusion.2
  728.9 5.8 fusion.1
  759.2 7.0 all-to-all-done.4
  (478 shorter events, 351.3 us)
Async XLA Ops:
  7.2 128.1 %all-gather.5.cloned.1.call-start = ((), (), s32[]{:S(2)}) async-start(), calls=%async_computation.6 | async-start | bytes 2162688 | tf_op jit(solution)/shard_map/all_gather | solution.py:843
  8.9 223.0 %all-gather.3.cloned.1.call-start = ((), (), s32[]{:S(2)}) async-start(), calls=%async_computation.5 | async-start | bytes 8650752 | tf_op jit(solution)/shard_map/all_gather | solution.py:847
  22.2 41.3 %collective-permute-start = (bf16[128,2048]{1,0:T(8,128)(2,1)S(1)}, bf16[128,2048]{1,0:T(8,128)(2,1)}, u32[]{:S(2)}, u32[]{:S(2)}) collective-permute-start(bf16[128,2048]{1,0:T(8,128)(2,1)S(1)} %copy-done.40), channel_id=1, source_target_pairs={{1,3},{3,5},{5,7},{7,6},{6,4},{4,2},{2,0},{0,1},{9,11},{11,13},{13... | collective-permute-start | bytes 1572872 | tf_op jit(solution)/shard_map/ppermute | solution.py:675
  22.7 40.7 %collective-permute-start.1 = (bf16[128,2048]{1,0:T(8,128)(2,1)S(1)}, bf16[128,2048]{1,0:T(8,128)(2,1)S(1)}, u32[]{:S(2)}, u32[]{:S(2)}) collective-permute-start(bf16[128,2048]{1,0:T(8,128)(2,1)S(1)} %copy-done.40), channel_id=1, source_target_pairs={{3,1},{5,3},{7,5},{6,7},{4,6},{2,4},{0,2},{1,0},{11,9},{13,11},{15... | collective-permute-start | bytes 1572872 | tf_op jit(solution)/shard_map/ppermute | solution.py:676
  24.2 30.7 %collective-permute-start.4 = (bf16[1,4,64,256]{3,2,1,0:T(8,128)(2,1)S(1)}, bf16[1,4,64,256]{3,2,1,0:T(8,128)(2,1)S(1)}, u32[]{:S(2)}, u32[]{:S(2)}) collective-permute-start(bf16[1,4,64,256]{3,2,1,0:T(8,128)(2,1)S(1)} %get-tuple-element.362), channel_id=1, source_target_pairs={{1,4},{3,2},{5,0},{7,1},{6,3},{4,5},{2,7},{0,6},{9,12},{11,10},{13... | collective-permute-start | bytes 393224 | tf_op jit(solution)/shard_map/ppermute | solution.py:818
  29.4 28.4 %collective-permute-start.5 = (bf16[1,4,64,256]{3,2,1,0:T(8,128)(2,1)S(1)}, bf16[1,4,64,256]{3,2,1,0:T(8,128)(2,1)S(1)}, u32[]{:S(2)}, u32[]{:S(2)}) collective-permute-start(bf16[1,4,64,256]{3,2,1,0:T(8,128)(2,1)S(1)} %get-tuple-element.361), channel_id=1, source_target_pairs={{1,5},{3,7},{5,6},{7,4},{6,2},{4,0},{2,1},{0,3},{9,13},{11,15},{13... | collective-permute-start | bytes 393224 | tf_op jit(solution)/shard_map/ppermute | solution.py:818
  101.7 24.3 %collective-permute-start.16 = (bf16[8,4,64,256]{3,2,1,0:T(8,128)(2,1)S(1)}, bf16[8,4,64,256]{3,2,1,0:T(8,128)(2,1)S(1)}, u32[]{:S(2)}, u32[]{:S(2)}) collective-permute-start(bf16[8,4,64,256]{3,2,1,0:T(8,128)(2,1)S(1)} %constant_dynamic-update-slice_fusion.25.rest_0_), channel_id=1, source_target_pairs={{0,16},{8,24},{16,0},{24,8},{1,17},{9,25},{17,1},{25,9},{2,18},{10... | collective-permute-start | bytes 3145736 | tf_op jit(solution)/shard_map/ppermute | solution.py:756
  104.0 31.3 %collective-permute-start.15 = (bf16[8,4,64,256]{3,2,1,0:T(8,128)(2,1)S(1)}, bf16[8,4,64,256]{3,2,1,0:T(8,128)(2,1)}, u32[]{:S(2)}, u32[]{:S(2)}) collective-permute-start(bf16[8,4,64,256]{3,2,1,0:T(8,128)(2,1)S(1)} %constant_dynamic-update-slice_fusion.25.rest_0_), channel_id=1, source_target_pairs={{0,8},{8,0},{16,24},{24,16},{1,9},{9,1},{17,25},{25,17},{2,10},{10... | collective-permute-start | bytes 3145736 | tf_op jit(solution)/shard_map/ppermute | solution.py:756
  131.2 29.8 %all-to-all-start = ((bf16[128,8,256]{2,0,1:T(8,128)(2,1)}), bf16[128,8,256]{2,0,1:T(8,128)(2,1)S(1)}, u32[]{:S(2)}, u32[]{:S(2)}) async-start(bf16[128,8,256]{2,0,1:T(8,128)(2,1)} %bitcast.151), calls=%async_computation | async-start | bytes 1048576 | tf_op jit(solution)/shard_map/all_to_all | solution.py:823
  317.7 72.8 %collective-permute-start.43 = (bf16[448,2048]{1,0:T(8,128)(2,1)}, bf16[448,2048]{1,0:T(8,128)(2,1)}, u32[]{:S(2)}, u32[]{:S(2)}) collective-permute-start(bf16[448,2048]{1,0:T(8,128)(2,1)} %convolution_convert_fusion), channel_id=1, source_target_pairs={{0,8},{8,0},{16,24},{24,16},{1,9},{9,1},{17,25},{25,17},{2,10},{10... | collective-permute-start | bytes 5505032 | tf_op jit(solution)/shard_map/ppermute | solution.py:887
  324.0 66.5 %collective-permute-start.42 = (bf16[1024,896]{1,0:T(8,128)(2,1)}, bf16[1024,896]{1,0:T(8,128)(2,1)}, u32[]{:S(2)}, u32[]{:S(2)}) collective-permute-start(bf16[1024,896]{1,0:T(8,128)(2,1)} %fusion.15), channel_id=1, source_target_pairs={{0,8},{8,0},{16,24},{24,16},{1,9},{9,1},{17,25},{25,17},{2,10},{10... | collective-permute-start | bytes 5505032 | tf_op jit(solution)/shard_map/ppermute | solution.py:887
  364.9 25.6 %collective-permute-start.44 = (bf16[1024,256]{1,0:T(8,128)(2,1)S(1)}, bf16[1024,256]{1,0:T(8,128)(2,1)S(1)}, u32[]{:S(2)}, u32[]{:S(2)}) collective-permute-start(bf16[1024,256]{1,0:T(8,128)(2,1)S(1)} %fusion.26), channel_id=1, source_target_pairs={{0,8},{8,0},{16,24},{24,16},{1,9},{9,1},{17,25},{25,17},{2,10},{10... | collective-permute-start | bytes 1572872 | tf_op jit(solution)/shard_map/ppermute | solution.py:887
  388.3 30.7 %collective-permute-start.47 = (bf16[256,256]{1,0:T(8,128)(2,1)S(1)}, bf16[256,256]{1,0:T(8,128)(2,1)S(1)}, u32[]{:S(2)}, u32[]{:S(2)}) collective-permute-start(bf16[256,256]{1,0:T(8,128)(2,1)S(1)} %get-tuple-element.347), channel_id=1, source_target_pairs={{1,3},{3,5},{5,7},{7,6},{6,4},{4,2},{2,0},{0,1},{9,11},{11,13},{13... | collective-permute-start | bytes 393224 | tf_op jit(solution)/shard_map/ppermute | solution.py:735
  389.8 29.1 %collective-permute-start.48 = (bf16[256,256]{1,0:T(8,128)(2,1)S(1)}, bf16[256,256]{1,0:T(8,128)(2,1)S(1)}, u32[]{:S(2)}, u32[]{:S(2)}) collective-permute-start(bf16[256,256]{1,0:T(8,128)(2,1)S(1)} %get-tuple-element.349), channel_id=1, source_target_pairs={{3,1},{5,3},{7,5},{6,7},{4,6},{2,4},{0,2},{1,0},{11,9},{13,11},{15... | collective-permute-start | bytes 393224 | tf_op jit(solution)/shard_map/ppermute | solution.py:735
  394.6 45.8 %collective-permute-start.55 = (bf16[512,896]{1,0:T(8,128)(2,1)S(1)}, bf16[512,896]{1,0:T(8,128)(2,1)}, u32[]{:S(2)}, u32[]{:S(2)}) collective-permute-start(bf16[512,896]{1,0:T(8,128)(2,1)S(1)} %get-tuple-element.164), channel_id=1, source_target_pairs={{0,16},{8,24},{16,0},{24,8},{1,17},{9,25},{17,1},{25,9},{2,18},{10... | collective-permute-start | bytes 2752520 | tf_op jit(solution)/shard_map/ppermute | solution.py:790
  422.6 38.4 %collective-permute-start.58 = (bf16[512,896]{1,0:T(8,128)(2,1)}, bf16[512,896]{1,0:T(8,128)(2,1)}, u32[]{:S(2)}, u32[]{:S(2)}) collective-permute-start(bf16[512,896]{1,0:T(8,128)(2,1)} %get-tuple-element.356), channel_id=1, source_target_pairs={{0,16},{8,24},{16,0},{24,8},{1,17},{9,25},{17,1},{25,9},{2,18},{10... | collective-permute-start | bytes 2752520 | tf_op jit(solution)/shard_map/ppermute | solution.py:790
  424.4 36.6 %collective-permute-start.45 = (bf16[256,256]{1,0:T(8,128)(2,1)S(1)}, bf16[256,256]{1,0:T(8,128)(2,1)S(1)}, u32[]{:S(2)}, u32[]{:S(2)}) collective-permute-start(bf16[256,256]{1,0:T(8,128)(2,1)S(1)} %get-tuple-element.337), channel_id=1, source_target_pairs={{1,3},{3,5},{5,7},{7,6},{6,4},{4,2},{2,0},{0,1},{9,11},{11,13},{13... | collective-permute-start | bytes 393224 | tf_op jit(solution)/shard_map/ppermute | solution.py:735
  437.0 24.0 %collective-permute-start.46 = (bf16[256,256]{1,0:T(8,128)(2,1)S(1)}, bf16[256,256]{1,0:T(8,128)(2,1)S(1)}, u32[]{:S(2)}, u32[]{:S(2)}) collective-permute-start(bf16[256,256]{1,0:T(8,128)(2,1)S(1)} %get-tuple-element.338), channel_id=1, source_target_pairs={{3,1},{5,3},{7,5},{6,7},{4,6},{2,4},{0,2},{1,0},{11,9},{13,11},{15... | collective-permute-start | bytes 393224 | tf_op jit(solution)/shard_map/ppermute | solution.py:735
  445.3 41.2 %collective-permute-start.63 = (bf16[224,2048]{1,0:T(8,128)(2,1)}, bf16[224,2048]{1,0:T(8,128)(2,1)}, u32[]{:S(2)}, u32[]{:S(2)}) collective-permute-start(bf16[224,2048]{1,0:T(8,128)(2,1)} %get-tuple-element.355), channel_id=1, source_target_pairs={{0,16},{8,24},{16,0},{24,8},{1,17},{9,25},{17,1},{25,9},{2,18},{10... | collective-permute-start | bytes 2752520 | tf_op jit(solution)/shard_map/ppermute | solution.py:790
  447.0 65.0 %collective-permute-start.66 = (bf16[224,2048]{1,0:T(8,128)(2,1)}, bf16[224,2048]{1,0:T(8,128)(2,1)}, u32[]{:S(2)}, u32[]{:S(2)}) collective-permute-start(bf16[224,2048]{1,0:T(8,128)(2,1)} %get-tuple-element.354), channel_id=1, source_target_pairs={{0,16},{8,24},{16,0},{24,8},{1,17},{9,25},{17,1},{25,9},{2,18},{10... | collective-permute-start | bytes 2752520 | tf_op jit(solution)/shard_map/ppermute | solution.py:790
  542.5 34.2 %collective-permute-start.70 = (bf16[2,512,4,256]{3,1,2,0:T(8,128)(2,1)}, bf16[2,512,4,256]{3,1,2,0:T(8,128)(2,1)}, u32[]{:S(2)}, u32[]{:S(2)}) collective-permute-start(bf16[2,512,4,256]{3,1,2,0:T(8,128)(2,1)} %bitcast.150), channel_id=1, source_target_pairs={{0,8},{8,0},{16,24},{24,16},{1,9},{9,1},{17,25},{25,17},{2,10},{10... | collective-permute-start | bytes 6291464 | tf_op jit(solution)/shard_map/ppermute | solution.py:771
  561.5 47.9 %all-to-all-start.1 = ((bf16[8,128,256]{2,1,0:T(8,128)(2,1)}), bf16[8,128,256]{2,1,0:T(8,128)(2,1)}, u32[]{:S(2)}, u32[]{:S(2)}) async-start(bf16[8,128,256]{2,1,0:T(8,128)(2,1)} %bitcast.158), calls=%async_computation.1 | async-start | bytes 1048576 | tf_op jit(solution)/shard_map/all_to_all | solution.py:823
  572.5 29.1 %collective-permute-start.72 = (bf16[1024,256]{1,0:T(8,128)(2,1)}, bf16[1024,256]{1,0:T(8,128)(2,1)}, u32[]{:S(2)}, u32[]{:S(2)}) collective-permute-start(bf16[1024,256]{1,0:T(8,128)(2,1)} %add_convert_fusion.17), channel_id=1, source_target_pairs={{3,1},{5,3},{7,5},{6,7},{4,6},{2,4},{0,2},{1,0},{11,9},{13,11},{15... | collective-permute-start | bytes 1572872 | tf_op jit(solution)/shard_map/ppermute | solution.py:735
  575.2 26.4 %collective-permute-start.71 = (bf16[1024,256]{1,0:T(8,128)(2,1)}, bf16[1024,256]{1,0:T(8,128)(2,1)}, u32[]{:S(2)}, u32[]{:S(2)}) collective-permute-start(bf16[1024,256]{1,0:T(8,128)(2,1)} %add_convert_fusion.18), channel_id=1, source_target_pairs={{1,3},{3,5},{5,7},{7,6},{6,4},{4,2},{2,0},{0,1},{9,11},{11,13},{13... | collective-permute-start | bytes 1572872 | tf_op jit(solution)/shard_map/ppermute | solution.py:735
  579.9 27.0 %collective-permute-start.73 = (bf16[1,512,4,256]{3,1,2,0:T(8,128)(2,1)}, bf16[1,512,4,256]{3,1,2,0:T(8,128)(2,1)}, u32[]{:S(2)}, u32[]{:S(2)}) collective-permute-start(bf16[1,512,4,256]{3,1,2,0:T(8,128)(2,1)} %get-tuple-element.330), channel_id=1, source_target_pairs={{0,16},{8,24},{16,0},{24,8},{1,17},{9,25},{17,1},{25,9},{2,18},{10... | collective-permute-start | bytes 3145736 | tf_op jit(solution)/shard_map/ppermute | solution.py:771
  603.6 29.7 %collective-permute-start.75 = (bf16[1024,256]{1,0:T(8,128)(2,1)}, bf16[1024,256]{1,0:T(8,128)(2,1)S(1)}, u32[]{:S(2)}, u32[]{:S(2)}) collective-permute-start(bf16[1024,256]{1,0:T(8,128)(2,1)} %add_convert_fusion.13), channel_id=1, source_target_pairs={{3,1},{5,3},{7,5},{6,7},{4,6},{2,4},{0,2},{1,0},{11,9},{13,11},{15... | collective-permute-start | bytes 1572872 | tf_op jit(solution)/shard_map/ppermute | solution.py:735
  605.1 28.3 %collective-permute-start.74 = (bf16[1024,256]{1,0:T(8,128)(2,1)S(1)}, bf16[1024,256]{1,0:T(8,128)(2,1)}, u32[]{:S(2)}, u32[]{:S(2)}) collective-permute-start(bf16[1024,256]{1,0:T(8,128)(2,1)S(1)} %add_convert_fusion.14), channel_id=1, source_target_pairs={{1,3},{3,5},{5,7},{7,6},{6,4},{4,2},{2,0},{0,1},{9,11},{11,13},{13... | collective-permute-start | bytes 1572872 | tf_op jit(solution)/shard_map/ppermute | solution.py:735
  609.4 33.3 %all-to-all-start.2 = ((bf16[8,256,256]{2,1,0:T(8,128)(2,1)}), bf16[8,256,256]{2,1,0:T(8,128)(2,1)S(1)}, u32[]{:S(2)}, u32[]{:S(2)}) async-start(bf16[8,256,256]{2,1,0:T(8,128)(2,1)} %bitcast.62), calls=%async_computation.2 | async-start | bytes 2097152 | tf_op jit(solution)/shard_map/all_to_all | solution.py:823
  639.8 55.6 %collective-permute-start.88 = (bf16[1024,896]{1,0:T(8,128)(2,1)S(1)}, bf16[1024,896]{1,0:T(8,128)(2,1)}, u32[]{:S(2)}, u32[]{:S(2)}) collective-permute-start(bf16[1024,896]{1,0:T(8,128)(2,1)S(1)} %pad_maximum_fusion.1), channel_id=1, source_target_pairs={{0,8},{8,0},{16,24},{24,16},{1,9},{9,1},{17,25},{25,17},{2,10},{10... | collective-permute-start | bytes 5505032 | tf_op jit(solution)/shard_map/ppermute | solution.py:966
  641.6 54.6 %collective-permute-start.89 = (bf16[448,2048]{1,0:T(8,128)(2,1)}, bf16[448,2048]{1,0:T(8,128)(2,1)}, u32[]{:S(2)}, u32[]{:S(2)}) collective-permute-start(bf16[448,2048]{1,0:T(8,128)(2,1)} %pad_maximum_fusion.2), channel_id=1, source_target_pairs={{0,8},{8,0},{16,24},{24,16},{1,9},{9,1},{17,25},{25,17},{2,10},{10... | collective-permute-start | bytes 5505032 | tf_op jit(solution)/shard_map/ppermute | solution.py:966
  700.3 43.4 %all-to-all-start.3 = ((bf16[8,64,256]{2,1,0:T(8,128)(2,1)}), bf16[8,64,256]{2,1,0:T(8,128)(2,1)}, u32[]{:S(2)}, u32[]{:S(2)}) async-start(bf16[8,64,256]{2,1,0:T(8,128)(2,1)} %bitcast.164), calls=%async_computation.3 | async-start | bytes 524288 | tf_op jit(solution)/shard_map/all_to_all | solution.py:823
  743.6 22.6 %all-to-all-start.4 = ((bf16[8,64,512]{2,1,0:T(8,128)(2,1)}), bf16[8,64,512]{2,1,0:T(8,128)(2,1)S(1)}, u32[]{:S(2)}, u32[]{:S(2)}) async-start(bf16[8,64,512]{2,1,0:T(8,128)(2,1)} %bitcast.162), calls=%async_computation.4 | async-start | bytes 1048576 | tf_op jit(solution)/shard_map/all_to_all | solution.py:823
  (123 other events, 1547.7 us)
Sparse Core Ops, SparseCore 0:
  11.6 68.2 all-gather.4
  101.8 85.9 all-gather.2

commit v3 on v2

--- a/solution.py
+++ b/solution.py
@@ -153,7 +153,7 @@
             jax.ShapeDtypeStruct((tokens // B, groups, LANES, LANES), HB),
         ],
         scratch_shapes=[pltpu.VMEM((groups, LANES, LANES), F)],
-        cost_estimate=pl.CostEstimate(flops=tokens * width * 1024, transcendentals=tokens * width * 16, bytes_accessed=tokens * width * 40),
+        cost_estimate=pl.CostEstimate(flops=tokens * width * 95000, transcendentals=tokens * width * 16, bytes_accessed=tokens * width * 40),
         name="wkv_forward",
     )(r, k, v, rate, gp, vec, start)
 
@@ -299,7 +299,7 @@
         out_specs=[row] * 5 + [full(adj.shape), full(sums.shape)],
         out_shape=[low] * 5 + [jax.ShapeDtypeStruct(adj.shape, F), jax.ShapeDtypeStruct(sums.shape, F)],
         input_output_aliases={11 + i: i for i in range(len(outs))},
-        cost_estimate=pl.CostEstimate(flops=count * width * 4096, transcendentals=count * width * 20, bytes_accessed=count * width * 60),
+        cost_estimate=pl.CostEstimate(flops=count * width * 184000, transcendentals=count * width * 20, bytes_accessed=count * width * 60),
         name="wkv_backward",
     )(r, k, v, rate, gp, y, gz, vec, states, adj, sums, *outs)
     return outs, adj, sums
@@ -402,7 +402,7 @@
         out_shape=[shape(cols, HB)] * 3 + [shape(cols, F)] * 2 + [shape(PAD, F)] + [shape(width, HB)] * 4,
         scratch_shapes=[pltpu.VMEM((8, width), F)],
         compiler_params=pltpu.CompilerParams(vmem_limit_bytes=VMEM),
-        cost_estimate=pl.CostEstimate(flops=total * width * (8 * cols + 14 * 256), transcendentals=total * 512, bytes_accessed=total * width * 12),
+        cost_estimate=pl.CostEstimate(flops=total * width * 13700, transcendentals=total * 512, bytes_accessed=total * width * 12),
         name="mix_forward",
     )(x, prm, rank, rank, at, *mats)
 
@@ -449,7 +449,7 @@
         out_shape=[shape(width, F), shape(width, HB), shape(width, HB), shape(cols, F), shape(cols, HB)],
         scratch_shapes=[pltpu.VMEM((8, width), F)],
         compiler_params=pltpu.CompilerParams(vmem_limit_bytes=VMEM),
-        cost_estimate=pl.CostEstimate(flops=2 * total * width * (width + cols), transcendentals=total * cols, bytes_accessed=total * width * 12),
+        cost_estimate=pl.CostEstimate(flops=total * width * 12000, transcendentals=total * cols, bytes_accessed=total * width * 12),
         name="residual_forward",
     )(x, w_output, prm, recept, go_cols, at, *z, *z_far)
 
@@ -497,7 +497,7 @@
     low = jax.ShapeDtypeStruct((total // parts, width), HB)
     few = jax.ShapeDtypeStruct((8, width), F)
     const = pl.BlockSpec((8, width), lambda i: (0, 0))
-    flops = steps * tile * width * 2 * (width + ghp.shape[1] + gsp.shape[1])
+    flops = steps * tile * width * 17500
     return pl.pallas_call(
         functools.partial(residual_backward_body, part == parts - 1),
         grid=(steps,),
@@ -510,15 +510,13 @@
     )(x1, x1, go_own, ghp, gsp, key, recept, w_output, prm, sums, ahead)
 
 
-def mix_backward_body(opens, closes, segs, x_ref, before_ref, gr_ref, gk_ref, gv_ref, gg_ref, grb_ref, t_ref, gx1_ref,
-                      prm_ref, two_ref, heads_ref, down_ref, up_ref, at_ref, *rest):
-    w_refs, rest = rest[:segs], rest[segs:]
+def mix_backward_body(opens, closes, x_ref, before_ref, gr_ref, gk_ref, gv_ref, gg_ref, grb_ref, t_ref, gx1_ref,
+                      prm_ref, two_ref, heads_ref, up_ref, downt_ref, upt_ref, at_ref, w_ref, *rest):
     given = rest[: 0 if opens else 3]
     out_ref, ahead, packed, *more = rest[len(given) :]
-    gmix, mstack, gx_ref = more[-3:]
+    gmix, mstack = more[-2:]
     at = pl.program_id(0)
     width, cols = x_ref.shape[1], gr_ref.shape[1]
-    part = width // segs
     tile = x_ref.shape[0]
 
     @pl.when(at == 0)
@@ -553,14 +551,12 @@
     for j, (slot, g_ref) in enumerate(((None, None), (1, gk_ref), (2, gv_ref), (0, gr_ref), (3, gg_ref))):
         own = jnp.where(group == j, low, zero)
         mstack[j * tile : (j + 1) * tile, :] = jnp.where(lane == 7 * MIX_RANK + j, jnp.ones_like(own), own)
-        lerp = prm(3 + j) + mm_nt(own, up_ref[...])
+        lerp = prm(3 + j) + mm(own, upt_ref[...])
         if j == 0:
-            gx = mm_nt(ge, down_ref[...])
+            gx = mm(ge, downt_ref[...])
             x_w = (xn + dx * lerp).astype(HB)
         else:
-            for i, w in enumerate(weight_cols(w_refs, slot)):
-                gx_ref[:, pl.ds(pl.multiple_of(at_ref[1 + i], part), part)] = mm_nt(g_ref[...], w)
-            gx = gx_ref[...]
+            gx = mm_nt(g_ref[...], w_ref[:, slot].reshape(width, cols))
         moved = gx * lerp
         gdx = moved if gdx is None else gdx + moved
         gsum = gx if gsum is None else gsum + gx
@@ -569,7 +565,7 @@
         part_m = jnp.where(group == j, mm(bits, up_ref[...]), 0.0)
         gm = part_m if gm is None else gm + part_m
     gm = (gm * slope).astype(HB)
-    gxm = mm_nt(gm, down_ref[...])
+    gxm = mm(gm, downt_ref[...])
     gdx = gdx + gxm * prm(2)
     gxn = gsum + gxm - gdx + shift_up(gdx, ahead[0:1, :])
     ahead[0:1, :] = gdx[0:1, :]
@@ -592,34 +588,78 @@
                 more[0][i] = packed[:, i * block : (i + 1) * block].astype(HB)
 
 
-def mix_backward(x, grads, t, gx1_parts, mats, rank, prm, two, heads, at, first_tile, steps, given, tile=256):
+def mix_backward(x, grads, t, gx1, mats, rank, down_t, up_t, prm, two, heads, at, segs, first_tile, steps, given, tile=256):
     total, width = x.shape
-    segs = len(mats)
-    cols = mats[0].shape[3]
+    cols = mats.shape[3]
     lines = 2 * PAD
     shape = jax.ShapeDtypeStruct
     fixed = lambda *s: pl.BlockSpec(s, lambda i: (0,) * len(s))
     top = first_tile
     row = lambda n: pl.BlockSpec((tile, n), lambda i: (top - i, 0))
-    per = total // tile // len(gx1_parts)
-    first = top // per * per
-    gx1 = gx1_parts[len(gx1_parts) - 1 - top // per]
     before = pl.BlockSpec((16, width), lambda i: (jnp.maximum((top - i) * (tile // 16) - 1, 0), 0))
     closes = top - steps < 0
     return pl.pallas_call(
-        functools.partial(mix_backward_body, not given, closes, segs),
+        functools.partial(mix_backward_body, not given, closes),
         grid=(steps,),
-        in_specs=[row(width), before] + [row(cols)] * 5 + [row(PAD), pl.BlockSpec((tile, width), lambda i: (top - first - i, 0))]
-        + [whole(a) for a in (prm, two, heads)] + rank_halves(width) + [SCALARS] + [whole(a) for a in mats]
+        in_specs=[row(width), before] + [row(cols)] * 5 + [row(PAD), row(width)]
+        + [whole(a) for a in (prm, two, heads)] + rank_halves(width)[1:] + [whole(down_t), whole(up_t), SCALARS, whole(mats)]
         + ([pl.BlockSpec(memory_space=pl.ANY), whole(given[1]), whole(given[2])] if given else []),
         out_specs=[row(width), fixed(8, width), fixed(lines, width)] + [fixed(segs, lines, width // segs)] * closes,
         out_shape=[shape((total, width), HB), shape((8, width), F), shape((lines, width), F)] + [shape((segs, lines, width // segs), HB)] * closes,
-        input_output_aliases={15 + segs: 0} if given else {},
-        scratch_shapes=[pltpu.VMEM((5 * tile, width), HB), pltpu.VMEM((5 * tile, PAD), HB), pltpu.VMEM((tile, width), F)],
+        input_output_aliases={17: 0} if given else {},
+        scratch_shapes=[pltpu.VMEM((5 * tile, width), HB), pltpu.VMEM((5 * tile, PAD), HB)],
         compiler_params=pltpu.CompilerParams(vmem_limit_bytes=VMEM),
-        cost_estimate=pl.CostEstimate(flops=steps * tile * width * (8 * cols + 26 * 256), transcendentals=total, bytes_accessed=steps * tile * width * 10),
+        cost_estimate=pl.CostEstimate(flops=steps * tile * width * 35000, transcendentals=total, bytes_accessed=steps * tile * width * 10),
         name="mix_backward",
-    )(x, x, *grads, t, gx1, prm, two, heads, rank, rank, at, *mats, *given)
+    )(x, x, *grads, t, gx1, prm, two, heads, rank, down_t, up_t, at, mats, *given)
+
+
+def outer_parts_body(at_ref, grad_ref, *rest):
+    *parts, low_ref, high_ref, out_ref = rest
+    cols = grad_ref.shape[1]
+    half = low_ref.shape[0]
+    rows = lambda i: pl.ds(pl.multiple_of(at_ref[i], cols), cols)
+    for i, ref in enumerate(parts):
+        out_ref[rows(i), :] = mm_tn(ref[...], grad_ref[...]).astype(HB)
+    far = mm_tn(low_ref[...], grad_ref[:half, :]) + mm_tn(high_ref[...], grad_ref[half:, :])
+    out_ref[rows(len(parts)), :] = far.astype(HB)
+
+
+def outer_parts(parts, far, at, grad, width):
+    total, cols = grad.shape
+    everything = lambda a: pl.BlockSpec(a.shape, lambda: (0,) * a.ndim)
+    return pl.pallas_call(
+        outer_parts_body,
+        in_specs=[SCALARS] + [everything(a) for a in (grad, *parts, *far)],
+        out_specs=pl.BlockSpec((width, cols), lambda: (0, 0)),
+        out_shape=jax.ShapeDtypeStruct((width, cols), HB),
+        compiler_params=pltpu.CompilerParams(vmem_limit_bytes=VMEM),
+        cost_estimate=pl.CostEstimate(flops=2 * total * cols * width, transcendentals=0, bytes_accessed=2 * total * width),
+        name="outer_parts",
+    )(at, grad, *parts, *far)
+
+
+def join_body(bit_ref, mine_ref, other_ref, out_ref):
+    out_ref[...] = jnp.where(pl.program_id(0) == bit_ref[0], mine_ref[...], other_ref[...]).astype(F)
+
+
+def join_halves(mine, other, bit):
+    count, width = mine.shape
+    rows = count // 4 if count % 64 == 0 else count
+    steps = count // rows
+    held = lambda own: pl.BlockSpec((rows, width), lambda h, i, b: (jnp.where((h == b[0]) == own, i, 0), 0))
+    return pl.pallas_call(
+        join_body,
+        grid_spec=pltpu.PrefetchScalarGridSpec(
+            num_scalar_prefetch=1,
+            grid=(2, steps),
+            in_specs=[held(True), held(False)],
+            out_specs=pl.BlockSpec((rows, width), lambda h, i, b: (h * steps + i, 0)),
+        ),
+        out_shape=jax.ShapeDtypeStruct((2 * count, width), F),
+        cost_estimate=pl.CostEstimate(flops=0, transcendentals=0, bytes_accessed=12 * count * width),
+        name="join_halves",
+    )(bit, mine, other)
 
 
 def ring_of(count):
@@ -666,7 +706,7 @@
     return lax.dynamic_update_slice(array, piece, starts(array.ndim, at))
 
 
-def ring_hops(part, other=None):
+def ring_hops(part, others=()):
     ring = Ring()
     half = part.shape[0] // 2
     held = [(0, part)]
@@ -674,8 +714,8 @@
     for step in range(1, ring.count // 2):
         going_right = lax.ppermute(going_right, "seq", ring.right)
         going_left = lax.ppermute(going_left, "seq", ring.left)
-        if step == 1 and other is not None:
-            going_right, going_left = after((going_right, going_left), other)
+        if step <= len(others):
+            going_right, going_left = after((going_right, going_left), others[step - 1])
         held += [(-step, going_right), (step, going_left)]
     far = lax.ppermute(going_right[:half], "seq", ring.right), lax.ppermute(going_left[half:], "seq", ring.left)
     return held, far
@@ -697,8 +737,8 @@
     return put(out, far[1], low)
 
 
-def gather_seq(part, dim, other=None):
-    return assembled(*ring_hops(part, other), dim)
+def gather_seq(part, dim, others=()):
+    return assembled(*ring_hops(part, others), dim)
 
 
 def after(value, other):
@@ -762,22 +802,27 @@
     return (lax.axis_index("seg").astype(jnp.uint32) & np.uint32(step)) // np.uint32(step) if step > 1 else lax.axis_index("seg").astype(jnp.uint32) & np.uint32(1)
 
 
-def seg_round(parts, step):
+def seg_round(parts, step, dim=0):
     count = lax.axis_size("seg")
     bit = seg_bit(step)
-    shaped = parts.reshape((parts.shape[0] // 2, 2) + parts.shape[1:])
-    keep = lax.squeeze(cut(shaped, bit, 1, 1), (1,))
-    give = lax.squeeze(cut(shaped, np.uint32(1) - bit, 1, 1), (1,))
+    shape = list(parts.shape)
+    shaped = parts.reshape(shape[:dim] + [shape[dim] // 2, 2] + shape[dim + 1 :])
+    keep = lax.squeeze(cut(shaped, bit, 1, dim + 1), (dim + 1,))
+    give = lax.squeeze(cut(shaped, np.uint32(1) - bit, 1, dim + 1), (dim + 1,))
     return keep, lax.ppermute(give, "seg", [(i, i ^ step) for i in range(count)])
 
 
+def seg_rest(keep, come, step, dim=0):
+    parts = (keep.astype(F) + come.astype(F)).astype(HB)
+    while step * 2 < lax.axis_size("seg"):
+        step *= 2
+        keep, come = seg_round(parts, step, dim)
+        parts = (keep.astype(F) + come.astype(F)).astype(HB)
+    return lax.squeeze(parts, (dim,))
+
+
 def scatter_seg(parts):
-    step = 1
-    while step < lax.axis_size("seg"):
-        keep, come = seg_round(parts, step)
-        parts = (keep.astype(F) + come.astype(F)).astype(HB)
-        step *= 2
-    return parts[0]
+    return seg_rest(*seg_round(parts, 1), 1)
 
 
 class Pump:
@@ -787,36 +832,25 @@
         self.rounds = [[(i, i ^ (2 << n)) for i in range(count)] for n in range((count // 2).bit_length() - 1)]
 
     def send(self):
-        self.coming = lax.ppermute(self.values[len(self.done)], "seg", self.rounds[0])
+        self.coming = [lax.ppermute(value, "seg", self.rounds[0]) for value in self.values[len(self.done)]]
 
     def turn(self, other):
         at = len(self.done)
-        if self.coming is None and at < len(self.values):
+        if at == len(self.values):
+            return other
+        if self.coming is None:
             self.values[at] = after(self.values[at], other)
             self.send()
             return self.values[at]
-        if at < len(self.values):
-            value = self.values[at]
-            value = (value.astype(F) + after(self.coming, other).astype(F)).astype(HB)
-            for pairs in self.rounds[1:]:
-                value = (value.astype(F) + lax.ppermute(value, "seg", pairs).astype(F)).astype(HB)
-            self.done.append(value)
-            if at + 1 < len(self.values):
-                self.send()
-            return value
-        return other
-
-
-def direct_exchange(array, cols):
-    ring = Ring(cols)
-    count, order = ring.count, ring.path
-    entry = lambda away: cut(array, ring.owner(away), cols, array.ndim - 1)[None]
-    senders = Ring()
-    out = put(jnp.zeros((count,) + entry(0).shape[1:], array.dtype), entry(0), {0: senders.owner(0)})
-    for away in sorted(range(1, count), key=lambda d: -min(d, count - d)):
-        pairs = [(order[i], order[(i + away) % count]) for i in range(count)]
-        out = put(out, lax.ppermute(entry(away), "seq", pairs), {0: senders.owner(-away)})
-    return out
+        come = after(self.coming, other)
+        sums = [(a.astype(F) + b.astype(F)).astype(HB) for a, b in zip(self.values[at], come)]
+        for pairs in self.rounds[1:]:
+            sums = [(a.astype(F) + lax.ppermute(a, "seg", pairs).astype(F)).astype(HB) for a in sums]
+        self.done.append(sums)
+        if at + 1 < len(self.values):
+            self.values[at + 1] = after(self.values[at + 1], sums)
+            self.send()
+        return sums
 
 
 def exchange_seq(value, split, join):
@@ -841,9 +875,10 @@
 
     low = jnp.pad(low_rank, ((0, 0), (0, 0), (0, PAD - ranks))).transpose(1, 0, 2).reshape(-1, 2 * PAD)
     rank = lax.all_gather(low, ("seg", "seq"), axis=0, tiled=True)
-    mine = direct_exchange(tm_mats[:4], cols)
+    blocks = tm_mats[:4].reshape(4, -1, count, cols).transpose(2, 0, 1, 3)
+    mine = exchange_seq(blocks.reshape(count, -1, cols), 0, 0).reshape(blocks.shape)
     mats = gather_seg(mine)
-    x = gather_seq(tokens, 0, mine)
+    x = gather_seq(tokens, 0, (mine, mats[segs // 2]))
     w_output = lax.all_gather(after(tm_mats[4], x), ("seg", "seq"), axis=0, tiled=True)
     go_cols = exchange_seq(after(out_grad, x), 1, 0)
     part = width // segs
@@ -864,8 +899,14 @@
     ring_cols = Ring(cols)
     z_at = jnp.stack([ring_cols.owner(away).astype(jnp.int32) for away in [a for a, _ in z_held] + [count // 2]])
 
+    joined_mats = jnp.zeros((segs,) + mine.shape, HB)
+    for i, value in enumerate(mats):
+        joined_mats = put(joined_mats, value[None], {0: (lax.axis_index("seg") ^ i).astype(jnp.uint32)})
+    joined_mats = joined_mats.reshape(segs * count, 4, -1, cols)
+    down_t, up_t = rank[:, :PAD].T, rank[:, PAD:].T
+    x_late, joined_mats, down_t, up_t = lax.optimization_barrier((x, joined_mats, down_t, up_t))
     x1, ck, cr, sg, gkv_cols = residual_forward(
-        x, [piece for _, piece in z_held], z_far, z_at, w_output, params, cm_recept, go_cols
+        x_late, [piece for _, piece in z_held], z_far, z_at, w_output, params, cm_recept, go_cols
     )
     gkv = gather_seq(gkv_cols, 1)
     hp = mm(ck, cm_key)
@@ -879,113 +920,97 @@
     bit = seg_bit(1)
     near = [(i, i ^ 1) for i in range(segs)]
 
-    def cm_half(which, ordered):
-        part = lambda a: cut(a, which * np.uint32(a.shape[1] // 2), a.shape[1] // 2, 1)
-        pairs = ((ck, ghp), (hid, gkv), (cr, gsp))
-        return tuple(mm_tn(part(a), b).astype(HB) for a, b in pairs[ordered:])
-
-    cm_come = tuple(lax.ppermute(value, "seg", near) for value in cm_half(np.uint32(1) - bit, 0))
-    cm_kept = cm_half(bit, 0)
-    gsp, ghp, cm_kept = lax.optimization_barrier((gsp, ghp, cm_kept))
+    def cm_half(a, b, which):
+        size = a.shape[1] // 2
+        return mm_tn(cut(a, which * np.uint32(size), size, 1), b).astype(HB)
+
+    def cm_round(a, b):
+        come = lax.ppermute(cm_half(a, b, np.uint32(1) - bit), "seg", near)
+        return cm_half(a, b, bit), come
+
+    cm_add = lambda pair: (pair[0].astype(F) + pair[1].astype(F)).astype(HB)
+    values, keys = cm_add(cm_round(hid, gkv)), cm_add(cm_round(ck, ghp))
+    recept = cm_round(cr, gsp)
+    third, most = keys.shape[0] // 48 * 16, values.shape[0] // 48 * 32
+    pump = Pump([(values[:most],)])
+    token = pump.turn(gsp)
+    gsp, ghp, _ = lax.optimization_barrier((gsp, ghp, (token, keys, recept[0])))
     go_own = put(jnp.zeros((total, width), HB), out_grad, {0: first_row})
 
     def piece_cols(array):
         return lambda start: cut(array, start, cols, 1).astype(F)
 
-    back = lambda part, *carried: residual_backward(
-        x1, go_own, ghp, gsp, cm_key, cm_recept, w_output, params, part, 2, *carried
+    start_row = jnp.zeros((8, width), F)
+    gx1, gz_parts, sums_two, ahead = residual_backward(
+        x1, go_own, ghp, gsp, cm_key, cm_recept, w_output, params, 0, 1, start_row, start_row
     )
-    start_row = jnp.zeros((8, width), F)
-    gx1_late, gz_late, sums_two, ahead = back(0, start_row, start_row)
-    cm_kept = [(a.astype(F) + b.astype(F)).astype(HB) for a, b in zip(cm_kept, after(cm_come, ahead))]
-    pump = Pump([a[i * (a.shape[0] // 2) : (i + 1) * (a.shape[0] // 2)] for a in cm_kept[:2] for i in range(2)] + cm_kept[2:])
-    sent = pump.turn(ahead)
-    late = Scatter(piece_cols(gz_late), cols)
-    sent = (late.hop(), sent)
-    gx1_early, gz_early, sums_two, ahead = back(1, sums_two, after(ahead, sent))
-    token = pump.turn(gz_early)
-    while late.step > 0:
-        sent = late.hop((gz_early, sent))
-    early = Scatter(piece_cols(gz_early), cols)
-    gz_late = late.finish((sent, token))
+    recept = cm_add(after(recept, ahead))
+    pump.values += [(recept,), (keys[:third],), (keys[third : 2 * third],), (keys[2 * third :], values[most:])]
+    ring = Scatter(piece_cols(gz_parts), cols)
+    sent = ring.hop()
+    token = pump.turn(sent)
+    while ring.step > 0:
+        sent = ring.hop(token)
+        token = pump.turn(sent)
+    gz = ring.finish(token)
+    go1_cols = lax.psum_scatter(after(gx1, gz), "seq", scatter_dimension=1, tiled=True)
 
     adj = jnp.zeros((groups, LANES, LANES), F)
     sums = jnp.zeros((8, cols), F)
     outs = ()
-    half = total // 2
     runs = 2
-    run = half // runs
-    wkv = lambda gz, at, adj, sums, outs: wkv_backward(r, k, v, rate, gp, y, gz, vec, states, at, run, adj, sums, outs)
-    sent = early.hop(None)
+    run = total // runs
     for i in range(runs):
-        outs, adj, sums = wkv(gz_late, total - (i + 1) * run, after(adj, sent), sums, outs)
+        outs, adj, sums = wkv_backward(r, k, v, rate, gp, y, gz, vec, states, total - (i + 1) * run, run, adj, sums, outs)
         sent = pump.turn(sums)
-        while early.step > early.hops * (runs - 1 - i) // runs:
-            sent = (early.hop(sums), sent)
-    gz_early = early.finish((sums, sent))
-    go1 = Scatter(piece_cols(jnp.concatenate([gx1_early, gx1_late], axis=0)), cols)
-    first_pieces = go1.piece_of
-    go1.piece_of = lambda owner: after(first_pieces(owner), gz_early)
-    sent = go1.hop()
-    for i in range(runs):
-        outs, adj, sums = wkv(gz_early, half - (i + 1) * run, after(adj, sent), sums, outs)
-        sent = (go1.hop(sums), pump.turn(sums))
+        adj = after(adj, (sent, block_out))
     gr, gk, gv, ggp, grb = outs
-    d_four = jnp.stack([mm_tn(a, b).astype(HB) for a, b in ((x_r, gr), (x_k, gk), (x_v, gv), (x_g, ggp))], axis=1)
-    keep, come = seg_round(d_four.reshape(segs, -1, 4, cols), 1)
+    d_four = jnp.stack([mm_tn(a, b).astype(HB) for a, b in ((x_r, gr), (x_k, gk), (x_v, gv), (x_g, ggp))])
+    keep, come = seg_round(d_four.reshape(4, segs, -1, cols), 1, 1)
     tiles = total // 256
-    splits = (tiles // 4, tiles // 4, tiles // 2)
+    splits = (tiles // 2, tiles // 4, tiles // 4)
 
     def mix(run, grad, given):
         return mix_backward(
-            x, (grad, gk, gv, ggp, grb), t, (gx1_late, gx1_early), mats, rank, params, sums_two, sums,
-            at, tiles - 1 - sum(splits[:run]), splits[run], given,
+            x, (grad, gk, gv, ggp, grb), t, gx1, joined_mats, rank, down_t, up_t, params, sums_two, sums,
+            at, segs, tiles - 1 - sum(splits[:run]), splits[run], given,
         )
 
-    def seg_rest(keep, come, step):
-        parts = (keep.astype(F) + come.astype(F)).astype(HB)
-        while step * 2 < segs:
-            step *= 2
-            keep, come = seg_round(parts, step)
-            parts = (keep.astype(F) + come.astype(F)).astype(HB)
-        return parts[0]
-
+    while len(pump.done) < len(pump.values):
+        sent = pump.turn(sums)
+    (value_a,), (recept,), (key_a,), (key_b,), (key_c, value_b) = pump.done
+    cm_sums = [jnp.concatenate([key_a, key_b, key_c], axis=0), jnp.concatenate([value_a, value_b], axis=0), recept]
+    cm_come = [lax.ppermute(value, "seg", near) for value in cm_sums]
     d_four = (keep.astype(F) + come.astype(F)).astype(HB)
-    keep, come = seg_round(d_four, 2)
+    keep, come = seg_round(d_four, 2, 1)
     gr, _ = lax.optimization_barrier((gr, (sent, keep)))
     out, ahead, packed = mix(0, gr, ())
-    while go1.step > 0:
-        sent = go1.hop(ahead)
-    sent = (sent, pump.turn(ahead))
-    d_four = seg_rest(keep, after(come, sent), 2)
-    d_four = exchange_seq(d_four.reshape(count, -1, 4, cols).transpose(0, 2, 1, 3).reshape(count, -1, cols), 0, 0)
-    out, ahead, packed = mix(1, gr, (out, after(ahead, (sent, keep)), packed))
-    while len(pump.done) < len(pump.values):
-        token = pump.turn(ahead)
-    cm_sums = [jnp.concatenate(pump.done[i : i + 2], axis=0) for i in (0, 2)] + pump.done[4:]
-    cm_come = [lax.ppermute(value, "seg", near) for value in cm_sums]
-    go1_cols = go1.finish(ahead).astype(HB)
-    z = assembled(z_held, z_far, 1)
-    d_out = mm_tn(z, go1_cols).astype(HB).reshape(segs, -1, cols)
+    d_four = seg_rest(keep, after(come, ahead), 2, 1)
+    d_four = exchange_seq(d_four.reshape(4, count, -1, cols).transpose(1, 0, 2, 3).reshape(count, -1, cols), 0, 0)
+    go1_cols = after(go1_cols, ahead)
+    d_out = outer_parts([piece for _, piece in z_held], z_far, z_at, go1_cols, width).reshape(segs, -1, cols)
     keep, come = seg_round(d_out, 1)
     d_out = (keep.astype(F) + come.astype(F)).astype(HB)
     keep, come = seg_round(d_out, 2)
-    ahead, d_four, cm_sums = after((ahead, d_four, cm_sums), keep)
-    out, _, _, packed = mix(2, gr, (out, ahead, packed))
-    d_out = exchange_seq(seg_rest(keep, after(come, packed), 2).reshape(count, -1, cols), 0, 0)
+    cm_come = after(cm_come, ahead)
+    out, ahead, packed = mix(1, gr, (out, after(ahead, (keep, cm_come)), packed))
+    d_out = exchange_seq(seg_rest(keep, after(come, ahead), 2).reshape(count, -1, cols), 0, 0)
+    out, _, _, packed = mix(2, gr, (out, after(ahead, d_four), packed))
+    d_out = after(d_out, packed)
 
     def joined(blocks, mats_in):
         return blocks.reshape(count, mats_in, -1, cols).transpose(1, 2, 0, 3).reshape(mats_in, -1, width).astype(F)
 
     d_mats = jnp.concatenate([joined(d_four, 4), joined(d_out, 1)], axis=0)
-    cm_grads = tuple(
-        jnp.where(bit == 0, jnp.concatenate([a, b], axis=0), jnp.concatenate([b, a], axis=0)).astype(F)
-        for a, b in zip(cm_sums, after(cm_come, packed))
-    )
-
     rest = scatter_seg(packed).T
     final = Scatter(lambda start: cut(out, start, rows, 0).astype(F), rows)
     final.hop()
+    which = bit.astype(jnp.int32).reshape(1)
+    cm_grads = []
+    for a, b in zip(cm_sums, cm_come):
+        cm_grads.append(join_halves(after(a, packed), b, which))
+        if final.step > 0:
+            final.hop(cm_grads[-1])
     rest = exchange_seq(rest.reshape(count, -1, 2 * PAD), 0, 0).astype(F)
     input_grad = final.finish()
     rest = jnp.sum(rest, axis=0)

time: 786 us -> 720 us (0.916)
  other arithmetic: 86.1 us -> 55.3 us
  starting transfers between devices: 126 us -> 110 us
  local copies, waits for them, and re-layouts: 82.7 us -> 68.3 us
  matrix products: 43.2 us -> 35.3 us
    all_to_all x5 -> x6, waiting for transfers between devices: 6.98 us -> 35.1 us  [exchange_seq(): lax.all_to_all(value, 'seq', split_axis=split, concat_axis=join, tiled=True)]
    ppermute x15 -> x9, starting transfers between devices: 31.6 us -> 5.36 us  [the longest x6 5.21 us: send(): lax.ppermute(value, 'seg', self.rounds[0])]
    convert_element_type x14 -> x9, other arithmetic: 38.7 us -> 13.1 us  [the longest x6 9.43 us: turn(): (a.astype(F) + b.astype(F)).astype(HB)]
    ppermute x3, waiting for transfers between devices: 22 us -> 0.01 us  [gather_seg(): lax.ppermute(value, 'seg', pairs)]
    ppermute x20 -> x12, waiting for transfers between devices: 20.4 us -> 4.09 us  [hop(): lax.ppermute(sent[1], 'seq', self.left)]
    ppermute x20 -> x12, starting transfers between devices: 27.4 us -> 11.3 us  [hop(): lax.ppermute(sent[0], 'seq', self.right)]
    pallas_call x3 -> x7, Pallas kernels: 74.7 us -> 90.6 us  [the longest x3 66.2 us: mix_backward(): pl.pallas_call(functools.partial(mix_backward_body, not given, closes), g...]
    ppermute x3, starting transfers between devices: 3.29 us -> 15.9 us  [ring_hops(): lax.ppermute(going_left[half:], 'seq', ring.left)]
  transfers between devices with their start and end apart: 98 -> 78, of which waited for: 41 -> 35; matrix products, arithmetic and copies ran while one was open for 23% -> 19% of each run, Pallas kernels for 25% -> 27%
where the time goes in v3:
time: 720 us; the launch traced here: 709 us
  Pallas kernels  234 us (32%)
  waiting for transfers between devices  182 us (25%)
  starting transfers between devices  110 us (15%)
  local copies, waits for them, and re-layouts  68.3 us (9%)
  other arithmetic  55.3 us (8%)
  matrix products  35.3 us (5%)
  between operations  24.6 us (3%)
    ppermute x9, waiting for transfers between devices, ring_hops(): going_right = lax.ppermute(going_right, 'seq', ring.right)  74.6 us
    pallas_call x3, Pallas kernels, mix_backward(): pl.pallas_call(functools.partial(mix_backward_body, not given, closes), g...  66.2 us
    ppermute x12, waiting for transfers between devices, hop(): lax.ppermute(sent[0], 'seq', self.right)  42.8 us
    pallas_call x2, Pallas kernels, wkv_backward(): pl.pallas_call(functools.partial(bwd_body, groups, nb), grid=(steps,), in...  41.8 us
    all_to_all x6, waiting for transfers between devices, exchange_seq(): lax.all_to_all(value, 'seq', split_axis=split, concat_axis=join, tiled=True)  35.1 us
    pallas_call x1, Pallas kernels, residual_backward(): pl.pallas_call(functools.partial(residual_backward_body, part == parts -...  32 us
    all_to_all x6, starting transfers between devices, exchange_seq(): lax.all_to_all(value, 'seq', split_axis=split, concat_axis=join, tiled=True)  28.1 us
    pallas_call x1, Pallas kernels, mix_forward(): pl.pallas_call(functools.partial(mix_forward_body, len(mats)), grid=(tota...  25.7 us
  transfers between devices with their start and end apart: 78, of which 35 were waited for; matrix products, arithmetic and copies ran while one was open for 19% of the time, Pallas kernels for 27%

profile of v3, /device:TPU:0, one launch (start us, length us, event | category | flops | bytes accessed | tf_op | source)
XLA Modules:
  0.0 709.4 jit_solution(8956107167099367112)
XLA Ops:
  10.2 7.3 %all-to-all-start = ((bf16[8,256,256]{2,1,0:T(8,128)(2,1)}), bf16[8,256,256]{2,1,0:T(8,128)(2,1)S(1)}, u32[]{:S(2)}, u32[]{:S(2)}) async-start(bf16[8,256,256]{2,1,0:T(8,128)(2,1)} %bitcast.2), calls=%async_computation | async-start | bytes 2097152 | tf_op jit(solution)/shard_map/all_to_all | solution.py:857
  21.0 24.9 %all-to-all-done = bf16[8,256,256]{2,1,0:T(8,128)(2,1)S(1)} async-done(((bf16[8,256,256]{2,1,0:T(8,128)(2,1)}), bf16[8,256,256]{2,1,0:T(8,128)(2,1)S(1)}, u32[]{:S(2)}, u32[]{:S(2)}) %all-to-all-start) | async-done | bytes 1048608 | tf_op jit(solution)/shard_map/all_to_all | solution.py:857
  50.7 6.7 collective-permute-start.3
  77.4 10.4 %collective-permute-done.5 = bf16[128,2048]{1,0:T(8,128)(2,1)S(1)} collective-permute-done((bf16[128,2048]{1,0:T(8,128)(2,1)}, bf16[128,2048]{1,0:T(8,128)(2,1)S(1)}, u32[]{:S(2)}, u32[]{:S(2)}) %collective-permute-start.5) | collective-permute-done | bytes 524320 | tf_op jit(solution)/shard_map/ppermute | solution.py:715
  105.9 25.7 %mix_forward.1 = (bf16[1024,256]{1,0:T(8,128)(2,1)}, bf16[1024,256]{1,0:T(8,128)(2,1)}, bf16[1024,256]{1,0:T(8,128)(2,1)}, f32[1024,256]{1,0:T(8,128)}, f32[1024...) custom-call(bf16[1024,2048]{1,0:T(8,128)(2,1)} %constant_dynamic-upd, ...), custom_call_target="tpu_custom_call" | custom-call | flops 28730982400 | bytes 25165824 | tf_op jit(solution)/shard_map/mix_forward/pallas_call | solution.py:397
  131.6 21.7 %wkv_forward.1 = (bf16[1024,256]{1,0:T(8,128)(2,1)}, f32[1024,256]{1,0:T(8,128)}, bf16[64,2,128,128]{3,2,1,0:T(8,128)(2,1)}) custom-call(bf16[1024,256]{1,0:T(8,128)(2,1)} %get-tuple-element.117.r_ref, bf16[1024,256]{1,0:T(8,128)(2,1)} %get-tuple-element.118.k_ref, bf16[1024,256]{1,0:T(8,128)(2,1)} %get-tuple-element.119.v_ref, ...), custom_call_target="tpu_custom_call" | custom-call | flops 24903680000 | bytes 10485760 | tf_op jit(solution)/shard_map/wkv_forward/pallas_call | solution.py:145
  155.4 30.6 %collective-permute-done.11.rest_1_ = bf16[1024,256]{1,0:T(8,128)(2,1)S(1)} collective-permute-done((bf16[1024,256]{1,0:T(8,128)(2,1)}, bf16[1024,256]{1,0:T(8,128)(2,1)S(1)}, u32[]{:S(2)}, u32[]{:S(2)}) %collective-permute-start.11) | collective-permute-done | bytes 524320 | tf_op jit(solution)/shard_map/ppermute | solution.py:715
  206.5 6.3 collective-permute-done.15.rest_5_
  215.2 13.9 %collective-permute-start.18 = (bf16[512,256]{1,0:T(8,128)(2,1)}, bf16[512,256]{1,0:T(8,128)(2,1)}, u32[]{:S(2)}, u32[]{:S(2)}) collective-permute-start(bf16[512,256]{1,0:T(8,128)(2,1)} %slice.401), channel_id=1, source_target_pairs={{3,1},{5,3},{7,5},{6,7},{4,6},{2,4},{0,2},{1,0},{11,9},{13,11},{15... | collective-permute-start | bytes 786440 | tf_op jit(solution)/shard_map/ppermute | solution.py:720
  234.3 22.2 %residual_forward.1 = (f32[1024,2048]{1,0:T(8,128)}, bf16[1024,2048]{1,0:T(8,128)(2,1)}, bf16[1024,2048]{1,0:T(8,128)(2,1)}, f32[1024,256]{1,0:T(8,128)}, bf16[1024,256]{1,0:T(8,128)(2,1)}) custom-call(bf16[1024,2048]{1,0:T(8,128)(2,1)} %constant_dynamic-update-slice_fusion.10.x_ref.before_ref, bf16[2048,2048]{1,0:T(8,128)(2,1)} %all-gather.5.cloned.1.call-done.w_ref, ...), custom_call_target="tpu_custom_call" | custom-call | flops 25165824000 | bytes 25165824 | tf_op jit(solution)/shard_map/residual_forward/pallas_call | solution.py:444
  258.7 10.3 %collective-permute-done.19 = bf16[1024,256]{1,0:T(8,128)(2,1)S(1)} collective-permute-done((bf16[1024,256]{1,0:T(8,128)(2,1)}, bf16[1024,256]{1,0:T(8,128)(2,1)S(1)}, u32[]{:S(2)}, u32[]{:S(2)}) %collective-permute-start.19) | collective-permute-done | bytes 524320 | tf_op jit(solution)/shard_map/ppermute | solution.py:715
  271.0 9.8 %collective-permute-done.21 = bf16[1024,256]{1,0:T(8,128)(2,1)} collective-permute-done((bf16[1024,256]{1,0:T(8,128)(2,1)S(1)}, bf16[1024,256]{1,0:T(8,128)(2,1)}, u32[]{:S(2)}, u32[]{:S(2)}) %collective-permute-start.21) | collective-permute-done | bytes 524320 | tf_op jit(solution)/shard_map/ppermute | solution.py:715
  288.3 4.7 collective-permute-done.23
  308.7 4.6 multiply_convert_fusion
  317.7 6.0 collective-permute-done.27
  328.6 5.0 collective-permute-done.28
  339.9 4.7 collective-permute-done.29
  366.0 32.0 %residual_backward.1 = (bf16[1024,2048]{1,0:T(8,128)(2,1)}, bf16[1024,2048]{1,0:T(8,128)(2,1)}, f32[8,2048]{1,0:T(8,128)}, f32[8,2048]{1,0:T(8,128)}) custom-call(f32[1024,2048]{1,0:T(8,128)} %get-tuple-element.123.x1_ref.before_ref, f32[1024,2048]{1,0:T(8,128)} %get-tuple-element.123.x1_ref.before_ref, ...), custom_call_target="tpu_custom_call" | custom-call | flops 36700160000 | bytes 25165824 | tf_op jit(solution)/shard_map/residual_backward/pallas_call | solution.py:501
  416.6 7.1 %collective-permute-done.43 = bf16[1024,256]{1,0:T(8,128)(2,1)S(1)} collective-permute-done((bf16[1024,256]{1,0:T(8,128)(2,1)S(1)}, bf16[1024,256]{1,0:T(8,128)(2,1)S(1)}, u32[]{:S(2)}, u32[]{:S(2)}) %collective-permute-start.43) | collective-permute-done | bytes 524320 | tf_op jit(solution)/shard_map/ppermute | solution.py:835
  442.0 5.2 collective-permute-done.44
  466.6 21.1 %wkv_backward.2 = (bf16[1024,256]{1,0:T(8,128)(2,1)}, bf16[1024,256]{1,0:T(8,128)(2,1)}, bf16[1024,256]{1,0:T(8,128)(2,1)}, bf16[1024,256]{1,0:T(8,128)(2,1)}, b...) custom-call(bf16[1024,256]{1,0:T(8,128)(2,1)} %get-tuple-element.117.r_ref, ...), custom_call_target="tpu_custom_call" | custom-call | flops 24117248000 | bytes 7864320 | tf_op jit(solution)/shard_map/wkv_backward/pallas_call | solution.py:294
  490.9 20.7 %wkv_backward.3 = (bf16[1024,256]{1,0:T(8,128)(2,1)}, bf16[1024,256]{1,0:T(8,128)(2,1)}, bf16[1024,256]{1,0:T(8,128)(2,1)}, bf16[1024,256]{1,0:T(8,128)(2,1)}, b...) custom-call(bf16[1024,256]{1,0:T(8,128)(2,1)} %get-tuple-element.117, ...), custom_call_target="tpu_custom_call", output_to_operand_aliasing={{0}: (11, {}), {1}: (12, {}), {2}: (13, {}), {3}: (14, {}),... | custom-call | flops 24117248000 | bytes 7864320 | tf_op jit(solution)/shard_map/wkv_backward/pallas_call | solution.py:294
  531.8 28.5 %mix_backward.3 = (bf16[1024,2048]{1,0:T(8,128)(2,1)}, f32[8,2048]{1,0:T(8,128)}, f32[512,2048]{1,0:T(8,128)}) custom-call(bf16[1024,2048]{1,0:T(8,128)(2,1)} %constant_dynamic-update-slice_fusion.10.x_ref.before_ref, bf16[1024,2048]{1,0:T(8,128)(2,1)} %constant_dynamic-update-slice_fusion.10.x_ref.before_ref, bf16[1024,256]{1,0:T(8,128)(2,1)} %get-tuple-element.173.gr_ref, ...), custom_call_target="tpu_custom_call" | custom-call | flops 36700160000 | bytes 10485760 | tf_op jit(solution)/shard_map/mix_backward/pallas_call | solution.py:601
  569.5 4.9 all-to-all-start.3
  576.3 18.4 %mix_backward.4 = (bf16[1024,2048]{1,0:T(8,128)(2,1)}, f32[8,2048]{1,0:T(8,128)}, f32[512,2048]{1,0:T(8,128)}) custom-call(bf16[1024,2048]{1,0:T(8,128)(2,1)} %constant_dynamic-update-slice_fusion.10.x_ref.before_ref, bf16[1024,2048]{1,0:T(8,128)(2,1)} %constant_dynamic-update-slice_fusion.10.x_ref.before_ref, ...), custom_call_target="tpu_custom_call", output_to_operand_aliasing={{0}: (17, {})} | custom-call | flops 18350080000 | bytes 5242880 | tf_op jit(solution)/shard_map/mix_backward/pallas_call | solution.py:601
  594.7 5.7 all-to-all-done.3
  600.4 19.2 %mix_backward.5 = (bf16[1024,2048]{1,0:T(8,128)(2,1)}, f32[8,2048]{1,0:T(8,128)}, f32[512,2048]{1,0:T(8,128)}, bf16[4,512,512]{2,1,0:T(8,128)(2,1)}) custom-call(bf16[1024,2048]{1,0:T(8,128)(2,1)} %constant_dynamic-update-slice_fusion.10.x_ref.before_ref, ...), custom_call_target="tpu_custom_call", output_to_operand_aliasing={{0}: (17, {})} | custom-call | flops 18350080000 | bytes 5242880 | tf_op jit(solution)/shard_map/mix_backward/pallas_call | solution.py:601
  626.8 7.2 %join_halves.3 = f32[2048,896]{1,0:T(8,128)} custom-call(s32[1]{0:T(128)} %bitcast.60.bit_ref, bf16[1024,896]{1,0:T(8,128)(2,1)} %pad_maximum_fusion.1.mine_ref, bf16[1024,896]{1,0:T(8,128)(2,1)} %collective-permute-done.54.other_ref), custom_call_target="tpu_custom_call" | custom-call | bytes 11010048 | tf_op jit(solution)/shard_map/join_halves/pallas_call | solution.py:651
  641.4 5.5 join_halves.5
  646.9 7.1 %join_halves.4 = f32[896,2048]{1,0:T(8,128)} custom-call(s32[1]{0:T(128)} %bitcast.60.bit_ref, bf16[448,2048]{1,0:T(8,128)(2,1)} %pad_maximum_fusion.2.mine_ref, bf16[448,2048]{1,0:T(8,128)(2,1)} %collective-permute-done.55.other_ref), custom_call_target="tpu_custom_call" | custom-call | bytes 11010048 | tf_op jit(solution)/shard_map/join_halves/pallas_call | solution.py:651
  666.5 6.1 collective-permute-done.62
  684.9 6.7 collective-permute-done.64
  (374 shorter events, 274.4 us)
Async XLA Ops:
  10.2 35.7 %all-to-all-start = ((bf16[8,256,256]{2,1,0:T(8,128)(2,1)}), bf16[8,256,256]{2,1,0:T(8,128)(2,1)S(1)}, u32[]{:S(2)}, u32[]{:S(2)}) async-start(bf16[8,256,256]{2,1,0:T(8,128)(2,1)} %bitcast.2), calls=%async_computation | async-start | bytes 2097152 | tf_op jit(solution)/shard_map/all_to_all | solution.py:857
  17.4 88.5 %all-gather.3.cloned.1.call-start = ((), (), s32[]{:S(2)}) async-start(), calls=%async_computation.7 | async-start | bytes 2162688 | tf_op jit(solution)/shard_map/all_gather | solution.py:877
  18.2 216.2 %all-gather.5.cloned.1.call-start = ((), (), s32[]{:S(2)}) async-start(), calls=%async_computation.8 | async-start | bytes 8650752 | tf_op jit(solution)/shard_map/all_gather | solution.py:882
  18.2 31.2 %collective-permute-start = (bf16[128,2048]{1,0:T(8,128)(2,1)S(1)}, bf16[128,2048]{1,0:T(8,128)(2,1)}, u32[]{:S(2)}, u32[]{:S(2)}) collective-permute-start(bf16[128,2048]{1,0:T(8,128)(2,1)S(1)} %copy-done.25), channel_id=1, source_target_pairs={{1,3},{3,5},{5,7},{7,6},{6,4},{4,2},{2,0},{0,1},{9,11},{11,13},{13... | collective-permute-start | bytes 1572872 | tf_op jit(solution)/shard_map/ppermute | solution.py:715
  20.3 29.1 %collective-permute-start.1 = (bf16[128,2048]{1,0:T(8,128)(2,1)S(1)}, bf16[128,2048]{1,0:T(8,128)(2,1)S(1)}, u32[]{:S(2)}, u32[]{:S(2)}) collective-permute-start(bf16[128,2048]{1,0:T(8,128)(2,1)S(1)} %copy-done.25), channel_id=1, source_target_pairs={{3,1},{5,3},{7,5},{6,7},{4,6},{2,4},{0,2},{1,0},{11,9},{13,11},{15... | collective-permute-start | bytes 1572872 | tf_op jit(solution)/shard_map/ppermute | solution.py:716
  45.9 24.0 %collective-permute-start.4 = (bf16[8,4,64,256]{3,2,1,0:T(8,128)(2,1)S(1)}, bf16[8,4,64,256]{3,2,1,0:T(8,128)(2,1)}, u32[]{:S(2)}, u32[]{:S(2)}) collective-permute-start(bf16[8,4,64,256]{3,2,1,0:T(8,128)(2,1)S(1)} %bitcast.150), channel_id=1, source_target_pairs={{0,16},{8,24},{16,0},{24,8},{1,17},{9,25},{17,1},{25,9},{2,18},{10... | collective-permute-start | bytes 3145736 | tf_op jit(solution)/shard_map/ppermute | solution.py:796
  49.4 20.5 %collective-permute-start.2 = (bf16[128,2048]{1,0:T(8,128)(2,1)}, bf16[128,2048]{1,0:T(8,128)(2,1)}, u32[]{:S(2)}, u32[]{:S(2)}) collective-permute-start(bf16[128,2048]{1,0:T(8,128)(2,1)} %collective-permute-done), channel_id=1, source_target_pairs={{1,3},{3,5},{5,7},{7,6},{6,4},{4,2},{2,0},{0,1},{9,11},{11,13},{13... | collective-permute-start | bytes 1572872 | tf_op jit(solution)/shard_map/ppermute | solution.py:715
  50.7 19.2 %collective-permute-start.3 = (bf16[128,2048]{1,0:T(8,128)(2,1)S(1)}, bf16[128,2048]{1,0:T(8,128)(2,1)}, u32[]{:S(2)}, u32[]{:S(2)}) collective-permute-start(bf16[128,2048]{1,0:T(8,128)(2,1)S(1)} %collective-permute-done.1), channel_id=1, source_target_pairs={{3,1},{5,3},{7,5},{6,7},{4,6},{2,4},{0,2},{1,0},{11,9},{13,11},{15... | collective-permute-start | bytes 1572872 | tf_op jit(solution)/shard_map/ppermute | solution.py:716
  69.9 17.9 %collective-permute-start.5 = (bf16[128,2048]{1,0:T(8,128)(2,1)}, bf16[128,2048]{1,0:T(8,128)(2,1)S(1)}, u32[]{:S(2)}, u32[]{:S(2)}) collective-permute-start(bf16[128,2048]{1,0:T(8,128)(2,1)} %collective-permute-done.2), channel_id=1, source_target_pairs={{1,3},{3,5},{5,7},{7,6},{6,4},{4,2},{2,0},{0,1},{9,11},{11,13},{13... | collective-permute-start | bytes 1572872 | tf_op jit(solution)/shard_map/ppermute | solution.py:715
  101.8 29.8 %all-to-all-start.1 = ((bf16[128,8,256]{2,0,1:T(8,128)(2,1)}), bf16[128,8,256]{2,0,1:T(8,128)(2,1)S(1)}, u32[]{:S(2)}, u32[]{:S(2)}) async-start(bf16[128,8,256]{2,0,1:T(8,128)(2,1)} %bitcast.146), calls=%async_computation.1 | async-start | bytes 1048576 | tf_op jit(solution)/shard_map/all_to_all | solution.py:857
  153.3 32.7 %collective-permute-start.11 = (bf16[1024,256]{1,0:T(8,128)(2,1)}, bf16[1024,256]{1,0:T(8,128)(2,1)S(1)}, u32[]{:S(2)}, u32[]{:S(2)}) collective-permute-start(bf16[1024,256]{1,0:T(8,128)(2,1)} %get-tuple-element.122.rest_0_), channel_id=1, source_target_pairs={{1,3},{3,5},{5,7},{7,6},{6,4},{4,2},{2,0},{0,1},{9,11},{11,13},{13... | collective-permute-start | bytes 1572872 | tf_op jit(solution)/shard_map/ppermute | solution.py:715
  155.4 30.7 %collective-permute-start.12 = (bf16[1024,256]{1,0:T(8,128)(2,1)}, bf16[1024,256]{1,0:T(8,128)(2,1)S(1)}, u32[]{:S(2)}, u32[]{:S(2)}) collective-permute-start(bf16[1024,256]{1,0:T(8,128)(2,1)} %get-tuple-element.122.rest_0_), channel_id=1, source_target_pairs={{3,1},{5,3},{7,5},{6,7},{4,6},{2,4},{0,2},{1,0},{11,9},{13,11},{15... | collective-permute-start | bytes 1572872 | tf_op jit(solution)/shard_map/ppermute | solution.py:716
  213.6 18.5 %collective-permute-start.17 = (bf16[512,256]{1,0:T(8,128)(2,1)}, bf16[512,256]{1,0:T(8,128)(2,1)S(1)}, u32[]{:S(2)}, u32[]{:S(2)}) collective-permute-start(bf16[512,256]{1,0:T(8,128)(2,1)} %slice.400), channel_id=1, source_target_pairs={{1,3},{3,5},{5,7},{7,6},{6,4},{4,2},{2,0},{0,1},{9,11},{11,13},{13... | collective-permute-start | bytes 786440 | tf_op jit(solution)/shard_map/ppermute | solution.py:720
  215.2 19.2 %collective-permute-start.18 = (bf16[512,256]{1,0:T(8,128)(2,1)}, bf16[512,256]{1,0:T(8,128)(2,1)}, u32[]{:S(2)}, u32[]{:S(2)}) collective-permute-start(bf16[512,256]{1,0:T(8,128)(2,1)} %slice.401), channel_id=1, source_target_pairs={{3,1},{5,3},{7,5},{6,7},{4,6},{2,4},{0,2},{1,0},{11,9},{13,11},{15... | collective-permute-start | bytes 786440 | tf_op jit(solution)/shard_map/ppermute | solution.py:720
  328.5 35.2 %collective-permute-start.36 = (bf16[1024,896]{1,0:T(8,128)(2,1)S(1)}, bf16[1024,896]{1,0:T(8,128)(2,1)S(1)}, u32[]{:S(2)}, u32[]{:S(2)}) collective-permute-start(bf16[1024,896]{1,0:T(8,128)(2,1)S(1)} %fusion.10), channel_id=1, source_target_pairs={{0,8},{8,0},{16,24},{24,16},{1,9},{9,1},{17,25},{25,17},{2,10},{10... | collective-permute-start | bytes 5505032 | tf_op jit(solution)/shard_map/ppermute | solution.py:928
  339.9 19.8 %collective-permute-start.35 = (bf16[448,2048]{1,0:T(8,128)(2,1)S(1)}, bf16[448,2048]{1,0:T(8,128)(2,1)S(1)}, u32[]{:S(2)}, u32[]{:S(2)}) collective-permute-start(bf16[448,2048]{1,0:T(8,128)(2,1)S(1)} %convolution_convert_fusion), channel_id=1, source_target_pairs={{0,8},{8,0},{16,24},{24,16},{1,9},{9,1},{17,25},{25,17},{2,10},{10... | collective-permute-start | bytes 5505032 | tf_op jit(solution)/shard_map/ppermute | solution.py:928
  359.6 46.9 %collective-permute-start.42 = (bf16[1024,256]{1,0:T(8,128)(2,1)}, bf16[1024,256]{1,0:T(8,128)(2,1)}, u32[]{:S(2)}, u32[]{:S(2)}) collective-permute-start(bf16[1024,256]{1,0:T(8,128)(2,1)} %fusion.21), channel_id=1, source_target_pairs={{0,8},{8,0},{16,24},{24,16},{1,9},{9,1},{17,25},{25,17},{2,10},{10... | collective-permute-start | bytes 1572872 | tf_op jit(solution)/shard_map/ppermute | solution.py:928
  360.5 47.4 %collective-permute-start.39 = (bf16[288,2048]{1,0:T(8,128)(2,1)S(1)}, bf16[288,2048]{1,0:T(8,128)(2,1)}, u32[]{:S(2)}, u32[]{:S(2)}) collective-permute-start(bf16[288,2048]{1,0:T(8,128)(2,1)S(1)} %slice.410), channel_id=1, source_target_pairs={{0,16},{8,24},{16,0},{24,8},{1,17},{9,25},{17,1},{25,9},{2,18},{10... | collective-permute-start | bytes 3538952 | tf_op jit(solution)/shard_map/ppermute | solution.py:835
  402.3 33.3 %all-to-all-start.2 = ((bf16[8,128,256]{2,1,0:T(8,128)(2,1)}), bf16[8,128,256]{2,1,0:T(8,128)(2,1)}, u32[]{:S(2)}, u32[]{:S(2)}) async-start(bf16[8,128,256]{2,1,0:T(8,128)(2,1)} %bitcast.46), calls=%async_computation.2 | async-start | bytes 1048576 | tf_op jit(solution)/shard_map/all_to_all | solution.py:857
  406.5 153.8 %reduce-scatter.2.cloned.1.call-start = ((), (), s32[]{:S(2)}) async-start(), calls=%async_computation.9 | async-start | bytes 4718592 | tf_op jit(solution)/shard_map/reduce_scatter | solution.py:956
  456.0 31.8 %collective-permute-start.51 = (bf16[160,2048]{1,0:T(8,128)(2,1)S(1)}, bf16[160,2048]{1,0:T(8,128)(2,1)S(1)}, u32[]{:S(2)}, u32[]{:S(2)}) collective-permute-start(bf16[160,2048]{1,0:T(8,128)(2,1)S(1)} %copy-done.7), channel_id=1, source_target_pairs={{0,16},{8,24},{16,0},{24,8},{1,17},{9,25},{17,1},{25,9},{2,18},{10... | collective-permute-start | bytes 1966088 | tf_op jit(solution)/shard_map/ppermute | solution.py:835
  456.4 31.3 %collective-permute-start.50 = (bf16[352,896]{1,0:T(8,128)(2,1)S(1)}, bf16[352,896]{1,0:T(8,128)(2,1)}, u32[]{:S(2)}, u32[]{:S(2)}) collective-permute-start(bf16[352,896]{1,0:T(8,128)(2,1)S(1)} %copy-done.9), channel_id=1, source_target_pairs={{0,16},{8,24},{16,0},{24,8},{1,17},{9,25},{17,1},{25,9},{2,18},{10... | collective-permute-start | bytes 1892360 | tf_op jit(solution)/shard_map/ppermute | solution.py:835
  523.9 42.9 %collective-permute-start.56 = (bf16[1024,256]{1,0:T(8,128)(2,1)}, bf16[1024,256]{1,0:T(8,128)(2,1)}, u32[]{:S(2)}, u32[]{:S(2)}) collective-permute-start(bf16[1024,256]{1,0:T(8,128)(2,1)} %add_convert_fusion.17.mine_ref), channel_id=1, source_target_pairs={{0,8},{8,0},{16,24},{24,16},{1,9},{9,1},{17,25},{25,17},{2,10},{10... | collective-permute-start | bytes 1572872 | tf_op jit(solution)/shard_map/ppermute | solution.py:983
  527.0 39.8 %collective-permute-start.55 = (bf16[448,2048]{1,0:T(8,128)(2,1)}, bf16[448,2048]{1,0:T(8,128)(2,1)}, u32[]{:S(2)}, u32[]{:S(2)}) collective-permute-start(bf16[448,2048]{1,0:T(8,128)(2,1)} %pad_maximum_fusion.2.mine_ref), channel_id=1, source_target_pairs={{0,8},{8,0},{16,24},{24,16},{1,9},{9,1},{17,25},{25,17},{2,10},{10... | collective-permute-start | bytes 5505032 | tf_op jit(solution)/shard_map/ppermute | solution.py:983
  528.5 38.3 %collective-permute-start.54 = (bf16[1024,896]{1,0:T(8,128)(2,1)}, bf16[1024,896]{1,0:T(8,128)(2,1)}, u32[]{:S(2)}, u32[]{:S(2)}) collective-permute-start(bf16[1024,896]{1,0:T(8,128)(2,1)} %pad_maximum_fusion.1.mine_ref), channel_id=1, source_target_pairs={{0,8},{8,0},{16,24},{24,16},{1,9},{9,1},{17,25},{25,17},{2,10},{10... | collective-permute-start | bytes 5505032 | tf_op jit(solution)/shard_map/ppermute | solution.py:983
  531.1 35.7 %collective-permute-start.57 = (bf16[4,1,512,256]{3,2,0,1:T(8,128)(2,1)S(1)}, bf16[4,1,512,256]{3,2,0,1:T(8,128)(2,1)}, u32[]{:S(2)}, u32[]{:S(2)}) collective-permute-start(bf16[4,1,512,256]{3,2,0,1:T(8,128)(2,1)S(1)} %get-tuple-element.274), channel_id=1, source_target_pairs={{0,16},{8,24},{16,0},{24,8},{1,17},{9,25},{17,1},{25,9},{2,18},{10... | collective-permute-start | bytes 3145736 | tf_op jit(solution)/shard_map/ppermute | solution.py:812
  569.5 30.9 %all-to-all-start.3 = ((bf16[8,256,256]{2,1,0:T(8,128)(2,1)}), bf16[8,256,256]{2,1,0:T(8,128)(2,1)S(1)}, u32[]{:S(2)}, u32[]{:S(2)}) async-start(bf16[8,256,256]{2,1,0:T(8,128)(2,1)} %bitcast.59), calls=%async_computation.4 | async-start | bytes 2097152 | tf_op jit(solution)/shard_map/all_to_all | solution.py:857
  626.8 32.2 %collective-permute-start.67 = (bf16[2,512,512]{1,2,0:T(8,128)(2,1)}, bf16[2,512,512]{1,2,0:T(8,128)(2,1)}, u32[]{:S(2)}, u32[]{:S(2)}) collective-permute-start(bf16[2,512,512]{1,2,0:T(8,128)(2,1)} %bitcast.172), channel_id=1, source_target_pairs={{0,8},{8,0},{16,24},{24,16},{1,9},{9,1},{17,25},{25,17},{2,10},{10... | collective-permute-start | bytes 3145736 | tf_op jit(solution)/shard_map/ppermute | solution.py:812
  636.3 17.8 %collective-permute-start.61 = (bf16[128,2048]{1,0:T(8,128)(2,1)}, bf16[128,2048]{1,0:T(8,128)(2,1)}, u32[]{:S(2)}, u32[]{:S(2)}) collective-permute-start(bf16[128,2048]{1,0:T(8,128)(2,1)} %pad_maximum_fusion.8), channel_id=1, source_target_pairs={{3,1},{5,3},{7,5},{6,7},{4,6},{2,4},{0,2},{1,0},{11,9},{13,11},{15... | collective-permute-start | bytes 1572872 | tf_op jit(solution)/shard_map/ppermute | solution.py:775
  637.1 17.0 %collective-permute-start.60 = (bf16[128,2048]{1,0:T(8,128)(2,1)}, bf16[128,2048]{1,0:T(8,128)(2,1)}, u32[]{:S(2)}, u32[]{:S(2)}) collective-permute-start(bf16[128,2048]{1,0:T(8,128)(2,1)} %pad_maximum_fusion.7), channel_id=1, source_target_pairs={{1,3},{3,5},{5,7},{7,6},{6,4},{4,2},{2,0},{0,1},{9,11},{11,13},{13... | collective-permute-start | bytes 1572872 | tf_op jit(solution)/shard_map/ppermute | solution.py:775
  660.6 17.3 %collective-permute-start.68 = (bf16[1,512,512]{1,2,0:T(8,128)(2,1)S(1)}, bf16[1,512,512]{1,2,0:T(8,128)(2,1)S(1)}, u32[]{:S(2)}, u32[]{:S(2)}) collective-permute-start(bf16[1,512,512]{1,2,0:T(8,128)(2,1)S(1)} %constant_dynamic-slice_fusion.15), channel_id=1, source_target_pairs={{0,16},{8,24},{16,0},{24,8},{1,17},{9,25},{17,1},{25,9},{2,18},{10... | collective-permute-start | bytes 1572872 | tf_op jit(solution)/shard_map/ppermute | solution.py:812
  678.9 19.8 %all-to-all-start.5 = ((bf16[8,64,512]{2,1,0:T(8,128)(2,1)}), bf16[8,64,512]{2,1,0:T(8,128)(2,1)}, u32[]{:S(2)}, u32[]{:S(2)}) async-start(bf16[8,64,512]{2,1,0:T(8,128)(2,1)} %bitcast.71), calls=%async_computation.6 | async-start | bytes 1048576 | tf_op jit(solution)/shard_map/all_to_all | solution.py:857
  (86 other events, 1115.1 us)
Sparse Core Ops, SparseCore 0:
  21.8 64.8 all-gather.2
  97.4 89.2 all-gather.4
  465.5 87.1 reduce-scatter.1
